TPU v7x, 128 devices: a whole 4x4x4 slice. The times are simulated.
128 devices in a mesh: row: 16 (over z, x), col: 8 (over y, core).
Axes of the slice: x: 4, y: 4, z: 4, core: 2. Of those that a mesh axis runs over, the one named last changes fastest.
Arguments:
- factor: float32 [16384, 16384], P('row', 'col'), may hold values from -0.24 to 0.24
- adjoint: float32 [16384, 16384], P('row', 'col'), may hold values from -6 to 6
- inverse: float32 [2, 256, 256], replicated, may hold values from -1 to 3, as said below
Outputs:
- adjoint_out: float32 [16384, 16384], P('row', 'col')
Inputs may be any that keep to these rules, and one draw needn't show every extreme that they name: Each inverse[j] is lower triangular, with every diagonal entry larger than the sum of the magnitudes of the other entries of its row.
All inputs are finite; a program needn't handle non-finite values.
Results may differ from a plain program's by a relative error of at most 0.00011.
Values sent between devices are 32-bit elements; how exact they have to be, the bound alone decides.
No kernel may reach another device: no remote copies, remote signals or barrier semaphores. Data moves between devices by JAX's collectives and lax.ppermute only.
A program may use at most 128 MiB of HBM per device.

v0:
```python
import jax
import jax.numpy as jnp
from jax import lax
from jax.sharding import PartitionSpec as P


def broadcast(value, axis, source):
    kept = jnp.where(lax.axis_index(axis) == source, value, 0).astype(value.dtype)
    return lax.psum(kept, axis)


def product(left, right):
    return jnp.dot(left, right, precision=lax.Precision.HIGHEST, preferred_element_type=jnp.float32)


def halved_lower(matrix):
    return jnp.tril(matrix) - 0.5 * jnp.diag(jnp.diagonal(matrix))


def panel_step(factor, current, column, inverse_tile, panel_tile, row_global, col_global):
    width = inverse_tile.shape[0]
    rows_count = lax.axis_size("row")
    cols_count = lax.axis_size("col")
    owner_row = panel_tile % rows_count
    owner_col = panel_tile % cols_count
    row_start = panel_tile // rows_count * width
    col_start = panel_tile // cols_count * width
    below = (row_global > panel_tile)[:, None]
    left_mask = (col_global < panel_tile)[None, :]
    on_owner_row = lax.axis_index("row") == owner_row
    on_owner_col = lax.axis_index("col") == owner_col
    factor_column = factor[:, col_start : col_start + width]
    panel_adjoint, panel_factor = (
        broadcast(column, "col", owner_col),
        broadcast(factor_column, "col", owner_col),
    )
    offdiag = jnp.where(below, product(panel_adjoint, inverse_tile), 0.0)
    factor_row = broadcast(factor[row_start : row_start + width], "row", owner_row)
    factor_row = jnp.where(left_mask, factor_row, 0.0)
    raw_row = jnp.where(on_owner_row, current[row_start : row_start + width], 0.0)
    raw_diag = jnp.where(on_owner_row, panel_adjoint[row_start : row_start + width], 0.0)
    part_row = jnp.where(left_mask, raw_row - product(offdiag.T, factor), 0.0)
    part_diag = raw_diag - product(offdiag.T, panel_factor)
    identity = jnp.eye(width, dtype=jnp.float32)
    factor_diag = lax.linalg.triangular_solve(inverse_tile, identity, left_side=True, lower=True)
    row_total, diag_total = lax.psum((part_row, part_diag), "row")
    dprime = jnp.tril(diag_total)
    wmat = product(
        product(inverse_tile.T, halved_lower(product(factor_diag.T, dprime))), inverse_tile
    )
    sym = wmat + wmat.T
    new_row = row_total - product(sym, factor_row)
    updated = current - product(offdiag, factor_row)
    row_block = jnp.where(on_owner_row & left_mask, new_row, updated[row_start : row_start + width])
    updated = updated.at[row_start : row_start + width].set(row_block)
    new_column = jnp.where(below, offdiag, column)
    diag_block = jnp.where(
        on_owner_row, halved_lower(sym), new_column[row_start : row_start + width]
    )
    new_column = new_column.at[row_start : row_start + width].set(diag_block)
    new_column = jnp.where(on_owner_col, new_column, updated[:, col_start : col_start + width])
    updated = updated.at[:, col_start : col_start + width].set(new_column)
    return (updated, column)


def per_device(factor, adjoint, inverse):
    width = inverse.shape[-1]
    rows_count = lax.axis_size("row")
    cols_count = lax.axis_size("col")
    tile_rows = factor.shape[0] // width
    tile_cols = factor.shape[1] // width
    total_tiles = tile_rows * rows_count
    first_tile = total_tiles // 2
    second_tile = first_tile - 1
    row_global = jnp.repeat(jnp.arange(tile_rows) * rows_count + lax.axis_index("row"), width)
    col_global = jnp.repeat(jnp.arange(tile_cols) * cols_count + lax.axis_index("col"), width)
    first_start = first_tile // cols_count * width
    second_start = second_tile // cols_count * width
    current, unused = panel_step(
        factor,
        adjoint,
        adjoint[:, first_start : first_start + width],
        inverse[0],
        first_tile,
        row_global,
        col_global,
    )
    current, unused = panel_step(
        factor,
        current,
        current[:, second_start : second_start + width],
        inverse[1],
        second_tile,
        row_global,
        col_global,
    )
    return current


def solution(mesh):
    return jax.shard_map(
        per_device,
        mesh=mesh,
        in_specs=(P("row", "col"), P("row", "col"), P()),
        out_specs=P("row", "col"),
        check_vma=False,
    )
```

profile of v0, /device:TPU:16, one launch (start us, length us, event | category | flops | bytes accessed | tf_op | source)
XLA Modules:
  0.0 466.4 jit_solution(8654706204541608279)
XLA Ops:
  6.5 3.8 slice_select_fusion.3
  10.6 4.9 %slice_select_fusion.1 = (f32[256,2048]{1,0:T(8,128)}, f32[256,2048]{1,0:T(8,128)}) fusion(f32[1024,2048]{1,0:T(8,128)} %param.17, pred[]{:T(512)S(6)} %eq.41, pred[]{:T(512)S(6)} %eq.38), kind=kLoop, calls=%fused_computation.21 | loop fusion | flops 1048576 | bytes 8388610 | tf_op jit(solution)/shard_map/jit(_where)/select_n | solution.py:8
  15.5 58.9 %all-reduce.15.cloned.1.call-done = (f32[1024,256]{1,0:T(8,128)}, f32[1024,256]{1,0:T(8,128)}) async-done(((f32[1024,256]{1,0:T(8,128)}, f32[1024,256]{1,0:T(8,128)}), (f32[1024,256]{1,0:T(8,128)}, f32[1024,256]{1,0:T(8,128)})) %all-reduce.15.cloned.1.call-update) | async-done | bytes 2097168 | tf_op jit(solution)/shard_map/psum | solution.py:9
  74.3 2.6 slice_select_fusion.7
  77.0 3.5 convolution_subtract_fusion.7
  80.5 11.0 %fusion.5 = f32[256,2048]{1,0:T(8,128)} fusion(f32[1024,256]{1,0:T(8,128)S(1)} %get-tuple-element.131, f32[1024,2048]{1,0:T(8,128)} %param.17, f32[1024,2048]{1,0:T(8,128)} %param.18, pred[]{:T(512)S(6)} %eq.38, pred[2048]{0:T(1024)(128)(4,1)S(1)} %lt.46), kind=kOutput, calls=%fused_computation.19 | convolution fusion | flops 6444023808 | bytes 13633537 | tf_op jit(solution)/shard_map/dot_general | solution.py:13
  92.6 3.7 while.10
  96.4 19.7 %custom-call.12 = f32[2,128,128]{1,2,0:T(8,128)S(1)} custom-call(f32[2,128,128]{2,1,0:T(8,128)S(1)} %get-tuple-element.92), custom_call_target="InvertDiagBlocksLowerTriangular" | custom-call | tf_op jit(solution)/shard_map/triangular_solve/custom-call.1 | solution.py:45
  117.7 84.1 %all-reduce.11.cloned.1.call-done = (f32[256,2048]{1,0:T(8,128)}, f32[256,2048]{1,0:T(8,128)}, f32[256,256]{1,0:T(8,128)}) async-done(((f32[256,2048]{1,0:T(8,128)}, f32[256,2048]{1,0:T(8,128)}, f32[256,256]{1,0:T(8,128)}), (f32[256,2048]{1,0:T(8,128)}, f32[256,2048]{1,0:T(8,128)}, f32[256,256]{1,0:T(8,128)})) %all-reduce.11.cloned.1.call-update) | async-done | bytes 4456464 | tf_op jit(solution)/shard_map/psum | solution.py:9
  203.3 2.3 gather_fusion
  207.1 2.3 gather_fusion.1
  209.4 23.6 %convolution_subtract_fusion.1 = f32[1024,2048]{1,0:T(8,128)S(1)} fusion(f32[1024,2048]{1,0:T(8,128)} %param.18, f32[1024,256]{1,0:T(8,128)S(1)} %get-tuple-element.131, f32[256,2048]{1,0:T(8,128)} %get-tuple-element.113, pred[2048]{0:T(1024)(128)(4,1)S(1)} %lt.46), kind=kOutput, calls=%fused_computation.9 | convolution fusion | flops 6445072384 | bytes 19924992 | tf_op jit(solution)/shard_map/dot_general | solution.py:13
  233.2 2.5 fusion.3
  236.6 3.4 copy-done
  241.4 61.1 %all-reduce.13.cloned.1.call-done = (f32[1024,256]{1,0:T(8,128)}, f32[1024,256]{1,0:T(8,128)}) async-done(((f32[1024,256]{1,0:T(8,128)}, f32[1024,256]{1,0:T(8,128)}), (f32[1024,256]{1,0:T(8,128)}, f32[1024,256]{1,0:T(8,128)})) %all-reduce.13.cloned.1.call-update) | async-done | bytes 2097168 | tf_op jit(solution)/shard_map/psum | solution.py:9
  302.6 2.6 slice_select_fusion.5
  305.2 3.5 convolution_subtract_fusion.6
  308.7 11.0 %fusion.4 = f32[256,2048]{1,0:T(8,128)} fusion(f32[1024,256]{1,0:T(8,128)S(1)} %get-tuple-element.133, f32[1024,2048]{1,0:T(8,128)} %param.17, f32[1024,2048]{1,0:T(8,128)} %copy-done, pred[]{:T(512)S(6)} %eq.41, pred[2048]{0:T(1024)(128)(4,1)S(1)} %lt.49), kind=kOutput, calls=%fused_computation.17 | convolution fusion | flops 6444023808 | bytes 13633537 | tf_op jit(solution)/shard_map/dot_general | solution.py:13
  320.6 4.1 while.11
  324.7 19.7 %custom-call.13 = f32[2,128,128]{1,2,0:T(8,128)S(1)} custom-call(f32[2,128,128]{2,1,0:T(8,128)S(1)} %get-tuple-element.93), custom_call_target="InvertDiagBlocksLowerTriangular" | custom-call | tf_op jit(solution)/shard_map/triangular_solve/custom-call.1 | solution.py:45
  346.0 84.0 %all-reduce.9.cloned.1.call-done = (f32[256,2048]{1,0:T(8,128)}, f32[256,2048]{1,0:T(8,128)}, f32[256,256]{1,0:T(8,128)}) async-done(((f32[256,2048]{1,0:T(8,128)}, f32[256,2048]{1,0:T(8,128)}, f32[256,256]{1,0:T(8,128)}), (f32[256,2048]{1,0:T(8,128)}, f32[256,2048]{1,0:T(8,128)}, f32[256,256]{1,0:T(8,128)})) %all-reduce.9.cloned.1.call-update) | async-done | bytes 4456464 | tf_op jit(solution)/shard_map/psum | solution.py:9
  430.1 11.8 %convolution_subtract_fusion = f32[1024,2048]{1,0:T(8,128)} fusion(f32[1024,2048]{1,0:T(8,128)} %copy-done, f32[1024,256]{1,0:T(8,128)S(1)} %get-tuple-element.133, f32[256,2048]{1,0:T(8,128)} %get-tuple-element.110, pred[2048]{0:T(1024)(128)(4,1)S(1)} %lt.49), kind=kOutput, calls=%fused_computation.8 | convolution fusion | flops 6445072384 | bytes 19924992 | tf_op jit(solution)/shard_map/dot_general | solution.py:13
  451.0 5.5 %fusion.1 = f32[1024,2048]{1,0:T(8,128)} fusion(f32[1024,2048]{1,0:T(8,128)} %convolution_subtract_fusion, f32[256,2048]{1,0:T(8,128)} %get-tuple-element.111, f32[256,256]{1,0:T(8,128)S(1)} %bitcast_add_fusion, f32[256,2048]{1,0:T(8,128)S(1)} %copy-done.3, pred[2048]{0:T(1024)(128)(4,1)S(1)} %broadcast_and_fusion, pred[2048]{0:T(1024)(128)(4,1)S(1)} %lt.49), kind=kOutput, calls=%fused_computation.12 | convolution fusion | flops 1612185600 | bytes 8654848 | tf_op jit(solution)/shard_map/dot_general | solution.py:13
  456.6 3.1 fusion.11
  (88 shorter events, 27.7 us)
Async XLA Ops:
  6.5 67.8 %all-reduce.15.cloned.1.call-start = ((), (), s32[]{:S(2)}) async-start(), calls=%async_computation.3 | async-start | bytes 4194304 | tf_op jit(solution)/shard_map/psum | solution.py:9
  10.3 191.5 %all-reduce.11.cloned.1.call-start = ((), (), s32[]{:S(2)}) async-start(), calls=%async_computation.1 | async-start | bytes 8912896 | tf_op jit(solution)/shard_map/psum | solution.py:9
  10.6 63.7 %copy-start.1 = (f32[2,256,256]{2,1,0:T(8,128)S(1)}, f32[2,256,256]{2,1,0:T(8,128)}, u32[]{:S(2)}) copy-start(f32[2,256,256]{2,1,0:T(8,128)} %param.19) | copy-start | bytes 1572868
  74.3 2.6 copy-start.9
  91.5 211.1 %all-reduce.13.cloned.1.call-start = ((), (), s32[]{:S(2)}) async-start(), calls=%async_computation.2 | async-start | bytes 4194304 | tf_op jit(solution)/shard_map/psum | solution.py:9
  116.7 85.1 %copy-start.5 = (f32[256,256]{1,0:T(8,128)}, f32[256,256]{1,0:T(8,128)S(1)}, u32[]{:S(2)}) copy-start(f32[256,256]{1,0:T(8,128)S(1)} %fusion.50) | copy-start | bytes 786436
  209.4 23.7 %copy-start.2 = (f32[256,2048]{1,0:T(8,128)S(1)}, f32[256,2048]{1,0:T(8,128)}, u32[]{:S(2)}) copy-start(f32[256,2048]{1,0:T(8,128)} %get-tuple-element.113) | copy-start | bytes 6291460
  209.4 23.7 %copy-start.7 = (f32[256,2048]{1,0:T(8,128)S(1)}, f32[256,2048]{1,0:T(8,128)}, u32[]{:S(2)}) copy-start(f32[256,2048]{1,0:T(8,128)} %get-tuple-element.114) | copy-start | bytes 6291460
  236.6 3.4 copy-start
  241.2 188.9 %all-reduce.9.cloned.1.call-start = ((), (), s32[]{:S(2)}) async-start(), calls=%async_computation | async-start | bytes 8912896 | tf_op jit(solution)/shard_map/psum | solution.py:9
  302.6 2.6 copy-start.10
  319.7 0.9 copy-start.8
  319.7 25.4 %copy-start.6 = (f32[256,256]{1,0:T(8,128)S(1)}, f32[256,256]{1,0:T(8,128)}, u32[]{:S(2)}) copy-start(f32[256,256]{1,0:T(8,128)} %copy-done.5) | copy-start | bytes 786436
  430.1 11.8 %copy-start.11 = (f32[256,256]{1,0:T(8,128)S(1)}, f32[256,256]{1,0:T(8,128)}, u32[]{:S(2)}) copy-start(f32[256,256]{1,0:T(8,128)} %get-tuple-element.112) | copy-start | bytes 786436
  446.0 0.7 copy-start.4
  446.7 4.4 copy-start.3
Sparse Core Ops, SparseCore 0:
  10.5 63.8 all-reduce.14
  91.6 110.1 all-reduce.10
  241.3 61.2 all-reduce.12
  319.8 110.1 all-reduce.8
where the time goes:
time: 467 us; the launch traced here: 466 us
  waiting for transfers between devices  288 us (62%)
  matrix products  83.8 us (18%)
  other arithmetic  56.6 us (12%)
  local copies, waits for them, and re-layouts  23.5 us (5%)
  between operations  13.7 us (3%)
    psum x4, waiting for transfers between devices, broadcast(): return lax.psum(kept, axis)  288 us
    dot_general x16, matrix products, product(): jnp.dot(left, right, precision=lax.Precision.HIGHEST, preferred_element_t...  82.1 us
    another operation x4, other arithmetic, panel_step(): lax.linalg.triangular_solve(inverse_tile, identity, left_side=True, lower...  40.1 us
    select_n x3, other arithmetic, broadcast(): jnp.where(lax.axis_index(axis) == source, value, 0).astype(value.dtype)  9.75 us
    gather x4, local copies, waits for them, and re-layouts, halved_lower(): return jnp.tril(matrix) - 0.5 * jnp.diag(jnp.diagonal(matrix))  9.37 us
  transfers between devices with their start and end apart: 4, of which 4 were waited for; matrix products, arithmetic and copies ran while one was open for 12% of the time, Pallas kernels for 0%

commit v1 on v0

v1 whole, which is shorter than its diff:
```python
import functools

import jax
import jax.numpy as jnp
from jax import lax
from jax.experimental import pallas as pl
from jax.experimental.pallas import tpu as pltpu
from jax.sharding import PartitionSpec as P

ROW = "row"
COL = "col"
RING = 4
VMEM = pl.BlockSpec(memory_space=pltpu.VMEM)
HBM = pl.BlockSpec(memory_space=pltpu.HBM)


def product(left, right):
    return jnp.dot(left, right, precision=lax.Precision.HIGHEST, preferred_element_type=jnp.float32)


def split(value):
    high = value.astype(jnp.bfloat16)
    return high, (value - high.astype(jnp.float32)).astype(jnp.bfloat16)


def product_split(left, right_high, right_low):
    left_high, left_low = split(left)
    dot = functools.partial(jnp.dot, preferred_element_type=jnp.float32)
    return dot(left_high, right_high) + (dot(left_low, right_high) + dot(left_high, right_low))


def masks(width):
    rows = lax.broadcasted_iota(jnp.int32, (width, width), 0)
    cols = lax.broadcasted_iota(jnp.int32, (width, width), 1)
    return rows > cols, rows == cols


def tril(matrix):
    below, diag = masks(matrix.shape[0])
    return jnp.where(below | diag, matrix, 0.0)


def halved_lower(matrix):
    below, diag = masks(matrix.shape[0])
    return jnp.where(below, matrix, jnp.where(diag, 0.5 * matrix, 0.0))


def params(megabytes):
    return pltpu.CompilerParams(vmem_limit_bytes=megabytes << 20)


def cost(flops, bytes_accessed):
    return pl.CostEstimate(flops=flops, bytes_accessed=bytes_accessed, transcendentals=0)


def in_hbm(value):
    return pltpu.with_memory_space_constraint(value, pltpu.HBM)


def tile_shape(*shape):
    return jax.ShapeDtypeStruct(shape, jnp.float32)


def invert_kernel(tiles, out, out_t, power, total):
    width = tiles.shape[-1]
    below, diag = masks(width)
    scales = []
    for j in range(2):
        tile = tiles[j]
        out_t[j] = tile.T
        only = jnp.where(diag, tile, 0.0)
        power[j] = jnp.where(below, tile / jnp.sum(only, axis=1, keepdims=True), 0.0)
        total[j] = jnp.where(diag, 1.0, 0.0) - power[j]
        scales.append(1.0 / jnp.sum(only, axis=0, keepdims=True))

    @pl.loop(0, (width - 1).bit_length() - 1)
    def _(step):
        for j in range(2):
            power[j] = product(power[j], power[j])
        for j in range(2):
            total[j] = total[j] + product(total[j], power[j])

    for j in range(2):
        out[j] = (total[j] * scales[j]).T


def invert(tiles):
    w = tiles.shape[-1]
    return pl.pallas_call(
        invert_kernel,
        out_shape=(pltpu.HBM((2, w, w), jnp.float32),) * 2,
        in_specs=[VMEM],
        out_specs=(VMEM,) * 2,
        scratch_shapes=[pltpu.VMEM((2, w, w), jnp.float32)] * 2,
        compiler_params=params(10),
        cost_estimate=cost(28 * 12 * w**3, 1 << 20),
        name="invert",
    )(tiles)


def sums_kernel(even, odd, inv0, factor, out, a0_out, l1_out, high, low, small):
    step = pl.program_id(0)
    w = inv0.shape[0]
    rows = lax.axis_size(ROW)
    first = lax.axis_index(ROW) == 0
    per_step = w // (w * 4 // rows)
    cols = 4 * w // rows
    piece = w // rows

    @pl.when(step == 0)
    def _():
        l0, c0 = even[: 2 * w], even[2 * w : 4 * w]
        l1, c1 = odd[: 2 * w], odd[2 * w : 4 * w]
        skip = first & (lax.broadcasted_iota(jnp.int32, l0.shape, 0) < w)
        a0 = jnp.where(skip, 0.0, product(l0, inv0[...]))
        below = jnp.where(skip, 0.0, l1)
        a0_out[...] = a0
        l1_out[...] = below
        high[:, :w], low[:, :w] = split(a0)
        high[:, w:], low[:, w:] = split(below)
        a0_t, below_t = a0.T, below.T
        diag_high, diag_low = split(jnp.where(skip, 0.0, c0))
        next_high, next_low = split(jnp.where(skip, 0.0, c1))
        raw = jnp.where(first, l0[:w], 0.0)
        raw_next = jnp.where(first, l1[:w], 0.0)
        small[0] = raw - product_split(a0_t, diag_high, diag_low)
        small[1] = raw_next - product_split(a0_t, next_high, next_low)
        small[2] = product_split(below_t, next_high, next_low) - product(c1[:w].T, raw_next)

    part = product_split(factor[...].T, high[...], low[...])
    out[:, :cols, :] = part[:, :w].reshape(per_step, cols, w)
    out[:, cols : 2 * cols, :] = part[:, w:].reshape(per_step, cols, w)
    start = pl.multiple_of(step * (per_step * piece), per_step * piece)
    for j in range(3):
        lines = small[j, pl.ds(start, per_step * piece), :]
        at = 2 * cols + j * piece
        out[:, at : at + piece, :] = lines.reshape(per_step, piece, w)


def sums(even, odd, inv0, factor):
    w = inv0.shape[0]
    rows = lax.axis_size(ROW)
    height = 2 * (4 * w // rows) + 3 * (w // rows)
    const = lambda i: (0, 0)
    whole = lambda value: pl.BlockSpec(value.shape, const, pipeline_mode=pl.Buffered(1))
    return pl.pallas_call(
        sums_kernel,
        grid=(4,),
        out_shape=(pltpu.HBM((rows, height, w), jnp.float32),)
        + (pltpu.HBM((2 * w, w), jnp.float32),) * 2,
        in_specs=[whole(even), whole(odd), whole(inv0)]
        + [pl.BlockSpec((2 * w, w), lambda i: (1, i))],
        out_specs=(
            pl.BlockSpec((rows // 4, height, w), lambda i: (i, 0, 0)),
            pl.BlockSpec((2 * w, w), const),
            pl.BlockSpec((2 * w, w), const),
        ),
        scratch_shapes=[
            pltpu.VMEM((2 * w, 2 * w), jnp.bfloat16),
            pltpu.VMEM((2 * w, 2 * w), jnp.bfloat16),
            pltpu.VMEM((3, w, w), jnp.float32),
        ],
        compiler_params=params(14),
        cost_estimate=cost(4 << 30, 8 << 20),
        name="sums",
    )(even, odd, inv0, in_hbm(factor))


def middle_kernel(terms, r31, inv1, out, r31_v, inv1_v, out_v, sems):
    rows = terms.shape[0]
    cols = (terms.shape[1] - 3 * (inv1.shape[0] // rows)) // 2
    fetches = [
        pltpu.make_async_copy(r31, r31_v, sems.at[0]),
        pltpu.make_async_copy(inv1, inv1_v, sems.at[1]),
    ]
    for fetch in fetches:
        fetch.start()
    total = terms[0]
    for i in range(1, rows):
        total = total + terms[i]
    top = total[:cols]
    for fetch in fetches:
        fetch.wait()
    bottom = product(total[cols : 2 * cols] - product(top, r31_v[...]), inv1_v[...])
    out_v[0, :cols, :] = top
    out_v[1, :cols, :] = bottom
    for i in range(2):
        out_v[i, cols:, :] = total[2 * cols :]
    stores = [
        pltpu.make_async_copy(out_v.at[min(i, 1)], out.at[i], sems.at[2 + i]) for i in range(rows)
    ]
    for store in stores:
        store.start()
    for store in stores:
        store.wait()


def middle(terms, r31, inv1):
    rows, height, w = terms.shape
    cols = (height - 3 * (w // rows)) // 2
    return pl.pallas_call(
        middle_kernel,
        out_shape=pltpu.HBM((rows, height - cols, w), jnp.float32),
        in_specs=[VMEM, HBM, HBM],
        out_specs=HBM,
        scratch_shapes=[
            pltpu.VMEM((w, w), jnp.float32),
            pltpu.VMEM((w, w), jnp.float32),
            pltpu.VMEM((2, height - cols, w), jnp.float32),
            pltpu.SemaphoreType.DMA((2 + rows,)),
        ],
        compiler_params=params(10),
        cost_estimate=cost(1 << 28, 6 << 20),
        name="middle",
    )(terms, in_hbm(r31), in_hbm(inv1))


def trail_kernel(adj, a0, l1, inv1, r31, own, down, up, across_first, across_second, out, r_high, r_low, r31_inv):
    step = pl.program_id(0)
    w = inv1.shape[0]
    left = 4 * w
    q = lax.axis_index(COL)
    last_q = lax.axis_size(COL) - 1
    z = lax.axis_index(ROW) // RING
    out[...] = adj[...]

    @pl.when(step == 0)
    def _():
        r31_inv[...] = product(r31[...], inv1[...])
        quarter = w // RING
        for j in range(2):
            values = (own[j], down[j], (across_first, across_second)[j][...], up[j])
            for k, value in enumerate(values):
                start = pl.multiple_of(j * w + lax.rem(z + k, RING) * quarter, quarter)
                high, low = split(value)
                r_high[pl.ds(start, quarter), :] = high
                r_low[pl.ds(start, quarter), :] = low

    @pl.when(step >= pl.num_programs(0) // 2)
    def _():
        first = a0[...]
        second = product(l1[...], inv1[...]) - product(first, r31_inv[...])
        lhs = jnp.concatenate([first, second], axis=1)
        out[:, :left] = adj[:, :left] - product_split(lhs, r_high[...], r_low[...])

        @pl.when(q == 0)
        def _():
            out[:, left : left + w] = first

        @pl.when(q == last_q)
        def _():
            out[:, left - w : left] = second


def trail(adjoint, a0, l1, inv1, r31, *pieces):
    rows, cols = adjoint.shape
    w = inv1.shape[0]
    steps = 8
    blk = rows // steps
    low = lambda i: (jnp.maximum(i - steps // 2, 0), 0)
    const = lambda i: (0, 0)
    one = pl.Buffered(1)
    panel = pltpu.HBM((2 * w, 4 * w), jnp.bfloat16)
    return pl.pallas_call(
        trail_kernel,
        grid=(steps,),
        out_shape=(tile_shape(*adjoint.shape), panel, panel),
        in_specs=[
            pl.BlockSpec((blk, cols), lambda i: (i, 0)),
            pl.BlockSpec((blk, w), low),
            pl.BlockSpec((blk, w), low),
            pl.BlockSpec(inv1.shape, const, pipeline_mode=one),
            pl.BlockSpec(r31.shape, const, pipeline_mode=one),
        ]
        + [VMEM] * len(pieces),
        out_specs=(
            pl.BlockSpec((blk, cols), lambda i: (i, 0)),
            pl.BlockSpec(panel.shape, const),
            pl.BlockSpec(panel.shape, const),
        ),
        scratch_shapes=[pltpu.VMEM((w, w), jnp.float32)],
        compiler_params=params(16),
        cost_estimate=cost(4 << 30, 22 << 20),
        name="trail",
    )(in_hbm(adjoint), a0, l1, inv1, r31, *pieces)


def final_kernel(
    base, got, inverse, inverse_t, diag_t, diag31, r31, r_high, r_low, out,
    got_v, inverse_v, inverse_tv, diag_tv, diag31_v, r31_v, r_high_v, r_low_v, rows_buf, tile_buf, sems
):
    w = inverse.shape[-1]
    left = 4 * w
    p = lax.axis_index(ROW)
    q = lax.axis_index(COL)
    rows = got.shape[0]
    last_p = rows - 1
    last_q = lax.axis_size(COL) - 1
    piece = w // rows
    cols = got.shape[1] - 3 * piece
    at_root = (p == 0) | (p == last_p)

    @pl.when(at_root)
    def _():
        start = jnp.where(p == 0, 2 * w, w)
        tiles = pl.ds(cols, 3 * piece)
        moves = [
            (got.at[:, tiles, :], got_v.at[:, tiles, :]),
            (diag_t, diag_tv),
            (inverse_t, inverse_tv),
            (inverse, inverse_v),
            (r31, r31_v),
            (diag31, diag31_v),
            (r_high, r_high_v),
            (r_low, r_low_v),
            (base.at[pl.ds(start, w), pl.ds(0, left)], rows_buf),
            (got.at[:, pl.ds(0, cols), :], got_v.at[:, pl.ds(0, cols), :]),
        ]
        fetches = [pltpu.make_async_copy(src, dst, sems.at[i]) for i, (src, dst) in enumerate(moves)]
        for fetch in fetches:
            fetch.start()
        for fetch in fetches[:6]:
            fetch.wait()
        dsum, t01, x11 = (
            got_v[:, cols + j * piece : cols + (j + 1) * piece, :].reshape(w, w) for j in range(3)
        )

        def adjoint_diag(j, dprime):
            inner = halved_lower(product(diag_tv[j], tril(dprime)))
            wmat = product(product(inverse_tv[j], inner), inverse_v[j])
            return wmat + wmat.T

        corner = r31_v[...]
        side = product(inverse_tv[1], x11 + product(corner.T, t01))
        g0 = adjoint_diag(0, dsum)
        a132 = product(t01 - product(g0, corner), inverse_v[1])
        t11 = side + product(a132.T, corner)
        g1 = adjoint_diag(1, diag31_v[...] - t11)
        lhs = jnp.where(
            p == 0,
            jnp.concatenate([g0, a132], axis=1),
            jnp.concatenate([a132.T, g1], axis=1),
        )
        for fetch in fetches[6:]:
            fetch.wait()
        update = product_split(lhs, r_high_v[...], r_low_v[...])
        rows_buf[...] = rows_buf[...] - update - got_v[:, :cols, :].reshape(left, w).T

        @pl.when(q == last_q)
        def _():
            rows_buf[:, left - w :] = jnp.where(p == 0, a132, halved_lower(g1))

        store = pltpu.make_async_copy(
            rows_buf, out.at[pl.ds(start, w), pl.ds(0, left)], sems.at[len(moves)]
        )
        store.start()

        @pl.when((p == 0) & (q == 0))
        def _():
            tile_buf[...] = halved_lower(g0)
            corner_store = pltpu.make_async_copy(
                tile_buf, out.at[pl.ds(2 * w, w), pl.ds(left, w)], sems.at[len(moves) + 1]
            )
            corner_store.start()
            corner_store.wait()

        store.wait()


def final(base, *operands):
    w = operands[1].shape[-1]
    return pl.pallas_call(
        final_kernel,
        out_shape=tile_shape(*base.shape),
        in_specs=[HBM] * (1 + len(operands)),
        out_specs=HBM,
        scratch_shapes=[pltpu.VMEM(value.shape, value.dtype) for value in operands]
        + [
            pltpu.VMEM((w, 4 * w), jnp.float32),
            pltpu.VMEM((w, w), jnp.float32),
            pltpu.SemaphoreType.DMA((12,)),
        ],
        input_output_aliases={0: 0},
        compiler_params=params(16),
        cost_estimate=cost(6 << 30, 8 << 20),
        name="final",
    )(base, *[in_hbm(value) for value in operands])


def column_near(block):
    last = lax.axis_size(COL) - 1
    near = lax.ppermute(block, COL, [(0, 2), (last, last - 2)])
    far = lax.ppermute(block, COL, [(0, last - 1), (last, 1)])
    return near, far


def column_across(block, near, far):
    q = lax.axis_index(COL)
    last = lax.axis_size(COL) - 1
    half = block.shape[0] // 2
    upper = lax.ppermute(near[:half], COL, [(2, 4), (last - 2, last - 4)])
    lower = lax.ppermute(far[half:], COL, [(last - 1, 4), (1, last - 4)])
    return jnp.where(
        (q == 0) | (q == last),
        block,
        jnp.where(
            (q == 2) | (q == last - 2),
            near,
            jnp.where((q == 1) | (q == last - 1), far, jnp.concatenate([upper, lower], axis=0)),
        ),
    )


def column_swap(mine):
    theirs = lax.ppermute(mine, COL, [(i, i ^ 1) for i in range(lax.axis_size(COL))])
    even = lax.axis_index(COL) % 2 == 0
    return jnp.where(even, mine, theirs), jnp.where(even, theirs, mine)


def row_quarters(block):
    p = lax.axis_index(ROW)
    last = lax.axis_size(ROW) - 1
    top = RING - 1
    quarters = block.reshape(RING, -1, block.shape[1])
    first = p == 0
    near = lax.ppermute(
        jnp.where(first, quarters[1], quarters[top - 1]), ROW, [(0, RING), (last, last - RING)]
    )
    far = lax.ppermute(jnp.where(first, quarters[top], quarters[0]), ROW, [(0, last - top), (last, top)])
    across = lax.ppermute(
        jnp.where(first, quarters[2], quarters[1]), ROW, [(0, 2 * RING), (last, last - 2 * RING)]
    )
    mine = jnp.where(first, quarters[0], quarters[top])
    mine = jnp.where((p == RING) | (p == last - RING), near, mine)
    mine = jnp.where((p == last - top) | (p == top), far, mine)
    return jnp.where((p == 2 * RING) | (p == last - 2 * RING), across, mine)


def row_spread(mine):
    top = RING - 1
    x = lax.axis_index(ROW) % RING
    lines = range(0, lax.axis_size(ROW), RING)
    near = lax.ppermute(mine, ROW, [e for s in lines for e in ((s, s + 1), (s + top, s + top - 1))])
    far = lax.ppermute(mine, ROW, [e for s in lines for e in ((s, s + top), (s + top, s))])
    across = lax.ppermute(mine, ROW, [e for s in lines for e in ((s, s + 2), (s + top, s + top - 2))])
    from_first = jnp.where(x == 0, mine, jnp.where(x == 1, near, jnp.where(x == 2, across, far)))
    from_last = jnp.where(x == top, mine, jnp.where(x == 2, near, jnp.where(x == 1, across, far)))
    return jnp.stack([from_first, from_last])


def ring_pairs(step):
    count = lax.axis_size(ROW)
    return [(i, (i + step * RING) % count) for i in range(count)]


def per_device(factor, adjoint, inverse):
    w = inverse.shape[-1]
    rows = lax.axis_size(ROW)
    p = lax.axis_index(ROW)
    q = lax.axis_index(COL)
    low, left = 2 * w, 4 * w

    start = jnp.where(q == 0, left, left - w)
    adj_col = lax.dynamic_slice(adjoint, (low, start), (low, w))
    fac_col = lax.dynamic_slice(factor, (low, start), (low, w))
    block = jnp.concatenate([adj_col, fac_col, adjoint[w:low, left - w : left]], axis=0)
    row_block = lax.dynamic_slice(factor, (jnp.where(p == 0, low, w), 0), (w, left))
    quarter = row_quarters(row_block)
    block, quarter = lax.optimization_barrier((block, quarter))
    near, far = column_near(block)
    own = row_spread(quarter)
    near, far, own = lax.optimization_barrier((near, far, own))
    mine = column_across(block, near, far)
    up = lax.ppermute(own, ROW, ring_pairs(1))
    down = lax.ppermute(own, ROW, ring_pairs(-1))
    even, odd = column_swap(mine)
    terms, a0, l1_below = sums(even, odd, inverse[0], factor)
    up, down, l1_below = lax.optimization_barrier((up, down, l1_below))
    across_first = lax.ppermute(up[0], ROW, ring_pairs(1))
    across_second = lax.ppermute(down[1], ROW, ring_pairs(-1))
    terms, across_first, across_second = lax.optimization_barrier((terms, across_first, across_second))
    terms = lax.all_to_all(terms, ROW, 0, 0)
    diag_t, inverse_t = invert(inverse)

    z = p // RING
    corner = [value[..., left - w :].reshape(-1, w) for value in (own[0], down[0], across_first, up[0])]
    corner = jnp.concatenate(corner, axis=0)
    corner = column_swap(column_across(corner, *column_near(corner)))[1]
    r31 = lax.dynamic_slice(
        jnp.concatenate([corner, corner], axis=0), ((RING - z) % RING * (w // RING), 0), (w, w)
    )
    base, r_high, r_low = trail(
        adjoint, a0, l1_below, inverse[1], r31, own, down, up, across_first, across_second
    )
    terms, diag_t, inverse_t = lax.optimization_barrier((terms, diag_t, inverse_t))
    shares = lax.all_to_all(middle(terms, r31, inverse[1]), ROW, 0, 0)
    return final(base, shares, inverse, inverse_t, diag_t, odd[2 * low :], r31, r_high, r_low)


def solution(mesh):
    return jax.shard_map(
        per_device,
        mesh=mesh,
        in_specs=(P(ROW, COL), P(ROW, COL), P()),
        out_specs=P(ROW, COL),
        check_vma=False,
    )
```

time: 467 us -> 177 us (0.38)
  waiting for transfers between devices: 288 us -> 64.4 us
  matrix products: 83.8 us -> 0 us
  other arithmetic: 56.6 us -> 9.69 us
  starting transfers between devices: 0.38 us -> 46.3 us
  Pallas kernels: 0 us -> 43.1 us
  between operations: 13.7 us -> 0.62 us
  local copies, waits for them, and re-layouts: 23.5 us -> 12 us
    psum x4 -> x0, waiting for transfers between devices: 288 us -> none  [broadcast(): return lax.psum(kept, axis)]
    dot_general x16 -> x0, matrix products: 82.1 us -> none  [product(): jnp.dot(left, right, precision=lax.Precision.HIGHEST, preferred_element_t...]
    ppermute x0 -> x20, waiting for transfers between devices: none -> 43.6 us  [the longest x2 18.4 us: column_across(): lower = lax.ppermute(far[half:], COL, [(last - 1, 4), (1, last - 4)])]
    pallas_call x0 -> x5, Pallas kernels: none -> 43.1 us  [the longest x1 12.7 us: trail(): pl.pallas_call(trail_kernel, grid=(steps,), out_shape=(tile_shape(*adjoin...]
    another operation x6 -> x2, other arithmetic: 41.5 us -> 0.11 us  [row_spread(): return jnp.stack([from_first, from_last])]
    ppermute x0 -> x20, starting transfers between devices: none -> 35.5 us  [the longest x1 6.21 us: row_spread(): lax.ppermute(mine, ROW, [e for s in lines for e in ((s, s + top), (s + to...]
    all_to_all x0 -> x2, waiting for transfers between devices: none -> 20.8 us  [the longest x1 11.4 us: per_device(): shares = lax.all_to_all(middle(terms, r31, inverse[1]), ROW, 0, 0)]
    all_to_all x0 -> x2, starting transfers between devices: none -> 10.8 us  [the longest x1 6.09 us: per_device(): terms = lax.all_to_all(terms, ROW, 0, 0)]
  transfers between devices with their start and end apart: 4 -> 22, of which waited for: 4 -> 13; matrix products, arithmetic and copies ran while one was open for 12% -> 7% of each run, Pallas kernels for 0% -> 17%
where the time goes in v1:
time: 177 us; the launch traced here: 176 us
  waiting for transfers between devices  64.4 us (36%)
  starting transfers between devices  46.3 us (26%)
  Pallas kernels  43.1 us (24%)
  local copies, waits for them, and re-layouts  12 us (7%)
  other arithmetic  9.69 us (5%)
    ppermute x2, waiting for transfers between devices, column_across(): lower = lax.ppermute(far[half:], COL, [(last - 1, 4), (1, last - 4)])  18.4 us
    pallas_call x1, Pallas kernels, trail(): pl.pallas_call(trail_kernel, grid=(steps,), out_shape=(tile_shape(*adjoin...  12.7 us
    all_to_all x1, waiting for transfers between devices, per_device(): shares = lax.all_to_all(middle(terms, r31, inverse[1]), ROW, 0, 0)  11.4 us
    pallas_call x1, Pallas kernels, invert(): pl.pallas_call(invert_kernel, out_shape=(pltpu.HBM((2, w, w), jnp.float32...  9.81 us
    pallas_call x1, Pallas kernels, final(): pl.pallas_call(final_kernel, out_shape=tile_shape(*base.shape), in_specs=...  9.59 us
    all_to_all x1, waiting for transfers between devices, per_device(): terms = lax.all_to_all(terms, ROW, 0, 0)  9.39 us
    pallas_call x1, Pallas kernels, sums(): pl.pallas_call(sums_kernel, grid=(4,), out_shape=(pltpu.HBM((rows, height...  7.88 us
    ppermute x1, starting transfers between devices, row_spread(): lax.ppermute(mine, ROW, [e for s in lines for e in ((s, s + top), (s + to...  6.21 us
  transfers between devices with their start and end apart: 22, of which 13 were waited for; matrix products, arithmetic and copies ran while one was open for 7% of the time, Pallas kernels for 17%

profile of v1, /device:TPU:16, one launch (start us, length us, event | category | flops | bytes accessed | tf_op | source)
XLA Modules:
  0.0 176.1 jit_solution(13313172419187404483)
XLA Ops:
  1.3 4.6 %collective-permute-start.2 = (f32[64,1024]{1,0:T(8,128)S(1)}, f32[64,1024]{1,0:T(8,128)}, u32[]{:S(2)}, u32[]{:S(2)}) collective-permute-start(f32[64,1024]{1,0:T(8,128)S(1)} %get-tuple-element.49), channel_id=1, source_target_pairs={{0,32},{120,88},{1,33},{121,89},{2,34},{122,90},{3,35},{123,91},{4... | collective-permute-start | bytes 786440 | tf_op jit(solution)/shard_map/ppermute | solution.py:426
  5.8 3.3 %collective-permute-start = (f32[64,1024]{1,0:T(8,128)S(1)}, f32[64,1024]{1,0:T(8,128)}, u32[]{:S(2)}, u32[]{:S(2)}) collective-permute-start(f32[64,1024]{1,0:T(8,128)S(1)} %get-tuple-element.50), channel_id=1, source_target_pairs={{0,64},{120,56},{1,65},{121,57},{2,66},{122,58},{3,67},{123,59},{4... | collective-permute-start | bytes 786440 | tf_op jit(solution)/shard_map/ppermute | solution.py:430
  13.5 2.7 %collective-permute-done = f32[64,1024]{1,0:T(8,128)} collective-permute-done((f32[64,1024]{1,0:T(8,128)S(1)}, f32[64,1024]{1,0:T(8,128)}, u32[]{:S(2)}, u32[]{:S(2)}) %collective-permute-start) | collective-permute-done | bytes 262176 | tf_op jit(solution)/shard_map/ppermute | solution.py:430
  20.9 6.2 %collective-permute-start.7 = (f32[64,1024]{1,0:T(8,128)S(1)}, f32[64,1024]{1,0:T(8,128)S(1)}, u32[]{:S(2)}, u32[]{:S(2)}) collective-permute-start(f32[64,1024]{1,0:T(8,128)S(1)} %select_select_fusion), channel_id=1, source_target_pairs={{0,24},{24,0},{32,56},{56,32},{64,88},{88,64},{96,120},{120,96},{1... | collective-permute-start | bytes 786440 | tf_op jit(solution)/shard_map/ppermute | solution.py:444
  29.7 2.3 %collective-permute-done.7 = f32[64,1024]{1,0:T(8,128)S(1)} collective-permute-done((f32[64,1024]{1,0:T(8,128)S(1)}, f32[64,1024]{1,0:T(8,128)S(1)}, u32[]{:S(2)}, u32[]{:S(2)}) %collective-permute-start.7) | collective-permute-done | bytes 262176 | tf_op jit(solution)/shard_map/ppermute | solution.py:444
  32.0 3.1 %collective-permute-done.6 = f32[64,1024]{1,0:T(8,128)S(1)} collective-permute-done((f32[64,1024]{1,0:T(8,128)S(1)}, f32[64,1024]{1,0:T(8,128)S(1)}, u32[]{:S(2)}, u32[]{:S(2)}) %collective-permute-start.6) | collective-permute-done | bytes 262176 | tf_op jit(solution)/shard_map/ppermute | solution.py:445
  35.1 3.1 %collective-permute-done.5 = f32[64,1024]{1,0:T(8,128)S(1)} collective-permute-done((f32[64,1024]{1,0:T(8,128)S(1)}, f32[64,1024]{1,0:T(8,128)S(1)}, u32[]{:S(2)}, u32[]{:S(2)}) %collective-permute-start.5) | collective-permute-done | bytes 262176 | tf_op jit(solution)/shard_map/ppermute | solution.py:443
  44.1 10.6 %collective-permute-done.9 = f32[640,256]{1,0:T(8,128)} collective-permute-done((f32[640,256]{1,0:T(8,128)}, f32[640,256]{1,0:T(8,128)}, u32[]{:S(2)}, u32[]{:S(2)}) %collective-permute-start.9) | collective-permute-done | bytes 655392 | tf_op jit(solution)/shard_map/ppermute | solution.py:402
  55.7 2.7 %fusion.1 = f32[1280,256]{1,0:T(8,128)} fusion(f32[1280,256]{1,0:T(8,128)S(1)} %pad_maximum_fusion, f32[1280,256]{1,0:T(8,128)} %collective-permute-done.3, f32[1280,256]{1,0:T(8,128)} %collective-permute-done.4, f32[640,256]{1,0:T(8,128)} %collective-permute-done.9, f32[640,256]{1,0:T(8,128)} %collective-permute-done.8, pred[]{:T(512)S(6)} %or.26, ...), kind=kLoop, calls=%fused_computation.3 | loop fusion | flops 1310720 | bytes 6553603 | tf_op jit(solution)/shard_map/jit(_where)/select_n | solution.py:403
  59.2 3.6 %collective-permute-start.12 = (f32[2,64,1024]{2,1,0:T(8,128)S(1)}, f32[2,64,1024]{2,1,0:T(8,128)S(1)}, u32[]{:S(2)}, u32[]{:S(2)}) collective-permute-start(f32[2,64,1024]{2,1,0:T(8,128)S(1)} %pad_maximum_fusion.1.own), channel_id=1, source_target_pairs={{0,96},{8,104},{16,112},{24,120},{32,0},{40,8},{48,16},{56,24},{64... | collective-permute-start | bytes 1572872 | tf_op jit(solution)/shard_map/ppermute | solution.py:475
  64.7 7.9 %sums.1 = (f32[16,176,256]{2,1,0:T(8,128)}, f32[512,256]{1,0:T(8,128)}, f32[512,256]{1,0:T(8,128)}) custom-call(f32[1280,256]{1,0:T(8,128)S(1)} %get-tuple-element.53.even, f32[1280,256]{1,0:T(8,128)S(1)} %get-tuple-element.52.odd, f32[256,256]{1,0:T(8,128)S(1)} %get-tuple-element.59.inv0, f32[1024,2048]{1,0:T(8,128)} %factor.1), custom_call_target="tpu_custom_call" | custom-call | flops 4294967296 | bytes 8388608 | tf_op jit(solution)/shard_map/sums/pallas_call | solution.py:146
  74.6 3.4 %collective-permute-done.11.up = f32[2,64,1024]{2,1,0:T(8,128)S(1)} collective-permute-done((f32[2,64,1024]{2,1,0:T(8,128)S(1)}, f32[2,64,1024]{2,1,0:T(8,128)S(1)}, u32[]{:S(2)}, u32[]{:S(2)}) %collective-permute-start.11) | collective-permute-done | bytes 524320 | tf_op jit(solution)/shard_map/ppermute | solution.py:474
  79.0 3.1 %collective-permute-start.14 = (f32[64,1024]{1,0:T(8,128)S(1)}, f32[64,1024]{1,0:T(8,128)S(1)}, u32[]{:S(2)}, u32[]{:S(2)}) collective-permute-start(f32[64,1024]{1,0:T(8,128)S(1)} %get-tuple-element.57), channel_id=1, source_target_pairs={{0,96},{8,104},{16,112},{24,120},{32,0},{40,8},{48,16},{56,24},{64... | collective-permute-start | bytes 786440 | tf_op jit(solution)/shard_map/ppermute | solution.py:480
  82.1 5.0 %collective-permute-done.13.across_first = f32[64,1024]{1,0:T(8,128)} collective-permute-done((f32[64,1024]{1,0:T(8,128)S(1)}, f32[64,1024]{1,0:T(8,128)}, u32[]{:S(2)}, u32[]{:S(2)}) %collective-permute-start.13) | collective-permute-done | bytes 262176 | tf_op jit(solution)/shard_map/ppermute | solution.py:479
  87.8 6.1 %all-to-all-start = ((f32[16,176,256]{2,1,0:T(8,128)}), f32[16,176,256]{2,1,0:T(8,128)S(1)}, u32[]{:S(2)}, u32[]{:S(2)}) async-start(f32[16,176,256]{2,1,0:T(8,128)} %get-tuple-element.41), calls=%async_computation | async-start | bytes 5767168 | tf_op jit(solution)/shard_map/all_to_all | solution.py:482
  100.6 7.7 %collective-permute-done.18 = f32[128,256]{1,0:T(8,128)S(1)} collective-permute-done((f32[128,256]{1,0:T(8,128)S(1)}, f32[128,256]{1,0:T(8,128)S(1)}, u32[]{:S(2)}, u32[]{:S(2)}) %collective-permute-start.18) | collective-permute-done | bytes 131104 | tf_op jit(solution)/shard_map/ppermute | solution.py:402
  108.3 2.5 %collective-permute-done.17 = f32[128,256]{1,0:T(8,128)S(1)} collective-permute-done((f32[128,256]{1,0:T(8,128)S(1)}, f32[128,256]{1,0:T(8,128)S(1)}, u32[]{:S(2)}, u32[]{:S(2)}) %collective-permute-start.17) | collective-permute-done | bytes 131104 | tf_op jit(solution)/shard_map/ppermute | solution.py:401
  111.6 9.8 %invert.1 = (f32[2,256,256]{2,1,0:T(8,128)}, f32[2,256,256]{2,1,0:T(8,128)}) custom-call(f32[2,256,256]{2,1,0:T(8,128)S(1)} %copy-done.4), custom_call_target="tpu_custom_call" | custom-call | flops 5637144576 | bytes 1048576 | tf_op jit(solution)/shard_map/invert/pallas_call | solution.py:89
  123.2 9.4 %all-to-all-done.terms = f32[16,176,256]{2,1,0:T(8,128)S(1)} async-done(((f32[16,176,256]{2,1,0:T(8,128)}), f32[16,176,256]{2,1,0:T(8,128)S(1)}, u32[]{:S(2)}, u32[]{:S(2)}) %all-to-all-start) | async-done | bytes 2883616 | tf_op jit(solution)/shard_map/all_to_all | solution.py:482
  132.6 3.1 %middle.1 = f32[16,112,256]{2,1,0:T(8,128)} custom-call(f32[16,176,256]{2,1,0:T(8,128)S(1)} %all-to-all-done.terms, f32[256,256]{1,0:T(8,128)} %fusion.2.r31, f32[256,256]{1,0:T(8,128)} %get-tuple-element.58.inv1), custom_call_target="tpu_custom_call" | custom-call | flops 268435456 | bytes 6291456 | tf_op jit(solution)/shard_map/middle/pallas_call | solution.py:201
  135.7 4.7 %all-to-all-start.1 = ((f32[16,112,256]{2,1,0:T(8,128)}), f32[16,112,256]{2,1,0:T(8,128)}, u32[]{:S(2)}, u32[]{:S(2)}) async-start(f32[16,112,256]{2,1,0:T(8,128)} %middle.1), calls=%async_computation.1 | async-start | bytes 3670016 | tf_op jit(solution)/shard_map/all_to_all | solution.py:496
  142.2 12.7 %trail.1 = (f32[1024,2048]{1,0:T(8,128)}, bf16[512,1024]{1,0:T(8,128)(2,1)}, bf16[512,1024]{1,0:T(8,128)(2,1)}) custom-call(f32[1024,2048]{1,0:T(8,128)} %adj.1, f32[512,256]{1,0:T(8,128)S(1)} %copy-done.11, f32[512,256]{1,0:T(8,128)S(1)} %copy-done.12, f32[256,256]{1,0:T(8,128)S(1)} %copy-done.2, f32[256,256]{1,0:T(8,128)S(1)} %copy-done.1, ...), custom_call_target="tpu_custom_call" | custom-call | flops 4294967296 | bytes 23068672 | tf_op jit(solution)/shard_map/trail/pallas_call | solution.py:264
  154.9 11.4 %all-to-all-done.1.got = f32[16,112,256]{2,1,0:T(8,128)} async-done(((f32[16,112,256]{2,1,0:T(8,128)}), f32[16,112,256]{2,1,0:T(8,128)}, u32[]{:S(2)}, u32[]{:S(2)}) %all-to-all-start.1) | async-done | bytes 1835040 | tf_op jit(solution)/shard_map/all_to_all | solution.py:496
  166.3 9.6 %final.1 = f32[1024,2048]{1,0:T(8,128)} custom-call(f32[1024,2048]{1,0:T(8,128)} %get-tuple-element.40.base, f32[16,112,256]{2,1,0:T(8,128)} %all-to-all-done.1.got, f32[2,256,256]{2,1,0:T(8,128)} %inverse.1, f32[2,256,256]{2,1,0:T(8,128)} %get-tuple-element.45.inverse_t, f32[2,256,256]{2,1,0:T(8,128)} %get-tuple-element.46.diag_t, ...), custom_call_target="tpu_custom_call", output_to_operand_aliasing={{}: (0, {})} | custom-call | flops 6442450944 | bytes 8388608 | tf_op jit(solution)/shard_map/final/pallas_call | solution.py:372
  (79 shorter events, 36.9 us)
Async XLA Ops:
  1.3 12.3 %collective-permute-start.2 = (f32[64,1024]{1,0:T(8,128)S(1)}, f32[64,1024]{1,0:T(8,128)}, u32[]{:S(2)}, u32[]{:S(2)}) collective-permute-start(f32[64,1024]{1,0:T(8,128)S(1)} %get-tuple-element.49), channel_id=1, source_target_pairs={{0,32},{120,88},{1,33},{121,89},{2,34},{122,90},{3,35},{123,91},{4... | collective-permute-start | bytes 786440 | tf_op jit(solution)/shard_map/ppermute | solution.py:426
  5.8 10.4 %collective-permute-start = (f32[64,1024]{1,0:T(8,128)S(1)}, f32[64,1024]{1,0:T(8,128)}, u32[]{:S(2)}, u32[]{:S(2)}) collective-permute-start(f32[64,1024]{1,0:T(8,128)S(1)} %get-tuple-element.50), channel_id=1, source_target_pairs={{0,64},{120,56},{1,65},{121,57},{2,66},{122,58},{3,67},{123,59},{4... | collective-permute-start | bytes 786440 | tf_op jit(solution)/shard_map/ppermute | solution.py:430
  9.2 7.1 %collective-permute-start.1 = (f32[64,1024]{1,0:T(8,128)S(1)}, f32[64,1024]{1,0:T(8,128)}, u32[]{:S(2)}, u32[]{:S(2)}) collective-permute-start(f32[64,1024]{1,0:T(8,128)S(1)} %get-tuple-element.51), channel_id=1, source_target_pairs={{0,96},{120,24},{1,97},{121,25},{2,98},{122,26},{3,99},{123,27},{4... | collective-permute-start | bytes 786440 | tf_op jit(solution)/shard_map/ppermute | solution.py:429
  17.4 21.0 %collective-permute-start.4 = (f32[1280,256]{1,0:T(8,128)S(1)}, f32[1280,256]{1,0:T(8,128)}, u32[]{:S(2)}, u32[]{:S(2)}) collective-permute-start(f32[1280,256]{1,0:T(8,128)S(1)} %pad_maximum_fusion), channel_id=1, source_target_pairs={{0,6},{7,1},{8,14},{15,9},{16,22},{23,17},{24,30},{31,25},{32,38},... | collective-permute-start | bytes 3932168 | tf_op jit(solution)/shard_map/ppermute | solution.py:393
  19.1 19.2 %collective-permute-start.3 = (f32[1280,256]{1,0:T(8,128)S(1)}, f32[1280,256]{1,0:T(8,128)}, u32[]{:S(2)}, u32[]{:S(2)}) collective-permute-start(f32[1280,256]{1,0:T(8,128)S(1)} %pad_maximum_fusion), channel_id=1, source_target_pairs={{0,2},{7,5},{8,10},{15,13},{16,18},{23,21},{24,26},{31,29},{32,34}... | collective-permute-start | bytes 3932168 | tf_op jit(solution)/shard_map/ppermute | solution.py:392
  20.9 11.2 %collective-permute-start.7 = (f32[64,1024]{1,0:T(8,128)S(1)}, f32[64,1024]{1,0:T(8,128)S(1)}, u32[]{:S(2)}, u32[]{:S(2)}) collective-permute-start(f32[64,1024]{1,0:T(8,128)S(1)} %select_select_fusion), channel_id=1, source_target_pairs={{0,24},{24,0},{32,56},{56,32},{64,88},{88,64},{96,120},{120,96},{1... | collective-permute-start | bytes 786440 | tf_op jit(solution)/shard_map/ppermute | solution.py:444
  27.1 8.0 %collective-permute-start.6 = (f32[64,1024]{1,0:T(8,128)S(1)}, f32[64,1024]{1,0:T(8,128)S(1)}, u32[]{:S(2)}, u32[]{:S(2)}) collective-permute-start(f32[64,1024]{1,0:T(8,128)S(1)} %select_select_fusion), channel_id=1, source_target_pairs={{0,16},{24,8},{32,48},{56,40},{64,80},{88,72},{96,112},{120,104},{... | collective-permute-start | bytes 786440 | tf_op jit(solution)/shard_map/ppermute | solution.py:445
  28.4 9.8 %collective-permute-start.5 = (f32[64,1024]{1,0:T(8,128)S(1)}, f32[64,1024]{1,0:T(8,128)S(1)}, u32[]{:S(2)}, u32[]{:S(2)}) collective-permute-start(f32[64,1024]{1,0:T(8,128)S(1)} %select_select_fusion), channel_id=1, source_target_pairs={{0,8},{24,16},{32,40},{56,48},{64,72},{88,80},{96,104},{120,112},{... | collective-permute-start | bytes 786440 | tf_op jit(solution)/shard_map/ppermute | solution.py:443
  41.4 13.3 %collective-permute-start.9 = (f32[640,256]{1,0:T(8,128)}, f32[640,256]{1,0:T(8,128)}, u32[]{:S(2)}, u32[]{:S(2)}) collective-permute-start(f32[640,256]{1,0:T(8,128)} %slice.76), channel_id=1, source_target_pairs={{6,4},{1,3},{14,12},{9,11},{22,20},{17,19},{30,28},{25,27},{38,36}... | collective-permute-start | bytes 1966088 | tf_op jit(solution)/shard_map/ppermute | solution.py:402
  42.7 13.0 %collective-permute-start.8 = (f32[640,256]{1,0:T(8,128)S(1)}, f32[640,256]{1,0:T(8,128)}, u32[]{:S(2)}, u32[]{:S(2)}) collective-permute-start(f32[640,256]{1,0:T(8,128)S(1)} %slice.75), channel_id=1, source_target_pairs={{2,4},{5,3},{10,12},{13,11},{18,20},{21,19},{26,28},{29,27},{34,36... | collective-permute-start | bytes 1966088 | tf_op jit(solution)/shard_map/ppermute | solution.py:401
  44.1 14.4 %copy-start.3 = (f32[2,256,256]{2,1,0:T(8,128)S(1)}, f32[2,256,256]{2,1,0:T(8,128)}, u32[]{:S(2)}) copy-start(f32[2,256,256]{2,1,0:T(8,128)} %inverse.1) | copy-start | bytes 1572868
  58.4 4.4 %collective-permute-start.10 = (f32[1280,256]{1,0:T(8,128)}, f32[1280,256]{1,0:T(8,128)}, u32[]{:S(2)}, u32[]{:S(2)}) collective-permute-start(f32[1280,256]{1,0:T(8,128)} %fusion.1), channel_id=1, source_target_pairs={{0,1},{1,0},{2,3},{3,2},{4,5},{5,4},{6,7},{7,6},{8,9},{9,8},{10,11... | collective-permute-start | bytes 3932168 | tf_op jit(solution)/shard_map/ppermute | solution.py:415
  59.2 15.5 %collective-permute-start.12 = (f32[2,64,1024]{2,1,0:T(8,128)S(1)}, f32[2,64,1024]{2,1,0:T(8,128)S(1)}, u32[]{:S(2)}, u32[]{:S(2)}) collective-permute-start(f32[2,64,1024]{2,1,0:T(8,128)S(1)} %pad_maximum_fusion.1.own), channel_id=1, source_target_pairs={{0,96},{8,104},{16,112},{24,120},{32,0},{40,8},{48,16},{56,24},{64... | collective-permute-start | bytes 1572872 | tf_op jit(solution)/shard_map/ppermute | solution.py:475
  62.8 15.3 %collective-permute-start.11 = (f32[2,64,1024]{2,1,0:T(8,128)S(1)}, f32[2,64,1024]{2,1,0:T(8,128)S(1)}, u32[]{:S(2)}, u32[]{:S(2)}) collective-permute-start(f32[2,64,1024]{2,1,0:T(8,128)S(1)} %pad_maximum_fusion.1.own), channel_id=1, source_target_pairs={{0,32},{8,40},{16,48},{24,56},{32,64},{40,72},{48,80},{56,88},{64,... | collective-permute-start | bytes 1572872 | tf_op jit(solution)/shard_map/ppermute | solution.py:474
  78.1 9.0 %collective-permute-start.13 = (f32[64,1024]{1,0:T(8,128)S(1)}, f32[64,1024]{1,0:T(8,128)}, u32[]{:S(2)}, u32[]{:S(2)}) collective-permute-start(f32[64,1024]{1,0:T(8,128)S(1)} %slice_bitcast_fusion.1), channel_id=1, source_target_pairs={{0,32},{8,40},{16,48},{24,56},{32,64},{40,72},{48,80},{56,88},{64,... | collective-permute-start | bytes 786440 | tf_op jit(solution)/shard_map/ppermute | solution.py:479
  79.0 8.1 %collective-permute-start.14 = (f32[64,1024]{1,0:T(8,128)S(1)}, f32[64,1024]{1,0:T(8,128)S(1)}, u32[]{:S(2)}, u32[]{:S(2)}) collective-permute-start(f32[64,1024]{1,0:T(8,128)S(1)} %get-tuple-element.57), channel_id=1, source_target_pairs={{0,96},{8,104},{16,112},{24,120},{32,0},{40,8},{48,16},{56,24},{64... | collective-permute-start | bytes 786440 | tf_op jit(solution)/shard_map/ppermute | solution.py:480
  87.8 44.8 %all-to-all-start = ((f32[16,176,256]{2,1,0:T(8,128)}), f32[16,176,256]{2,1,0:T(8,128)S(1)}, u32[]{:S(2)}, u32[]{:S(2)}) async-start(f32[16,176,256]{2,1,0:T(8,128)} %get-tuple-element.41), calls=%async_computation | async-start | bytes 5767168 | tf_op jit(solution)/shard_map/all_to_all | solution.py:482
  94.8 16.8 %copy-start.4 = (f32[2,256,256]{2,1,0:T(8,128)S(1)}, f32[2,256,256]{2,1,0:T(8,128)}, u32[]{:S(2)}) copy-start(f32[2,256,256]{2,1,0:T(8,128)} %inverse.1) | copy-start | bytes 1572868
  96.6 1.4 collective-permute-start.16
  97.2 2.0 %collective-permute-start.15 = (f32[256,256]{1,0:T(8,128)S(1)}, f32[256,256]{1,0:T(8,128)S(1)}, u32[]{:S(2)}, u32[]{:S(2)}) collective-permute-start(f32[256,256]{1,0:T(8,128)S(1)} %pad_maximum_fusion.2), channel_id=1, source_target_pairs={{0,2},{7,5},{8,10},{15,13},{16,18},{23,21},{24,26},{31,29},{32,34}... | collective-permute-start | bytes 786440 | tf_op jit(solution)/shard_map/ppermute | solution.py:392
  98.0 10.4 %collective-permute-start.18 = (f32[128,256]{1,0:T(8,128)S(1)}, f32[128,256]{1,0:T(8,128)S(1)}, u32[]{:S(2)}, u32[]{:S(2)}) collective-permute-start(f32[128,256]{1,0:T(8,128)S(1)} %slice.94), channel_id=1, source_target_pairs={{6,4},{1,3},{14,12},{9,11},{22,20},{17,19},{30,28},{25,27},{38,36}... | collective-permute-start | bytes 393224 | tf_op jit(solution)/shard_map/ppermute | solution.py:402
  99.3 11.5 %collective-permute-start.17 = (f32[128,256]{1,0:T(8,128)S(1)}, f32[128,256]{1,0:T(8,128)S(1)}, u32[]{:S(2)}, u32[]{:S(2)}) collective-permute-start(f32[128,256]{1,0:T(8,128)S(1)} %slice.93), channel_id=1, source_target_pairs={{2,4},{5,3},{10,12},{13,11},{18,20},{21,19},{26,28},{29,27},{34,36... | collective-permute-start | bytes 393224 | tf_op jit(solution)/shard_map/ppermute | solution.py:401
  111.6 9.8 %collective-permute-start.19 = (f32[256,256]{1,0:T(8,128)}, f32[256,256]{1,0:T(8,128)}, u32[]{:S(2)}, u32[]{:S(2)}) collective-permute-start(f32[256,256]{1,0:T(8,128)} %fusion.4), channel_id=1, source_target_pairs={{0,1},{1,0},{2,3},{3,2},{4,5},{5,4},{6,7},{7,6},{8,9},{9,8},{10,11... | collective-permute-start | bytes 786440 | tf_op jit(solution)/shard_map/ppermute | solution.py:415
  135.7 30.5 %all-to-all-start.1 = ((f32[16,112,256]{2,1,0:T(8,128)}), f32[16,112,256]{2,1,0:T(8,128)}, u32[]{:S(2)}, u32[]{:S(2)}) async-start(f32[16,112,256]{2,1,0:T(8,128)} %middle.1), calls=%async_computation.1 | async-start | bytes 3670016 | tf_op jit(solution)/shard_map/all_to_all | solution.py:496
  (12 other events, 75.8 us)

commit v2 on v1

v2 whole, which is shorter than its diff:
```python
import functools

import jax
import jax.numpy as jnp
from jax import lax
from jax.experimental import pallas as pl
from jax.experimental.pallas import tpu as pltpu
from jax.sharding import PartitionSpec as P

ROW = "row"
COL = "col"
RING = 4
VMEM = pl.BlockSpec(memory_space=pltpu.VMEM)
HBM = pl.BlockSpec(memory_space=pltpu.HBM)


def product(left, right):
    return jnp.dot(left, right, precision=lax.Precision.HIGHEST, preferred_element_type=jnp.float32)


def split(value):
    high = value.astype(jnp.bfloat16)
    return high, (value - high.astype(jnp.float32)).astype(jnp.bfloat16)


def product_split(left, right_high, right_low):
    left_high, left_low = split(left)
    dot = functools.partial(jnp.dot, preferred_element_type=jnp.float32)
    return dot(left_high, right_high) + (dot(left_low, right_high) + dot(left_high, right_low))


def masks(width):
    rows = lax.broadcasted_iota(jnp.int32, (width, width), 0)
    cols = lax.broadcasted_iota(jnp.int32, (width, width), 1)
    return rows > cols, rows == cols


def tril(matrix):
    below, diag = masks(matrix.shape[0])
    return jnp.where(below | diag, matrix, 0.0)


def halved_lower(matrix):
    below, diag = masks(matrix.shape[0])
    return jnp.where(below, matrix, jnp.where(diag, 0.5 * matrix, 0.0))


def params(megabytes):
    return pltpu.CompilerParams(vmem_limit_bytes=megabytes << 20)


def cost(flops, bytes_accessed):
    return pl.CostEstimate(flops=flops, bytes_accessed=bytes_accessed, transcendentals=0)


def in_hbm(value):
    return pltpu.with_memory_space_constraint(value, pltpu.HBM)


def tile_shape(*shape):
    return jax.ShapeDtypeStruct(shape, jnp.float32)


def invert_kernel(tiles, adj, a0, out, out_t, base, power, total, held, sems):
    width = tiles.shape[-1]
    low, left = 2 * width, 4 * width
    q = lax.axis_index(COL)
    half = low // 2
    keep = [(slice(i * half, (i + 1) * half), slice(0, adj.shape[1])) for i in range(2)]
    keep += [(slice(low + i * half, low + (i + 1) * half), slice(left, adj.shape[1])) for i in range(2)]
    stage = [held.at[i, :, slice(0, at[1].stop - at[1].start)] for i, at in enumerate(keep)]
    loads = [pltpu.make_async_copy(adj.at[at], dst, sems.at[i]) for i, (at, dst) in enumerate(zip(keep, stage))]
    stores = [pltpu.make_async_copy(src, base.at[at], sems.at[i + 4]) for i, (at, src) in enumerate(zip(keep, stage))]
    for load in loads:
        load.start()
    below, diag = masks(width)
    scales = []
    for j in range(2):
        tile = tiles[j]
        out_t[j] = tile.T
        only = jnp.where(diag, tile, 0.0)
        power[j] = jnp.where(below, tile / jnp.sum(only, axis=1, keepdims=True), 0.0)
        total[j] = jnp.where(diag, 1.0, 0.0) - power[j]
        scales.append(1.0 / jnp.sum(only, axis=0, keepdims=True))

    for load in loads:
        load.wait()

    @pl.when(q == 0)
    def _():
        for i in range(2):
            held[2 + i, :, :width] = a0[i * half : (i + 1) * half, :]

    for store in stores:
        store.start()

    @pl.loop(0, (width - 1).bit_length() - 1)
    def _(step):
        for j in range(2):
            power[j] = product(power[j], power[j])
        for j in range(2):
            total[j] = total[j] + product(total[j], power[j])

    for j in range(2):
        out[j] = (total[j] * scales[j]).T
    for store in stores:
        store.wait()


def invert(tiles, adjoint, a0):
    w = tiles.shape[-1]
    return pl.pallas_call(
        invert_kernel,
        out_shape=(pltpu.HBM((2, w, w), jnp.float32),) * 2 + (pltpu.HBM(adjoint.shape, jnp.float32),),
        in_specs=[VMEM, HBM, VMEM],
        out_specs=(VMEM,) * 2 + (HBM,),
        scratch_shapes=[pltpu.VMEM((2, w, w), jnp.float32)] * 2
        + [pltpu.VMEM((4, w, adjoint.shape[1]), jnp.float32), pltpu.SemaphoreType.DMA((8,))],
        compiler_params=params(14),
        cost_estimate=cost(28 * 12 * w**3, 1 << 20),
        name="invert",
    )(tiles, in_hbm(adjoint), in_hbm(a0))


def corner_kernel(own, down, up, across_first, out, held, sems):
    w = out.shape[0]
    quarter = w // RING
    z = lax.axis_index(ROW) // RING
    left = own.shape[-1]
    tile = (slice(None), slice(left - w, left))
    sources = (own.at[(0,) + tile], down.at[(0,) + tile], across_first.at[tile], up.at[(0,) + tile])
    fetches = [pltpu.make_async_copy(src, held.at[k], sems.at[k]) for k, src in enumerate(sources)]
    for fetch in fetches:
        fetch.start()
    for fetch in fetches:
        fetch.wait()
    for k in range(RING):
        start = pl.multiple_of(lax.rem(z + k, RING) * quarter, quarter)
        out[pl.ds(start, quarter), :] = held[k]


def gather_corner(own, down, up, across_first):
    w = own.shape[1] * RING
    return pl.pallas_call(
        corner_kernel,
        out_shape=tile_shape(w, w),
        in_specs=[HBM] * 4,
        out_specs=VMEM,
        scratch_shapes=[
            pltpu.VMEM((RING, w // RING, w), jnp.float32),
            pltpu.SemaphoreType.DMA((RING,)),
        ],
        compiler_params=params(4),
        cost_estimate=cost(1 << 10, 1 << 19),
        name="corner",
    )(*[in_hbm(value) for value in (own, down, up, across_first)])


def small_rows(w, rows):
    return -(-3 * (w // lax.axis_size(COL) // rows) // 8) * 8


def sums_kernel(even_top, even_bottom, odd_top, odd_bottom, inv0, factor, out, a0_out, l1_out, high, low, small, tall):
    step = pl.program_id(0)
    w = inv0.shape[0]
    rows = lax.axis_size(ROW)
    first = lax.axis_index(ROW) == 0
    per_step = w // (w * 4 // rows)
    cols = 4 * w // rows
    piece = small.shape[1] // rows

    @pl.when(step == 0)
    def _():
        cut = w // 2
        l0, l1 = even_top[: 2 * w], odd_top[: 2 * w]
        c0 = jnp.concatenate([even_top[2 * w :], even_bottom[: 2 * w - cut]], axis=0)
        c1 = jnp.concatenate([odd_top[2 * w :], odd_bottom[: 2 * w - cut]], axis=0)
        skip = first & (lax.broadcasted_iota(jnp.int32, l0.shape, 0) < w)
        a0 = jnp.where(skip, 0.0, product(l0, inv0[...]))
        below = jnp.where(skip, 0.0, l1)
        a0_out[...] = a0
        l1_out[...] = below
        high[:, :w], low[:, :w] = split(a0)
        high[:, w:], low[:, w:] = split(below)
        tall[0] = a0.T
        tall[1] = below.T
        share = w // lax.axis_size(COL)
        mine = pl.ds(pl.multiple_of(lax.axis_index(COL) * share, share), share)
        diag_below = jnp.where(skip, 0.0, c0)
        next_below = jnp.where(skip, 0.0, c1)
        raw_next = jnp.where(first, l1[:w], 0.0)
        tall[2, :, :w] = c1[:w].T
        small[0] = jnp.where(first, even_top[mine, :], 0.0) - product(tall[0, mine, :], diag_below)
        small[1] = jnp.where(first, odd_top[mine, :], 0.0) - product(tall[0, mine, :], next_below)
        small[2] = product(tall[1, mine, :], next_below) - product(tall[2, mine, :w], raw_next)

    part = product_split(factor[...].T, high[...], low[...])
    out[:, :cols, :] = part[:, :w].reshape(per_step, cols, w)
    out[:, cols : 2 * cols, :] = part[:, w:].reshape(per_step, cols, w)
    lines = per_step * piece
    for j in range(3):
        part = small[j, pl.ds(pl.multiple_of(step * lines, lines), lines), :]
        at = 2 * cols + j * piece
        out[:, at : at + piece, :] = part.reshape(per_step, piece, w)
    at = 2 * cols + 3 * piece
    out[:, at:, :] = jnp.zeros((per_step, out.shape[1] - at, w), jnp.float32)


def sums(even_top, even_bottom, odd_top, odd_bottom, inv0, factor):
    w = inv0.shape[0]
    rows = lax.axis_size(ROW)
    share = w // lax.axis_size(COL)
    height = 2 * (4 * w // rows) + small_rows(w, rows)
    const = lambda i: (0, 0)
    whole = lambda value: pl.BlockSpec(value.shape, const, pipeline_mode=pl.Buffered(1))
    return pl.pallas_call(
        sums_kernel,
        grid=(4,),
        out_shape=(pltpu.HBM((rows, height, w), jnp.float32),)
        + (pltpu.HBM((2 * w, w), jnp.float32),) * 2,
        in_specs=[whole(even_top), whole(even_bottom), whole(odd_top), whole(odd_bottom), whole(inv0)]
        + [pl.BlockSpec((2 * w, w), lambda i: (1, i))],
        out_specs=(
            pl.BlockSpec((rows // 4, height, w), lambda i: (i, 0, 0)),
            pl.BlockSpec((2 * w, w), const),
            pl.BlockSpec((2 * w, w), const),
        ),
        scratch_shapes=[
            pltpu.VMEM((2 * w, 2 * w), jnp.bfloat16),
            pltpu.VMEM((2 * w, 2 * w), jnp.bfloat16),
            pltpu.VMEM((3, share, w), jnp.float32),
            pltpu.VMEM((3, w, 2 * w), jnp.float32),
        ],
        compiler_params=params(14),
        cost_estimate=cost(4 << 30, 8 << 20),
        name="sums",
    )(even_top, even_bottom, odd_top, odd_bottom, inv0, in_hbm(factor))


def middle_kernel(terms, r31, inv1, out, out_small, r31_v, inv1_v, out_v, small_v, sems):
    rows, cols = out.shape[:2]
    fetches = [
        pltpu.make_async_copy(r31, r31_v, sems.at[0]),
        pltpu.make_async_copy(inv1, inv1_v, sems.at[1]),
    ]
    for fetch in fetches:
        fetch.start()
    small = terms[0, 2 * cols :, :]
    for i in range(1, rows):
        small = small + terms[i, 2 * cols :, :]
    for i in range(rows):
        small_v[i] = small
    stores = [pltpu.make_async_copy(small_v, out_small, sems.at[2])]
    stores[0].start()
    total = terms[0, : 2 * cols, :]
    for i in range(1, rows):
        total = total + terms[i, : 2 * cols, :]
    top = total[:cols]
    for fetch in fetches:
        fetch.wait()
    out_v[0] = top
    out_v[1] = product(total[cols:] - product(top, r31_v[...]), inv1_v[...])
    stores += [pltpu.make_async_copy(out_v.at[min(i, 1)], out.at[i], sems.at[3 + i]) for i in range(rows)]
    for store in stores[1:]:
        store.start()
    for store in stores:
        store.wait()


def middle(terms, r31, inv1):
    rows, height, w = terms.shape
    small = small_rows(w, rows)
    cols = (height - small) // 2
    return pl.pallas_call(
        middle_kernel,
        out_shape=(pltpu.HBM((rows, cols, w), jnp.float32), pltpu.HBM((rows, small, w), jnp.float32)),
        in_specs=[VMEM, HBM, HBM],
        out_specs=(HBM, HBM),
        scratch_shapes=[
            pltpu.VMEM((w, w), jnp.float32),
            pltpu.VMEM((w, w), jnp.float32),
            pltpu.VMEM((2, cols, w), jnp.float32),
            pltpu.VMEM((rows, small, w), jnp.float32),
            pltpu.SemaphoreType.DMA((3 + rows,)),
        ],
        compiler_params=params(10),
        cost_estimate=cost(1 << 28, 6 << 20),
        name="middle",
    )(terms, in_hbm(r31), in_hbm(inv1))


def trail_kernel(
    adj, a0, l1, inv1, r31, own, down, up, across_first, across_second, base, out, r_high, r_low,
    small, own_v, down_v, up_v, first_v, second_v, sems
):
    step = pl.program_id(0)
    w = inv1.shape[0]
    left = 4 * w
    q = lax.axis_index(COL)
    last_q = lax.axis_size(COL) - 1
    z = lax.axis_index(ROW) // RING

    @pl.when(step == 0)
    def _():
        sources = (own, down, up, across_first, across_second)
        targets = (own_v, down_v, up_v, first_v, second_v)
        fetches = [
            pltpu.make_async_copy(src, dst, sems.at[i]) for i, (src, dst) in enumerate(zip(sources, targets))
        ]
        for fetch in fetches:
            fetch.start()
        small[0], small[1] = split(inv1[...])
        small[2], small[3] = split(product(r31[...], inv1[...]))
        for fetch in fetches:
            fetch.wait()
        quarter = w // RING
        for j in range(2):
            values = (own_v[j], down_v[j], (first_v, second_v)[j][...], up_v[j])
            for k, value in enumerate(values):
                start = pl.multiple_of(j * w + lax.rem(z + k, RING) * quarter, quarter)
                high, low = split(value)
                r_high[pl.ds(start, quarter), :] = high
                r_low[pl.ds(start, quarter), :] = low

    first = a0[...]
    second = product_split(l1[...], small[0], small[1]) - product_split(first, small[2], small[3])
    lhs = jnp.concatenate([first, second], axis=1)
    out[...] = adj[...] - product_split(lhs, r_high[...], r_low[...])

    @pl.when(q == last_q)
    def _():
        out[:, left - w :] = second


def trail(adjoint, base, a0, l1, inv1, r31, *pieces):
    rows, cols = adjoint.shape
    w = inv1.shape[0]
    steps = 4
    blk = rows // 2 // steps
    low = lambda i: (i, 0)
    block = lambda i: (steps + i, 0)
    const = lambda i: (0, 0)
    one = pl.Buffered(1)
    panel = pltpu.HBM((2 * w, 4 * w), jnp.bfloat16)
    return pl.pallas_call(
        trail_kernel,
        grid=(steps,),
        out_shape=(pltpu.HBM(adjoint.shape, jnp.float32), panel, panel),
        in_specs=[
            pl.BlockSpec((blk, 4 * w), block),
            pl.BlockSpec((blk, w), low),
            pl.BlockSpec((blk, w), low),
            pl.BlockSpec(inv1.shape, const, pipeline_mode=one),
            pl.BlockSpec(r31.shape, const, pipeline_mode=one),
        ]
        + [HBM] * (len(pieces) + 1),
        out_specs=(
            pl.BlockSpec((blk, 4 * w), block),
            pl.BlockSpec(panel.shape, const),
            pl.BlockSpec(panel.shape, const),
        ),
        scratch_shapes=[pltpu.VMEM((4, w, w), jnp.bfloat16)]
        + [pltpu.VMEM(piece.shape, jnp.float32) for piece in pieces]
        + [pltpu.SemaphoreType.DMA((len(pieces),))],
        input_output_aliases={5 + len(pieces): 0},
        compiler_params=params(16),
        cost_estimate=cost(4 << 30, 10 << 20),
        name="trail",
    )(
        in_hbm(adjoint),
        in_hbm(a0),
        in_hbm(l1),
        in_hbm(inv1),
        in_hbm(r31),
        *[in_hbm(piece) for piece in pieces],
        in_hbm(base),
    )


def chain_kernel(
    mine, before, after, across, theirs, inverse, inverse_t, diag_t, diag31, r31, lhs, corner, diag, tiles
):
    w = inverse.shape[-1]
    rows = mine.shape[0]
    p = lax.axis_index(ROW)
    q = lax.axis_index(COL)
    share = w // lax.axis_size(COL)
    piece = share // rows

    @pl.when((p == 0) | (p == rows - 1))
    def _():
        core = lax.rem(q, 2)
        for k, shared in ((0, mine), (1, after), (2, across), (3, before)):
            chip = lax.rem(q // 2 + k, RING)
            for other in range(2):
                at = chip * 2 + (1 - core if other else core)
                target = pl.ds(pl.multiple_of(at * share, share), share)
                for j in range(3):
                    lines = slice(j * piece, (j + 1) * piece)
                    value = theirs[k, :, lines, :] if other else shared[:, lines, :]
                    tiles[j, target, :] = value.reshape(share, w)
        t01, x11 = tiles[1], tiles[2]

        def adjoint_diag(j, dprime):
            inner = halved_lower(product(diag_t[j], tril(dprime)))
            wmat = product(product(inverse_t[j], inner), inverse[j])
            return wmat + wmat.T

        known = r31[...]
        side = product(inverse_t[1], x11 + product(known.T, t01))
        g0 = adjoint_diag(0, tiles[0])
        a132 = product(t01 - product(g0, known), inverse[1])
        diag[...] = halved_lower(g0)

        @pl.when(p == 0)
        def _():
            lhs[:, :w] = g0
            lhs[:, w:] = a132
            corner[...] = a132

        @pl.when(p != 0)
        def _():
            a132_t = a132.T
            g1 = adjoint_diag(1, diag31[...] - side - product(a132_t, known))
            lhs[:, :w] = a132_t
            lhs[:, w:] = g1
            corner[...] = halved_lower(g1)


def chain(*operands):
    w = operands[5].shape[-1]
    return pl.pallas_call(
        chain_kernel,
        out_shape=tuple(pltpu.HBM((w, n * w), jnp.float32) for n in (2, 1, 1)),
        in_specs=[VMEM] * len(operands),
        out_specs=(VMEM,) * 3,
        scratch_shapes=[pltpu.VMEM((3, w, w), jnp.float32)],
        compiler_params=params(14),
        cost_estimate=cost(1 << 20, 1 << 10),
        name="chain",
    )(*operands)


def final_kernel(base, got, lhs, corner, diag, r_high, r_low, out, *scratch):
    got_v, lhs_v, corner_v, diag_v, r_high_v, r_low_v, rows_buf, sems = scratch
    rows, cols, w = got.shape
    left = 4 * w
    p = lax.axis_index(ROW)
    q = lax.axis_index(COL)
    last_q = lax.axis_size(COL) - 1

    @pl.when((p == 0) | (p == rows - 1))
    def _():
        start = jnp.where(p == 0, 2 * w, w)
        region = (pl.ds(start, w), pl.ds(0, left))
        moves = [
            (lhs, lhs_v),
            (r_high, r_high_v),
            (r_low, r_low_v),
            (base.at[region], rows_buf),
            (got, got_v),
            (corner, corner_v),
            (diag, diag_v),
        ]
        fetches = [pltpu.make_async_copy(src, dst, sems.at[i]) for i, (src, dst) in enumerate(moves)]
        for fetch in fetches:
            fetch.start()
        for fetch in fetches:
            fetch.wait()
        stores = []
        for j in range(4):
            at = slice(j * w, (j + 1) * w)
            piece = rows // 4
            value = rows_buf[:, at] - got_v[j * piece : (j + 1) * piece].reshape(w, w).T
            rows_buf[:, at] = value - product_split(lhs_v[...], r_high_v[:, at], r_low_v[:, at])
            if j == 3:

                @pl.when(q == last_q)
                def _():
                    rows_buf[:, at] = corner_v[...]

            stores.append(
                pltpu.make_async_copy(
                    rows_buf.at[:, at], out.at[pl.ds(start, w), at], sems.at[len(moves) + j]
                )
            )
            stores[-1].start()

        @pl.when((p == 0) & (q == 0))
        def _():
            store = pltpu.make_async_copy(
                diag_v, out.at[pl.ds(2 * w, w), pl.ds(left, w)], sems.at[len(moves) + 4]
            )
            store.start()
            store.wait()

        for store in stores:
            store.wait()


def final(base, *operands):
    w = operands[1].shape[0]
    return pl.pallas_call(
        final_kernel,
        out_shape=tile_shape(*base.shape),
        in_specs=[HBM] * (1 + len(operands)),
        out_specs=HBM,
        scratch_shapes=[
            pltpu.VMEM(operands[i].shape, operands[i].dtype) for i in range(len(operands))
        ]
        + [pltpu.VMEM((w, 4 * w), jnp.float32), pltpu.SemaphoreType.DMA((12,))],
        input_output_aliases={0: 0},
        compiler_params=params(16),
        cost_estimate=cost(2 << 30, 8 << 20),
        name="final",
    )(base, *[in_hbm(value) for value in operands])


def column_hops(top, bottom):
    q = lax.axis_index(COL)
    last = lax.axis_size(COL) - 1
    near, far = [(0, 2), (last, last - 2)], [(0, last - 1), (last, 1)]
    near_top = lax.ppermute(top, COL, near)
    far_bottom = lax.ppermute(bottom, COL, far)
    near_bottom = lax.ppermute(bottom, COL, near)
    far_top = lax.ppermute(top, COL, far)
    upper = lax.ppermute(near_top, COL, [(2, 4), (last - 2, last - 4)])
    lower = lax.ppermute(far_bottom, COL, [(last - 1, 4), (1, last - 4)])

    def choose(own, near_value, far_value, across):
        value = jnp.where((q == 1) | (q == last - 1), far_value, across)
        value = jnp.where((q == 2) | (q == last - 2), near_value, value)
        return jnp.where((q == 0) | (q == last), own, value)

    return choose(top, near_top, far_top, upper), choose(bottom, near_bottom, far_bottom, lower)


def column_swap(mine):
    theirs = lax.ppermute(mine, COL, [(i, i ^ 1) for i in range(lax.axis_size(COL))])
    even = lax.axis_index(COL) % 2 == 0
    return jnp.where(even, mine, theirs), jnp.where(even, theirs, mine)


def row_quarters(block):
    p = lax.axis_index(ROW)
    last = lax.axis_size(ROW) - 1
    top = RING - 1
    quarters = block.reshape(RING, -1, block.shape[1])
    first = p == 0
    near = lax.ppermute(
        jnp.where(first, quarters[1], quarters[top - 1]), ROW, [(0, RING), (last, last - RING)]
    )
    far = lax.ppermute(jnp.where(first, quarters[top], quarters[0]), ROW, [(0, last - top), (last, top)])
    across = lax.ppermute(
        jnp.where(first, quarters[2], quarters[1]), ROW, [(0, 2 * RING), (last, last - 2 * RING)]
    )
    mine = jnp.where(first, quarters[0], quarters[top])
    mine = jnp.where((p == RING) | (p == last - RING), near, mine)
    mine = jnp.where((p == last - top) | (p == top), far, mine)
    return jnp.where((p == 2 * RING) | (p == last - 2 * RING), across, mine)


def row_spread(mine):
    top = RING - 1
    x = lax.axis_index(ROW) % RING
    lines = range(0, lax.axis_size(ROW), RING)
    near = lax.ppermute(mine, ROW, [e for s in lines for e in ((s, s + 1), (s + top, s + top - 1))])
    far = lax.ppermute(mine, ROW, [e for s in lines for e in ((s, s + top), (s + top, s))])
    across = lax.ppermute(mine, ROW, [e for s in lines for e in ((s, s + 2), (s + top, s + top - 2))])
    from_first = jnp.where(x == 0, mine, jnp.where(x == 1, near, jnp.where(x == 2, across, far)))
    from_last = jnp.where(x == top, mine, jnp.where(x == 2, near, jnp.where(x == 1, across, far)))
    return jnp.stack([from_first, from_last])


def ring_pairs(step):
    count = lax.axis_size(ROW)
    return [(i, (i + step * RING) % count) for i in range(count)]


def per_device(factor, adjoint, inverse):
    w = inverse.shape[-1]
    rows = lax.axis_size(ROW)
    p = lax.axis_index(ROW)
    q = lax.axis_index(COL)
    low, left = 2 * w, 4 * w

    start = jnp.where(q == 0, left, left - w)
    adj_col = lax.dynamic_slice(adjoint, (low, start), (low, w))
    fac_col = lax.dynamic_slice(factor, (low, start), (low, w))
    cut = w // 2
    top = jnp.concatenate([adj_col, fac_col[:cut]], axis=0)
    bottom = jnp.concatenate([fac_col[cut:], adjoint[w:low, left - w : left]], axis=0)
    row_block = lax.dynamic_slice(factor, (jnp.where(p == 0, low, w), 0), (w, left))
    quarter = row_quarters(row_block)
    top, bottom, quarter = lax.optimization_barrier((top, bottom, quarter))
    top, bottom = column_hops(top, bottom)
    own = row_spread(quarter)
    up = lax.ppermute(own, ROW, ring_pairs(1))
    down = lax.ppermute(own, ROW, ring_pairs(-1))
    top, bottom, up, down = lax.optimization_barrier((top, bottom, up, down))
    even_top, odd_top = column_swap(top)
    even_bottom, odd_bottom = column_swap(bottom)
    terms, a0, l1_below = sums(
        even_top, even_bottom, odd_top, odd_bottom, inverse[0], factor
    )
    across_first = lax.ppermute(up[0], ROW, ring_pairs(1))
    across_second = lax.ppermute(down[1], ROW, ring_pairs(-1))
    terms, across_first, across_second = lax.optimization_barrier((terms, across_first, across_second))
    terms = lax.all_to_all(terms, ROW, 0, 0)
    diag_t, inverse_t, base = invert(inverse, adjoint, a0)

    r31 = gather_corner(own, down, up, across_first)
    last = lax.axis_size(COL) - 1
    near = lax.ppermute(r31, COL, [(last, last - 2)])
    far = lax.ppermute(r31, COL, [(last, 1)])
    across = lax.ppermute(r31, COL, [(last, last - 4)])
    r31 = jnp.where(q == last - 2, near, jnp.where(q == 1, far, jnp.where(q == last - 4, across, r31)))
    r31 = jnp.where(q % 2 == 1, r31, lax.ppermute(r31, COL, [(i, i - 1) for i in range(1, last + 1, 2)]))
    terms, diag_t, inverse_t, base = lax.optimization_barrier((terms, diag_t, inverse_t, base))
    shares, small = middle(terms, r31, inverse[1])
    small = lax.all_to_all(small, ROW, 0, 0)
    base, r_high, r_low = trail(
        adjoint, base, a0, l1_below, inverse[1], r31, own, down, up, across_first, across_second
    )
    small, shares, base, r_high, r_low = lax.optimization_barrier((small, shares, base, r_high, r_low))
    shares = lax.all_to_all(shares, ROW, 0, 0)
    count = lax.axis_size(COL)
    before, after, across = (
        lax.ppermute(small, COL, [(i, (i + step) % count) for i in range(count)]) for step in (2, -2, 4)
    )
    theirs = lax.ppermute(
        jnp.stack([small, after, across, before]), COL, [(i, i ^ 1) for i in range(count)]
    )
    lhs, corner, diag = chain(
        small, before, after, across, theirs, inverse, inverse_t, diag_t, odd_bottom[low - cut :], r31
    )
    return final(base, shares, lhs, corner, diag, r_high, r_low)


def solution(mesh):
    return jax.shard_map(
        per_device,
        mesh=mesh,
        in_specs=(P(ROW, COL), P(ROW, COL), P()),
        out_specs=P(ROW, COL),
        check_vma=False,
    )
```

time: 177 us -> 157 us (0.89)
  waiting for transfers between devices: 64.4 us -> 39.3 us
  starting transfers between devices: 46.3 us -> 58.7 us
  local copies, waits for them, and re-layouts: 12 us -> 6.26 us
  other arithmetic: 9.69 us -> 7.81 us
    all_to_all x1 -> x2, waiting for transfers between devices: 11.4 us -> 1.96 us  [the longest x1 1.95 us: per_device(): shares = lax.all_to_all(shares, ROW, 0, 0)]
    ppermute x8 -> x14, waiting for transfers between devices: 21.9 us -> 14.5 us  [the longest x1 6.91 us: column_hops(): lower = lax.ppermute(far_bottom, COL, [(last - 1, 4), (1, last - 4)])]
    all_to_all x1 -> x2, starting transfers between devices: 4.68 us -> 10.9 us  [the longest x1 7.28 us: per_device(): shares = lax.all_to_all(shares, ROW, 0, 0)]
    slice x9 -> x3, local copies, waits for them, and re-layouts: 7.38 us -> 1.97 us  [the longest x1 1.03 us: per_device(): fac_col[cut:]]
    pallas_call x1, Pallas kernels: 9.59 us -> 4.41 us  [final(): pl.pallas_call(final_kernel, out_shape=tile_shape(*base.shape), in_specs=...]
    ppermute x1, waiting for transfers between devices: 4.96 us -> 0.51 us  [per_device(): across_first = lax.ppermute(up[0], ROW, ring_pairs(1))]
    ppermute x8 -> x14, starting transfers between devices: 10 us -> 14.3 us  [the longest x3 2.57 us: per_device(): lax.ppermute(small, COL, [(i, (i + step) % count) for i in range(count)])]
    pallas_call x1, Pallas kernels: 9.81 us -> 13.6 us  [invert(): pl.pallas_call(invert_kernel, out_shape=(pltpu.HBM((2, w, w), jnp.float32...]
  transfers between devices with their start and end apart: 22 -> 29, of which waited for: 13 -> 13; matrix products, arithmetic and copies ran while one was open for 7% -> 6% of each run, Pallas kernels for 17% -> 23%
where the time goes in v2:
time: 157 us; the launch traced here: 155 us
  starting transfers between devices  58.7 us (37%)
  Pallas kernels  42.4 us (27%)
  waiting for transfers between devices  39.3 us (25%)
  other arithmetic  7.81 us (5%)
  local copies, waits for them, and re-layouts  6.26 us (4%)
    pallas_call x1, Pallas kernels, invert(): pl.pallas_call(invert_kernel, out_shape=(pltpu.HBM((2, w, w), jnp.float32...  13.6 us
    all_to_all x1, waiting for transfers between devices, per_device(): terms = lax.all_to_all(terms, ROW, 0, 0)  10.9 us
    pallas_call x1, Pallas kernels, trail(): pl.pallas_call(trail_kernel, grid=(steps,), out_shape=(pltpu.HBM(adjoint....  8.55 us
    pallas_call x1, Pallas kernels, sums(): pl.pallas_call(sums_kernel, grid=(4,), out_shape=(pltpu.HBM((rows, height...  7.29 us
    all_to_all x1, starting transfers between devices, per_device(): shares = lax.all_to_all(shares, ROW, 0, 0)  7.28 us
    ppermute x1, waiting for transfers between devices, column_hops(): lower = lax.ppermute(far_bottom, COL, [(last - 1, 4), (1, last - 4)])  6.91 us
    all_to_all x1, starting transfers between devices, per_device(): terms = lax.all_to_all(terms, ROW, 0, 0)  6.7 us
    ppermute x1, starting transfers between devices, row_spread(): lax.ppermute(mine, ROW, [e for s in lines for e in ((s, s + top), (s + to...  5.99 us
  transfers between devices with their start and end apart: 29, of which 13 were waited for; matrix products, arithmetic and copies ran while one was open for 6% of the time, Pallas kernels for 23%

profile of v2, /device:TPU:16, one launch (start us, length us, event | category | flops | bytes accessed | tf_op | source)
XLA Modules:
  0.0 155.0 jit_solution(6960214876836980482)
XLA Ops:
  0.0 2.0 %dynamic-slice_select_fusion.1 = (f32[64,1024]{1,0:T(8,128)}, f32[64,1024]{1,0:T(8,128)S(1)}, f32[64,1024]{1,0:T(8,128)S(1)}) fusion(f32[1024,2048]{1,0:T(8,128)} %factor.1, s32[]{:T(128)S(6)} %add.16, s32[]{:T(128)S(6)} %add.15, pred[]{:T(512)S(6)} %eq.83, s32[]{:T(128)S(6)} %select_n.177, s32[]{:T(128)S(6)} %add.17), kind=kLoop, calls=%fused_computation.19 | loop fusion | flops 196608 | bytes 1835025 | tf_op jit(solution)/shard_map/jit(_where)/select_n | solution.py:551
  2.0 4.7 %collective-permute-start.2 = (f32[64,1024]{1,0:T(8,128)}, f32[64,1024]{1,0:T(8,128)}, u32[]{:S(2)}, u32[]{:S(2)}) collective-permute-start(f32[64,1024]{1,0:T(8,128)} %get-tuple-element.71), channel_id=1, source_target_pairs={{0,32},{120,88},{1,33},{121,89},{2,34},{122,90},{3,35},{123,91},{4... | collective-permute-start | bytes 786440 | tf_op jit(solution)/shard_map/ppermute | solution.py:550
  6.6 3.3 %collective-permute-start = (f32[64,1024]{1,0:T(8,128)S(1)}, f32[64,1024]{1,0:T(8,128)}, u32[]{:S(2)}, u32[]{:S(2)}) collective-permute-start(f32[64,1024]{1,0:T(8,128)S(1)} %get-tuple-element.72), channel_id=1, source_target_pairs={{0,64},{120,56},{1,65},{121,57},{2,66},{122,58},{3,67},{123,59},{4... | collective-permute-start | bytes 786440 | tf_op jit(solution)/shard_map/ppermute | solution.py:554
  10.0 2.0 %collective-permute-start.1 = (f32[64,1024]{1,0:T(8,128)S(1)}, f32[64,1024]{1,0:T(8,128)}, u32[]{:S(2)}, u32[]{:S(2)}) collective-permute-start(f32[64,1024]{1,0:T(8,128)S(1)} %get-tuple-element.73), channel_id=1, source_target_pairs={{0,96},{120,24},{1,97},{121,25},{2,98},{122,26},{3,99},{123,27},{4... | collective-permute-start | bytes 786440 | tf_op jit(solution)/shard_map/ppermute | solution.py:553
  19.8 6.0 %collective-permute-start.11 = (f32[64,1024]{1,0:T(8,128)S(1)}, f32[64,1024]{1,0:T(8,128)S(1)}, u32[]{:S(2)}, u32[]{:S(2)}) collective-permute-start(f32[64,1024]{1,0:T(8,128)S(1)} %select_select_fusion.3), channel_id=1, source_target_pairs={{0,24},{24,0},{32,56},{56,32},{64,88},{88,64},{96,120},{120,96},{1... | collective-permute-start | bytes 786440 | tf_op jit(solution)/shard_map/ppermute | solution.py:568
  28.6 2.0 %collective-permute-start.10 = (f32[64,1024]{1,0:T(8,128)S(1)}, f32[64,1024]{1,0:T(8,128)}, u32[]{:S(2)}, u32[]{:S(2)}) collective-permute-start(f32[64,1024]{1,0:T(8,128)S(1)} %select_select_fusion.3), channel_id=1, source_target_pairs={{0,16},{24,8},{32,48},{56,40},{64,80},{88,72},{96,112},{120,104},{... | collective-permute-start | bytes 786440 | tf_op jit(solution)/shard_map/ppermute | solution.py:569
  32.5 2.0 %collective-permute-start.9 = (f32[64,1024]{1,0:T(8,128)S(1)}, f32[64,1024]{1,0:T(8,128)}, u32[]{:S(2)}, u32[]{:S(2)}) collective-permute-start(f32[64,1024]{1,0:T(8,128)S(1)} %select_select_fusion.3), channel_id=1, source_target_pairs={{0,8},{24,16},{32,40},{56,48},{64,72},{88,80},{96,104},{120,112},{... | collective-permute-start | bytes 786440 | tf_op jit(solution)/shard_map/ppermute | solution.py:567
  36.8 3.8 %collective-permute-done.9 = f32[64,1024]{1,0:T(8,128)} collective-permute-done((f32[64,1024]{1,0:T(8,128)S(1)}, f32[64,1024]{1,0:T(8,128)}, u32[]{:S(2)}, u32[]{:S(2)}) %collective-permute-start.9) | collective-permute-done | bytes 262176 | tf_op jit(solution)/shard_map/ppermute | solution.py:567
  41.8 2.2 %collective-permute-start.13 = (f32[2,64,1024]{2,1,0:T(8,128)S(1)}, f32[2,64,1024]{2,1,0:T(8,128)S(1)}, u32[]{:S(2)}, u32[]{:S(2)}) collective-permute-start(f32[2,64,1024]{2,1,0:T(8,128)S(1)} %pad_maximum_fusion.2.own), channel_id=1, source_target_pairs={{0,96},{8,104},{16,112},{24,120},{32,0},{40,8},{48,16},{56,24},{64... | collective-permute-start | bytes 1572872 | tf_op jit(solution)/shard_map/ppermute | solution.py:599
  47.2 6.9 %collective-permute-done.8 = f32[640,256]{1,0:T(8,128)S(1)} collective-permute-done((f32[640,256]{1,0:T(8,128)S(1)}, f32[640,256]{1,0:T(8,128)S(1)}, u32[]{:S(2)}, u32[]{:S(2)}) %collective-permute-start.8) | collective-permute-done | bytes 655392 | tf_op jit(solution)/shard_map/ppermute | solution.py:528
  54.3 3.4 %collective-permute-done.13.down = f32[2,64,1024]{2,1,0:T(8,128)S(1)} collective-permute-done((f32[2,64,1024]{2,1,0:T(8,128)S(1)}, f32[2,64,1024]{2,1,0:T(8,128)S(1)}, u32[]{:S(2)}, u32[]{:S(2)}) %collective-permute-start.13) | collective-permute-done | bytes 524320 | tf_op jit(solution)/shard_map/ppermute | solution.py:599
  63.1 7.3 %sums.1 = (f32[16,136,256]{2,1,0:T(8,128)}, f32[512,256]{1,0:T(8,128)}, f32[512,256]{1,0:T(8,128)}) custom-call(f32[640,256]{1,0:T(8,128)S(1)} %get-tuple-element.77.even_top, f32[640,256]{1,0:T(8,128)S(1)} %get-tuple-element.75.even_bottom, f32[640,256]{1,0:T(8,128)S(1)} %get-tuple-element.76.odd_top, f32[640,256]{1,0:T(8,128)S(1)} %get-tuple-element.74.odd_bottom, ...), custom_call_target="tpu_custom_call" | custom-call | flops 4294967296 | bytes 8388608 | tf_op jit(solution)/shard_map/sums/pallas_call | solution.py:216
  71.7 6.7 %all-to-all-start = ((f32[16,136,256]{2,1,0:T(8,128)}), f32[16,136,256]{2,1,0:T(8,128)S(1)}, u32[]{:S(2)}, u32[]{:S(2)}) async-start(f32[16,136,256]{2,1,0:T(8,128)} %get-tuple-element.46), calls=%async_computation | async-start | bytes 4456448 | tf_op jit(solution)/shard_map/all_to_all | solution.py:609
  86.6 13.6 %invert.1 = (f32[2,256,256]{2,1,0:T(8,128)}, f32[2,256,256]{2,1,0:T(8,128)}, f32[1024,2048]{1,0:T(8,128)}) custom-call(f32[2,256,256]{2,1,0:T(8,128)S(1)} %copy-done.1, f32[1024,2048]{1,0:T(8,128)} %adj.3, f32[512,256]{1,0:T(8,128)} %get-tuple-element.47.a0), custom_call_target="tpu_custom_call" | custom-call | flops 5637144576 | bytes 1048576 | tf_op jit(solution)/shard_map/invert/pallas_call | solution.py:112
  101.0 10.9 %all-to-all-done.terms = f32[16,136,256]{2,1,0:T(8,128)S(1)} async-done(((f32[16,136,256]{2,1,0:T(8,128)}), f32[16,136,256]{2,1,0:T(8,128)S(1)}, u32[]{:S(2)}, u32[]{:S(2)}) %all-to-all-start) | async-done | bytes 2228256 | tf_op jit(solution)/shard_map/all_to_all | solution.py:609
  111.8 2.8 %middle.1 = (f32[16,64,256]{2,1,0:T(8,128)}, f32[16,8,256]{2,1,0:T(8,128)}) custom-call(f32[16,136,256]{2,1,0:T(8,128)S(1)} %all-to-all-done.terms, f32[256,256]{1,0:T(8,128)} %broadcast_select_fusion.4.r31, f32[256,256]{1,0:T(8,128)} %get-tuple-element.80.inv1), custom_call_target="tpu_custom_call" | custom-call | flops 268435456 | bytes 6291456 | tf_op jit(solution)/shard_map/middle/pallas_call | solution.py:274
  114.7 3.7 %all-to-all-start.1 = ((f32[16,8,256]{2,1,0:T(8,128)}), f32[16,8,256]{2,1,0:T(8,128)S(1)}, u32[]{:S(2)}, u32[]{:S(2)}) async-start(f32[16,8,256]{2,1,0:T(8,128)} %get-tuple-element.53), calls=%async_computation.1 | async-start | bytes 262144 | tf_op jit(solution)/shard_map/all_to_all | solution.py:621
  118.4 8.5 %trail.1 = (f32[1024,2048]{1,0:T(8,128)}, bf16[512,1024]{1,0:T(8,128)(2,1)}, bf16[512,1024]{1,0:T(8,128)(2,1)}) custom-call(f32[1024,2048]{1,0:T(8,128)} %adj.3, f32[512,256]{1,0:T(8,128)} %get-tuple-element.47.a0, f32[512,256]{1,0:T(8,128)} %get-tuple-element.55.l1, f32[256,256]{1,0:T(8,128)} %get-tuple-element.80.inv1, ...), custom_call_target="tpu_custom_call", output_to_operand_aliasing={{0}: (10, {})} | custom-call | flops 4294967296 | bytes 10485760 | tf_op jit(solution)/shard_map/trail/pallas_call | solution.py:345
  126.9 7.3 %all-to-all-start.2 = ((f32[16,64,256]{2,1,0:T(8,128)}), f32[16,64,256]{2,1,0:T(8,128)}, u32[]{:S(2)}, u32[]{:S(2)}) async-start(f32[16,64,256]{2,1,0:T(8,128)} %get-tuple-element.62), calls=%async_computation.2 | async-start | bytes 2097152 | tf_op jit(solution)/shard_map/all_to_all | solution.py:626
  134.5 2.3 %collective-permute-start.23 = (f32[16,8,256]{2,1,0:T(8,128)S(1)}, f32[16,8,256]{2,1,0:T(8,128)S(1)}, u32[]{:S(2)}, u32[]{:S(2)}) collective-permute-start(f32[16,8,256]{2,1,0:T(8,128)S(1)} %all-to-all-done.1.mine), channel_id=1, source_target_pairs={{0,6},{1,7},{2,0},{3,1},{4,2},{5,3},{6,4},{7,5},{8,14},{9,15},{10,... | collective-permute-start | bytes 393224 | tf_op jit(solution)/shard_map/ppermute | solution.py:629
  136.8 4.3 %collective-permute-done.24.across = f32[16,8,256]{2,1,0:T(8,128)S(1)} collective-permute-done((f32[16,8,256]{2,1,0:T(8,128)S(1)}, f32[16,8,256]{2,1,0:T(8,128)S(1)}, u32[]{:S(2)}, u32[]{:S(2)}) %collective-permute-start.24) | collective-permute-done | bytes 131104 | tf_op jit(solution)/shard_map/ppermute | solution.py:629
  144.5 4.0 %chain.1 = (f32[256,512]{1,0:T(8,128)}, f32[256,256]{1,0:T(8,128)}, f32[256,256]{1,0:T(8,128)}) custom-call(f32[16,8,256]{2,1,0:T(8,128)S(1)} %all-to-all-done.1.mine, f32[16,8,256]{2,1,0:T(8,128)S(1)} %collective-permute-done.22.before, f32[16,8,256]{2,1,0:T(8,128)S(1)} %collective-permute-done.23.after, f32[16,8,256]{2,1,0:T(8,128)S(1)} %collective-permute-done.24.across, ...), custom_call_target="tpu_custom_call" | custom-call | flops 1048576 | bytes 1024 | tf_op jit(solution)/shard_map/chain/pallas_call | solution.py:432
  148.5 2.0 %all-to-all-done.2.got = f32[16,64,256]{2,1,0:T(8,128)} async-done(((f32[16,64,256]{2,1,0:T(8,128)}), f32[16,64,256]{2,1,0:T(8,128)}, u32[]{:S(2)}, u32[]{:S(2)}) %all-to-all-start.2) | async-done | bytes 1048608 | tf_op jit(solution)/shard_map/all_to_all | solution.py:626
  150.5 4.4 %final.1 = f32[1024,2048]{1,0:T(8,128)} custom-call(f32[1024,2048]{1,0:T(8,128)} %get-tuple-element.61.base, f32[16,64,256]{2,1,0:T(8,128)} %all-to-all-done.2.got, f32[256,512]{1,0:T(8,128)} %get-tuple-element.66.lhs, f32[256,256]{1,0:T(8,128)} %get-tuple-element.67.corner, f32[256,256]{1,0:T(8,128)} %get-tuple-element.68.diag, ...), custom_call_target="tpu_custom_call", output_to_operand_aliasing={{}: (0, {})} | custom-call | flops 2147483648 | bytes 8388608 | tf_op jit(solution)/shard_map/final/pallas_call | solution.py:503
  (79 shorter events, 38.4 us)
Async XLA Ops:
  2.0 14.1 %collective-permute-start.2 = (f32[64,1024]{1,0:T(8,128)}, f32[64,1024]{1,0:T(8,128)}, u32[]{:S(2)}, u32[]{:S(2)}) collective-permute-start(f32[64,1024]{1,0:T(8,128)} %get-tuple-element.71), channel_id=1, source_target_pairs={{0,32},{120,88},{1,33},{121,89},{2,34},{122,90},{3,35},{123,91},{4... | collective-permute-start | bytes 786440 | tf_op jit(solution)/shard_map/ppermute | solution.py:550
  6.6 10.7 %collective-permute-start = (f32[64,1024]{1,0:T(8,128)S(1)}, f32[64,1024]{1,0:T(8,128)}, u32[]{:S(2)}, u32[]{:S(2)}) collective-permute-start(f32[64,1024]{1,0:T(8,128)S(1)} %get-tuple-element.72), channel_id=1, source_target_pairs={{0,64},{120,56},{1,65},{121,57},{2,66},{122,58},{3,67},{123,59},{4... | collective-permute-start | bytes 786440 | tf_op jit(solution)/shard_map/ppermute | solution.py:554
  10.0 7.3 %collective-permute-start.1 = (f32[64,1024]{1,0:T(8,128)S(1)}, f32[64,1024]{1,0:T(8,128)}, u32[]{:S(2)}, u32[]{:S(2)}) collective-permute-start(f32[64,1024]{1,0:T(8,128)S(1)} %get-tuple-element.73), channel_id=1, source_target_pairs={{0,96},{120,24},{1,97},{121,25},{2,98},{122,26},{3,99},{123,27},{4... | collective-permute-start | bytes 786440 | tf_op jit(solution)/shard_map/ppermute | solution.py:553
  18.4 8.9 %collective-permute-start.3 = (f32[640,256]{1,0:T(8,128)S(1)}, f32[640,256]{1,0:T(8,128)S(1)}, u32[]{:S(2)}, u32[]{:S(2)}) collective-permute-start(f32[640,256]{1,0:T(8,128)S(1)} %get-tuple-element.38), channel_id=1, source_target_pairs={{0,2},{7,5},{8,10},{15,13},{16,18},{23,21},{24,26},{31,29},{32,34}... | collective-permute-start | bytes 1966088 | tf_op jit(solution)/shard_map/ppermute | solution.py:523
  19.1 16.3 %collective-permute-start.7 = (f32[640,256]{1,0:T(8,128)S(1)}, f32[640,256]{1,0:T(8,128)S(1)}, u32[]{:S(2)}, u32[]{:S(2)}) collective-permute-start(f32[640,256]{1,0:T(8,128)S(1)} %get-tuple-element.39), channel_id=1, source_target_pairs={{0,6},{7,1},{8,14},{15,9},{16,22},{23,17},{24,30},{31,25},{32,38},... | collective-permute-start | bytes 1966088 | tf_op jit(solution)/shard_map/ppermute | solution.py:524
  19.8 12.0 %collective-permute-start.11 = (f32[64,1024]{1,0:T(8,128)S(1)}, f32[64,1024]{1,0:T(8,128)S(1)}, u32[]{:S(2)}, u32[]{:S(2)}) collective-permute-start(f32[64,1024]{1,0:T(8,128)S(1)} %select_select_fusion.3), channel_id=1, source_target_pairs={{0,24},{24,0},{32,56},{56,32},{64,88},{88,64},{96,120},{120,96},{1... | collective-permute-start | bytes 786440 | tf_op jit(solution)/shard_map/ppermute | solution.py:568
  25.8 18.2 %collective-permute-start.4 = (f32[640,256]{1,0:T(8,128)S(1)}, f32[640,256]{1,0:T(8,128)}, u32[]{:S(2)}, u32[]{:S(2)}) collective-permute-start(f32[640,256]{1,0:T(8,128)S(1)} %get-tuple-element.38), channel_id=1, source_target_pairs={{0,6},{7,1},{8,14},{15,9},{16,22},{23,17},{24,30},{31,25},{32,38},... | collective-permute-start | bytes 1966088 | tf_op jit(solution)/shard_map/ppermute | solution.py:526
  27.3 18.6 %collective-permute-start.5 = (f32[640,256]{1,0:T(8,128)S(1)}, f32[640,256]{1,0:T(8,128)}, u32[]{:S(2)}, u32[]{:S(2)}) collective-permute-start(f32[640,256]{1,0:T(8,128)S(1)} %collective-permute-done.3), channel_id=1, source_target_pairs={{2,4},{5,3},{10,12},{13,11},{18,20},{21,19},{26,28},{29,27},{34,36... | collective-permute-start | bytes 1966088 | tf_op jit(solution)/shard_map/ppermute | solution.py:527
  28.6 6.1 %collective-permute-start.10 = (f32[64,1024]{1,0:T(8,128)S(1)}, f32[64,1024]{1,0:T(8,128)}, u32[]{:S(2)}, u32[]{:S(2)}) collective-permute-start(f32[64,1024]{1,0:T(8,128)S(1)} %select_select_fusion.3), channel_id=1, source_target_pairs={{0,16},{24,8},{32,48},{56,40},{64,80},{88,72},{96,112},{120,104},{... | collective-permute-start | bytes 786440 | tf_op jit(solution)/shard_map/ppermute | solution.py:569
  32.5 8.0 %collective-permute-start.9 = (f32[64,1024]{1,0:T(8,128)S(1)}, f32[64,1024]{1,0:T(8,128)}, u32[]{:S(2)}, u32[]{:S(2)}) collective-permute-start(f32[64,1024]{1,0:T(8,128)S(1)} %select_select_fusion.3), channel_id=1, source_target_pairs={{0,8},{24,16},{32,40},{56,48},{64,72},{88,80},{96,104},{120,112},{... | collective-permute-start | bytes 786440 | tf_op jit(solution)/shard_map/ppermute | solution.py:567
  34.8 12.4 %collective-permute-start.6 = (f32[640,256]{1,0:T(8,128)S(1)}, f32[640,256]{1,0:T(8,128)S(1)}, u32[]{:S(2)}, u32[]{:S(2)}) collective-permute-start(f32[640,256]{1,0:T(8,128)S(1)} %get-tuple-element.39), channel_id=1, source_target_pairs={{0,2},{7,5},{8,10},{15,13},{16,18},{23,21},{24,26},{31,29},{32,34}... | collective-permute-start | bytes 1966088 | tf_op jit(solution)/shard_map/ppermute | solution.py:525
  35.5 18.7 %collective-permute-start.8 = (f32[640,256]{1,0:T(8,128)S(1)}, f32[640,256]{1,0:T(8,128)S(1)}, u32[]{:S(2)}, u32[]{:S(2)}) collective-permute-start(f32[640,256]{1,0:T(8,128)S(1)} %collective-permute-done.7), channel_id=1, source_target_pairs={{6,4},{1,3},{14,12},{9,11},{22,20},{17,19},{30,28},{25,27},{38,36}... | collective-permute-start | bytes 1966088 | tf_op jit(solution)/shard_map/ppermute | solution.py:528
  41.8 15.9 %collective-permute-start.13 = (f32[2,64,1024]{2,1,0:T(8,128)S(1)}, f32[2,64,1024]{2,1,0:T(8,128)S(1)}, u32[]{:S(2)}, u32[]{:S(2)}) collective-permute-start(f32[2,64,1024]{2,1,0:T(8,128)S(1)} %pad_maximum_fusion.2.own), channel_id=1, source_target_pairs={{0,96},{8,104},{16,112},{24,120},{32,0},{40,8},{48,16},{56,24},{64... | collective-permute-start | bytes 1572872 | tf_op jit(solution)/shard_map/ppermute | solution.py:599
  44.0 15.3 %collective-permute-start.12 = (f32[2,64,1024]{2,1,0:T(8,128)S(1)}, f32[2,64,1024]{2,1,0:T(8,128)S(1)}, u32[]{:S(2)}, u32[]{:S(2)}) collective-permute-start(f32[2,64,1024]{2,1,0:T(8,128)S(1)} %pad_maximum_fusion.2.own), channel_id=1, source_target_pairs={{0,32},{8,40},{16,48},{24,56},{32,64},{40,72},{48,80},{56,88},{64,... | collective-permute-start | bytes 1572872 | tf_op jit(solution)/shard_map/ppermute | solution.py:598
  60.7 9.7 %collective-permute-start.17 = (f32[64,1024]{1,0:T(8,128)S(1)}, f32[64,1024]{1,0:T(8,128)S(1)}, u32[]{:S(2)}, u32[]{:S(2)}) collective-permute-start(f32[64,1024]{1,0:T(8,128)S(1)} %slice_bitcast_fusion.1), channel_id=1, source_target_pairs={{0,96},{8,104},{16,112},{24,120},{32,0},{40,8},{48,16},{56,24},{64... | collective-permute-start | bytes 786440 | tf_op jit(solution)/shard_map/ppermute | solution.py:607
  62.3 9.4 %collective-permute-start.16 = (f32[64,1024]{1,0:T(8,128)S(1)}, f32[64,1024]{1,0:T(8,128)}, u32[]{:S(2)}, u32[]{:S(2)}) collective-permute-start(f32[64,1024]{1,0:T(8,128)S(1)} %slice_bitcast_fusion.2), channel_id=1, source_target_pairs={{0,32},{8,40},{16,48},{24,56},{32,64},{40,72},{48,80},{56,88},{64,... | collective-permute-start | bytes 786440 | tf_op jit(solution)/shard_map/ppermute | solution.py:606
  71.7 40.2 %all-to-all-start = ((f32[16,136,256]{2,1,0:T(8,128)}), f32[16,136,256]{2,1,0:T(8,128)S(1)}, u32[]{:S(2)}, u32[]{:S(2)}) async-start(f32[16,136,256]{2,1,0:T(8,128)} %get-tuple-element.46), calls=%async_computation | async-start | bytes 4456448 | tf_op jit(solution)/shard_map/all_to_all | solution.py:609
  80.1 4.1 %collective-permute-start.20 = (f32[256,256]{1,0:T(8,128)}, f32[256,256]{1,0:T(8,128)}, u32[]{:S(2)}, u32[]{:S(2)}) collective-permute-start(f32[256,256]{1,0:T(8,128)} %corner.1), channel_id=1, source_target_pairs={{7,3},{15,11},{23,19},{31,27},{39,35},{47,43},{55,51},{63,59},{71,... | collective-permute-start | bytes 786440 | tf_op jit(solution)/shard_map/ppermute | solution.py:616
  85.3 14.9 %collective-permute-start.21 = (f32[256,256]{1,0:T(8,128)S(1)}, f32[256,256]{1,0:T(8,128)S(1)}, u32[]{:S(2)}, u32[]{:S(2)}) collective-permute-start(f32[256,256]{1,0:T(8,128)S(1)} %select_select_fusion.2), channel_id=1, source_target_pairs={{1,0},{3,2},{5,4},{7,6},{9,8},{11,10},{13,12},{15,14},{17,16},{19,... | collective-permute-start | bytes 786440 | tf_op jit(solution)/shard_map/ppermute | solution.py:618
  114.7 12.3 %all-to-all-start.1 = ((f32[16,8,256]{2,1,0:T(8,128)}), f32[16,8,256]{2,1,0:T(8,128)S(1)}, u32[]{:S(2)}, u32[]{:S(2)}) async-start(f32[16,8,256]{2,1,0:T(8,128)} %get-tuple-element.53), calls=%async_computation.1 | async-start | bytes 262144 | tf_op jit(solution)/shard_map/all_to_all | solution.py:621
  126.9 23.5 %all-to-all-start.2 = ((f32[16,64,256]{2,1,0:T(8,128)}), f32[16,64,256]{2,1,0:T(8,128)}, u32[]{:S(2)}, u32[]{:S(2)}) async-start(f32[16,64,256]{2,1,0:T(8,128)} %get-tuple-element.62), calls=%async_computation.2 | async-start | bytes 2097152 | tf_op jit(solution)/shard_map/all_to_all | solution.py:626
  134.2 6.9 %collective-permute-start.24 = (f32[16,8,256]{2,1,0:T(8,128)S(1)}, f32[16,8,256]{2,1,0:T(8,128)S(1)}, u32[]{:S(2)}, u32[]{:S(2)}) collective-permute-start(f32[16,8,256]{2,1,0:T(8,128)S(1)} %all-to-all-done.1.mine), channel_id=1, source_target_pairs={{0,4},{1,5},{2,6},{3,7},{4,0},{5,1},{6,2},{7,3},{8,12},{9,13},{10,... | collective-permute-start | bytes 393224 | tf_op jit(solution)/shard_map/ppermute | solution.py:629
  134.5 6.6 %collective-permute-start.23 = (f32[16,8,256]{2,1,0:T(8,128)S(1)}, f32[16,8,256]{2,1,0:T(8,128)S(1)}, u32[]{:S(2)}, u32[]{:S(2)}) collective-permute-start(f32[16,8,256]{2,1,0:T(8,128)S(1)} %all-to-all-done.1.mine), channel_id=1, source_target_pairs={{0,6},{1,7},{2,0},{3,1},{4,2},{5,3},{6,4},{7,5},{8,14},{9,15},{10,... | collective-permute-start | bytes 393224 | tf_op jit(solution)/shard_map/ppermute | solution.py:629
  136.8 5.7 %collective-permute-start.22 = (f32[16,8,256]{2,1,0:T(8,128)S(1)}, f32[16,8,256]{2,1,0:T(8,128)S(1)}, u32[]{:S(2)}, u32[]{:S(2)}) collective-permute-start(f32[16,8,256]{2,1,0:T(8,128)S(1)} %all-to-all-done.1.mine), channel_id=1, source_target_pairs={{0,2},{1,3},{2,4},{3,5},{4,6},{5,7},{6,0},{7,1},{8,10},{9,11},{10,... | collective-permute-start | bytes 393224 | tf_op jit(solution)/shard_map/ppermute | solution.py:629
  (14 other events, 187.4 us)

commit v3 on v2

--- a/solution.py
+++ b/solution.py
@@ -122,38 +122,43 @@
     )(tiles, in_hbm(adjoint), in_hbm(a0))
 
 
-def corner_kernel(own, down, up, across_first, out, held, sems):
-    w = out.shape[0]
+def rows_kernel(own, down, up, across_first, across_second, corner, r_high, r_low, held, sems):
+    w = corner.shape[0]
+    left = own.shape[-1]
     quarter = w // RING
     z = lax.axis_index(ROW) // RING
-    left = own.shape[-1]
-    tile = (slice(None), slice(left - w, left))
-    sources = (own.at[(0,) + tile], down.at[(0,) + tile], across_first.at[tile], up.at[(0,) + tile])
+    sources = [own.at[0], down.at[0], across_first, up.at[0], own.at[1], down.at[1], across_second, up.at[1]]
     fetches = [pltpu.make_async_copy(src, held.at[k], sems.at[k]) for k, src in enumerate(sources)]
     for fetch in fetches:
         fetch.start()
-    for fetch in fetches:
+    for k, fetch in enumerate(fetches):
         fetch.wait()
-    for k in range(RING):
-        start = pl.multiple_of(lax.rem(z + k, RING) * quarter, quarter)
-        out[pl.ds(start, quarter), :] = held[k]
-
-
-def gather_corner(own, down, up, across_first):
-    w = own.shape[1] * RING
+        place = pl.multiple_of(lax.rem(z + k, RING) * quarter, quarter)
+        high, low = split(held[k])
+        target = pl.ds(k // RING * w + place, quarter)
+        r_high[target, :] = high
+        r_low[target, :] = low
+        if k < RING:
+            corner[pl.ds(place, quarter), :] = held[k, :, left - w :]
+
+
+def gather_rows(*pieces):
+    shape = pieces[0].shape
+    w, left = shape[1] * RING, shape[2]
+    panel = pltpu.HBM((2 * w, left), jnp.bfloat16)
     return pl.pallas_call(
-        corner_kernel,
-        out_shape=tile_shape(w, w),
-        in_specs=[HBM] * 4,
-        out_specs=VMEM,
+        rows_kernel,
+        out_shape=(tile_shape(w, w), panel, panel),
+        in_specs=[HBM] * len(pieces),
+        out_specs=(VMEM,) * 3,
         scratch_shapes=[
-            pltpu.VMEM((RING, w // RING, w), jnp.float32),
-            pltpu.SemaphoreType.DMA((RING,)),
+            pltpu.VMEM((2 * RING, shape[1], left), jnp.float32),
+            pltpu.SemaphoreType.DMA((2 * RING,)),
         ],
-        compiler_params=params(4),
+        compiler_params=params(8),
         cost_estimate=cost(1 << 10, 1 << 19),
-        name="corner",
-    )(*[in_hbm(value) for value in (own, down, up, across_first)])
+        name="rows",
+    )(*[in_hbm(value) for value in pieces])
 
 
 def small_rows(w, rows):
@@ -289,38 +294,16 @@
     )(terms, in_hbm(r31), in_hbm(inv1))
 
 
-def trail_kernel(
-    adj, a0, l1, inv1, r31, own, down, up, across_first, across_second, base, out, r_high, r_low,
-    small, own_v, down_v, up_v, first_v, second_v, sems
-):
-    step = pl.program_id(0)
+def trail_kernel(adj, a0, l1, inv1, r31, r_high, r_low, base, out, small):
     w = inv1.shape[0]
     left = 4 * w
     q = lax.axis_index(COL)
     last_q = lax.axis_size(COL) - 1
-    z = lax.axis_index(ROW) // RING
-
-    @pl.when(step == 0)
+
+    @pl.when(pl.program_id(0) == 0)
     def _():
-        sources = (own, down, up, across_first, across_second)
-        targets = (own_v, down_v, up_v, first_v, second_v)
-        fetches = [
-            pltpu.make_async_copy(src, dst, sems.at[i]) for i, (src, dst) in enumerate(zip(sources, targets))
-        ]
-        for fetch in fetches:
-            fetch.start()
         small[0], small[1] = split(inv1[...])
         small[2], small[3] = split(product(r31[...], inv1[...]))
-        for fetch in fetches:
-            fetch.wait()
-        quarter = w // RING
-        for j in range(2):
-            values = (own_v[j], down_v[j], (first_v, second_v)[j][...], up_v[j])
-            for k, value in enumerate(values):
-                start = pl.multiple_of(j * w + lax.rem(z + k, RING) * quarter, quarter)
-                high, low = split(value)
-                r_high[pl.ds(start, quarter), :] = high
-                r_low[pl.ds(start, quarter), :] = low
 
     first = a0[...]
     second = product_split(l1[...], small[0], small[1]) - product_split(first, small[2], small[3])
@@ -332,49 +315,35 @@
         out[:, left - w :] = second
 
 
-def trail(adjoint, base, a0, l1, inv1, r31, *pieces):
+def trail(adjoint, base, a0, l1, inv1, r31, r_high, r_low):
     rows, cols = adjoint.shape
     w = inv1.shape[0]
-    steps = 4
+    steps = 2
     blk = rows // 2 // steps
     low = lambda i: (i, 0)
     block = lambda i: (steps + i, 0)
-    const = lambda i: (0, 0)
-    one = pl.Buffered(1)
-    panel = pltpu.HBM((2 * w, 4 * w), jnp.bfloat16)
+    whole = lambda value: pl.BlockSpec(value.shape, lambda i: (0, 0), pipeline_mode=pl.Buffered(1))
     return pl.pallas_call(
         trail_kernel,
         grid=(steps,),
-        out_shape=(pltpu.HBM(adjoint.shape, jnp.float32), panel, panel),
+        out_shape=pltpu.HBM(adjoint.shape, jnp.float32),
         in_specs=[
             pl.BlockSpec((blk, 4 * w), block),
             pl.BlockSpec((blk, w), low),
             pl.BlockSpec((blk, w), low),
-            pl.BlockSpec(inv1.shape, const, pipeline_mode=one),
-            pl.BlockSpec(r31.shape, const, pipeline_mode=one),
-        ]
-        + [HBM] * (len(pieces) + 1),
-        out_specs=(
-            pl.BlockSpec((blk, 4 * w), block),
-            pl.BlockSpec(panel.shape, const),
-            pl.BlockSpec(panel.shape, const),
-        ),
-        scratch_shapes=[pltpu.VMEM((4, w, w), jnp.bfloat16)]
-        + [pltpu.VMEM(piece.shape, jnp.float32) for piece in pieces]
-        + [pltpu.SemaphoreType.DMA((len(pieces),))],
-        input_output_aliases={5 + len(pieces): 0},
+            whole(inv1),
+            whole(r31),
+            whole(r_high),
+            whole(r_low),
+            HBM,
+        ],
+        out_specs=pl.BlockSpec((blk, 4 * w), block),
+        scratch_shapes=[pltpu.VMEM((4, w, w), jnp.bfloat16)],
+        input_output_aliases={7: 0},
         compiler_params=params(16),
         cost_estimate=cost(4 << 30, 10 << 20),
         name="trail",
-    )(
-        in_hbm(adjoint),
-        in_hbm(a0),
-        in_hbm(l1),
-        in_hbm(inv1),
-        in_hbm(r31),
-        *[in_hbm(piece) for piece in pieces],
-        in_hbm(base),
-    )
+    )(*[in_hbm(value) for value in (adjoint, a0, l1, inv1, r31, r_high, r_low, base)])
 
 
 def chain_kernel(
@@ -597,7 +566,6 @@
     own = row_spread(quarter)
     up = lax.ppermute(own, ROW, ring_pairs(1))
     down = lax.ppermute(own, ROW, ring_pairs(-1))
-    top, bottom, up, down = lax.optimization_barrier((top, bottom, up, down))
     even_top, odd_top = column_swap(top)
     even_bottom, odd_bottom = column_swap(bottom)
     terms, a0, l1_below = sums(
@@ -609,7 +577,7 @@
     terms = lax.all_to_all(terms, ROW, 0, 0)
     diag_t, inverse_t, base = invert(inverse, adjoint, a0)
 
-    r31 = gather_corner(own, down, up, across_first)
+    r31, r_high, r_low = gather_rows(own, down, up, across_first, across_second)
     last = lax.axis_size(COL) - 1
     near = lax.ppermute(r31, COL, [(last, last - 2)])
     far = lax.ppermute(r31, COL, [(last, 1)])
@@ -619,10 +587,8 @@
     terms, diag_t, inverse_t, base = lax.optimization_barrier((terms, diag_t, inverse_t, base))
     shares, small = middle(terms, r31, inverse[1])
     small = lax.all_to_all(small, ROW, 0, 0)
-    base, r_high, r_low = trail(
-        adjoint, base, a0, l1_below, inverse[1], r31, own, down, up, across_first, across_second
-    )
-    small, shares, base, r_high, r_low = lax.optimization_barrier((small, shares, base, r_high, r_low))
+    base = trail(adjoint, base, a0, l1_below, inverse[1], r31, r_high, r_low)
+    small, shares, base = lax.optimization_barrier((small, shares, base))
     shares = lax.all_to_all(shares, ROW, 0, 0)
     count = lax.axis_size(COL)
     before, after, across = (

time: 157 us -> 154 us (0.981)
  starting transfers between devices: 58.7 us -> 56.6 us
    ppermute x1, waiting for transfers between devices: 3.44 us -> 1.51 us  [per_device(): down = lax.ppermute(own, ROW, ring_pairs(-1))]
    all_to_all x1, starting transfers between devices: 7.28 us -> 5.52 us  [per_device(): shares = lax.all_to_all(shares, ROW, 0, 0)]
    all_to_all x1, waiting for transfers between devices: 0.01 us -> 1.74 us  [per_device(): small = lax.all_to_all(small, ROW, 0, 0)]
  transfers between devices with their start and end apart: 29 -> 29, of which waited for: 13 -> 13; matrix products, arithmetic and copies ran while one was open for 6% -> 6% of each run, Pallas kernels for 23% -> 22%
where the time goes in v3:
time: 154 us; the launch traced here: 152 us
  starting transfers between devices  56.6 us (37%)
  Pallas kernels  41.5 us (27%)
  waiting for transfers between devices  39.3 us (26%)
  other arithmetic  7.83 us (5%)
  local copies, waits for them, and re-layouts  6.24 us (4%)
    pallas_call x1, Pallas kernels, invert(): pl.pallas_call(invert_kernel, out_shape=(pltpu.HBM((2, w, w), jnp.float32...  13.6 us
    all_to_all x1, waiting for transfers between devices, per_device(): terms = lax.all_to_all(terms, ROW, 0, 0)  10.8 us
    ppermute x1, waiting for transfers between devices, column_hops(): lower = lax.ppermute(far_bottom, COL, [(last - 1, 4), (1, last - 4)])  7.42 us
    pallas_call x1, Pallas kernels, sums(): pl.pallas_call(sums_kernel, grid=(4,), out_shape=(pltpu.HBM((rows, height...  7.3 us
    all_to_all x1, starting transfers between devices, per_device(): terms = lax.all_to_all(terms, ROW, 0, 0)  6.48 us
    pallas_call x1, Pallas kernels, trail(): pl.pallas_call(trail_kernel, grid=(steps,), out_shape=pltpu.HBM(adjoint.s...  6.21 us
    ppermute x1, starting transfers between devices, row_spread(): lax.ppermute(mine, ROW, [e for s in lines for e in ((s, s + top), (s + to...  5.99 us
    ppermute x3, waiting for transfers between devices, per_device(): lax.ppermute(small, COL, [(i, (i + step) % count) for i in range(count)])  5.99 us
  transfers between devices with their start and end apart: 29, of which 13 were waited for; matrix products, arithmetic and copies ran while one was open for 6% of the time, Pallas kernels for 22%

profile of v3, /device:TPU:16, one launch (start us, length us, event | category | flops | bytes accessed | tf_op | source)
XLA Modules:
  0.0 152.0 jit_solution(3055571575854832050)
XLA Ops:
  0.0 2.0 %dynamic-slice_select_fusion.1 = (f32[64,1024]{1,0:T(8,128)}, f32[64,1024]{1,0:T(8,128)S(1)}, f32[64,1024]{1,0:T(8,128)S(1)}) fusion(f32[1024,2048]{1,0:T(8,128)} %factor.1, s32[]{:T(128)S(6)} %add.16, s32[]{:T(128)S(6)} %add.15, pred[]{:T(512)S(6)} %eq.83, s32[]{:T(128)S(6)} %select_n.177, s32[]{:T(128)S(6)} %add.17), kind=kLoop, calls=%fused_computation.19 | loop fusion | flops 196608 | bytes 1835025 | tf_op jit(solution)/shard_map/jit(_where)/select_n | solution.py:520
  2.0 4.5 %collective-permute-start.2 = (f32[64,1024]{1,0:T(8,128)}, f32[64,1024]{1,0:T(8,128)}, u32[]{:S(2)}, u32[]{:S(2)}) collective-permute-start(f32[64,1024]{1,0:T(8,128)} %get-tuple-element.59), channel_id=1, source_target_pairs={{0,32},{120,88},{1,33},{121,89},{2,34},{122,90},{3,35},{123,91},{4... | collective-permute-start | bytes 786440 | tf_op jit(solution)/shard_map/ppermute | solution.py:519
  6.6 3.3 %collective-permute-start = (f32[64,1024]{1,0:T(8,128)S(1)}, f32[64,1024]{1,0:T(8,128)}, u32[]{:S(2)}, u32[]{:S(2)}) collective-permute-start(f32[64,1024]{1,0:T(8,128)S(1)} %get-tuple-element.60), channel_id=1, source_target_pairs={{0,64},{120,56},{1,65},{121,57},{2,66},{122,58},{3,67},{123,59},{4... | collective-permute-start | bytes 786440 | tf_op jit(solution)/shard_map/ppermute | solution.py:523
  9.9 2.0 %collective-permute-start.1 = (f32[64,1024]{1,0:T(8,128)S(1)}, f32[64,1024]{1,0:T(8,128)}, u32[]{:S(2)}, u32[]{:S(2)}) collective-permute-start(f32[64,1024]{1,0:T(8,128)S(1)} %get-tuple-element.61), channel_id=1, source_target_pairs={{0,96},{120,24},{1,97},{121,25},{2,98},{122,26},{3,99},{123,27},{4... | collective-permute-start | bytes 786440 | tf_op jit(solution)/shard_map/ppermute | solution.py:522
  19.8 6.0 %collective-permute-start.13 = (f32[64,1024]{1,0:T(8,128)S(1)}, f32[64,1024]{1,0:T(8,128)S(1)}, u32[]{:S(2)}, u32[]{:S(2)}) collective-permute-start(f32[64,1024]{1,0:T(8,128)S(1)} %select_select_fusion.3), channel_id=1, source_target_pairs={{0,24},{24,0},{32,56},{56,32},{64,88},{88,64},{96,120},{120,96},{1... | collective-permute-start | bytes 786440 | tf_op jit(solution)/shard_map/ppermute | solution.py:537
  28.6 2.0 %collective-permute-start.12 = (f32[64,1024]{1,0:T(8,128)S(1)}, f32[64,1024]{1,0:T(8,128)}, u32[]{:S(2)}, u32[]{:S(2)}) collective-permute-start(f32[64,1024]{1,0:T(8,128)S(1)} %select_select_fusion.3), channel_id=1, source_target_pairs={{0,16},{24,8},{32,48},{56,40},{64,80},{88,72},{96,112},{120,104},{... | collective-permute-start | bytes 786440 | tf_op jit(solution)/shard_map/ppermute | solution.py:538
  32.5 2.0 %collective-permute-start.11 = (f32[64,1024]{1,0:T(8,128)S(1)}, f32[64,1024]{1,0:T(8,128)}, u32[]{:S(2)}, u32[]{:S(2)}) collective-permute-start(f32[64,1024]{1,0:T(8,128)S(1)} %select_select_fusion.3), channel_id=1, source_target_pairs={{0,8},{24,16},{32,40},{56,48},{64,72},{88,80},{96,104},{120,112},{... | collective-permute-start | bytes 786440 | tf_op jit(solution)/shard_map/ppermute | solution.py:536
  37.2 3.3 %collective-permute-done.11 = f32[64,1024]{1,0:T(8,128)} collective-permute-done((f32[64,1024]{1,0:T(8,128)S(1)}, f32[64,1024]{1,0:T(8,128)}, u32[]{:S(2)}, u32[]{:S(2)}) %collective-permute-start.11) | collective-permute-done | bytes 262176 | tf_op jit(solution)/shard_map/ppermute | solution.py:536
  41.7 2.2 %collective-permute-start.16 = (f32[2,64,1024]{2,1,0:T(8,128)S(1)}, f32[2,64,1024]{2,1,0:T(8,128)S(1)}, u32[]{:S(2)}, u32[]{:S(2)}) collective-permute-start(f32[2,64,1024]{2,1,0:T(8,128)S(1)} %pad_maximum_fusion.2.own), channel_id=1, source_target_pairs={{0,96},{8,104},{16,112},{24,120},{32,0},{40,8},{48,16},{56,24},{64... | collective-permute-start | bytes 1572872 | tf_op jit(solution)/shard_map/ppermute | solution.py:568
  47.2 7.4 %collective-permute-done.9 = f32[640,256]{1,0:T(8,128)S(1)} collective-permute-done((f32[640,256]{1,0:T(8,128)S(1)}, f32[640,256]{1,0:T(8,128)S(1)}, u32[]{:S(2)}, u32[]{:S(2)}) %collective-permute-start.9) | collective-permute-done | bytes 655392 | tf_op jit(solution)/shard_map/ppermute | solution.py:497
  60.1 7.3 %sums.1 = (f32[16,136,256]{2,1,0:T(8,128)}, f32[512,256]{1,0:T(8,128)}, f32[512,256]{1,0:T(8,128)}) custom-call(f32[640,256]{1,0:T(8,128)S(1)} %get-tuple-element.65.even_top, f32[640,256]{1,0:T(8,128)S(1)} %get-tuple-element.63.even_bottom, f32[640,256]{1,0:T(8,128)S(1)} %get-tuple-element.64.odd_top, f32[640,256]{1,0:T(8,128)S(1)} %get-tuple-element.62.odd_bottom, ...), custom_call_target="tpu_custom_call" | custom-call | flops 4294967296 | bytes 8388608 | tf_op jit(solution)/shard_map/sums/pallas_call | solution.py:221
  70.0 6.5 %all-to-all-start = ((f32[16,136,256]{2,1,0:T(8,128)}), f32[16,136,256]{2,1,0:T(8,128)S(1)}, u32[]{:S(2)}, u32[]{:S(2)}) async-start(f32[16,136,256]{2,1,0:T(8,128)} %get-tuple-element.36), calls=%async_computation | async-start | bytes 4456448 | tf_op jit(solution)/shard_map/all_to_all | solution.py:577
  76.5 3.0 %rows.1 = (f32[256,256]{1,0:T(8,128)}, bf16[512,1024]{1,0:T(8,128)(2,1)}, bf16[512,1024]{1,0:T(8,128)(2,1)}) custom-call(f32[2,64,1024]{2,1,0:T(8,128)} %copy-done.4, f32[2,64,1024]{2,1,0:T(8,128)} %copy-done.5, f32[2,64,1024]{2,1,0:T(8,128)} %copy-done.6, f32[64,1024]{1,0:T(8,128)} %copy-done.9, f32[64,1024]{1,0:T(8,128)} %copy-done.8), custom_call_target="tpu_custom_call" | custom-call | flops 1024 | bytes 524288 | tf_op jit(solution)/shard_map/rows/pallas_call | solution.py:149
  86.0 13.6 %invert.1 = (f32[2,256,256]{2,1,0:T(8,128)}, f32[2,256,256]{2,1,0:T(8,128)}, f32[1024,2048]{1,0:T(8,128)}) custom-call(f32[2,256,256]{2,1,0:T(8,128)S(1)} %copy-done.1, f32[1024,2048]{1,0:T(8,128)} %adj.3, f32[512,256]{1,0:T(8,128)} %get-tuple-element.37.a0), custom_call_target="tpu_custom_call" | custom-call | flops 5637144576 | bytes 1048576 | tf_op jit(solution)/shard_map/invert/pallas_call | solution.py:112
  100.3 10.8 %all-to-all-done.terms = f32[16,136,256]{2,1,0:T(8,128)S(1)} async-done(((f32[16,136,256]{2,1,0:T(8,128)}), f32[16,136,256]{2,1,0:T(8,128)S(1)}, u32[]{:S(2)}, u32[]{:S(2)}) %all-to-all-start) | async-done | bytes 2228256 | tf_op jit(solution)/shard_map/all_to_all | solution.py:577
  111.2 2.9 %middle.1 = (f32[16,64,256]{2,1,0:T(8,128)}, f32[16,8,256]{2,1,0:T(8,128)}) custom-call(f32[16,136,256]{2,1,0:T(8,128)S(1)} %all-to-all-done.terms, f32[256,256]{1,0:T(8,128)} %broadcast_select_fusion.4.r31, f32[256,256]{1,0:T(8,128)} %get-tuple-element.68.inv1), custom_call_target="tpu_custom_call" | custom-call | flops 268435456 | bytes 6291456 | tf_op jit(solution)/shard_map/middle/pallas_call | solution.py:279
  114.1 3.5 %all-to-all-start.1 = ((f32[16,8,256]{2,1,0:T(8,128)}), f32[16,8,256]{2,1,0:T(8,128)S(1)}, u32[]{:S(2)}, u32[]{:S(2)}) async-start(f32[16,8,256]{2,1,0:T(8,128)} %get-tuple-element.45), calls=%async_computation.1 | async-start | bytes 262144 | tf_op jit(solution)/shard_map/all_to_all | solution.py:589
  117.6 6.2 %trail.1.base = f32[1024,2048]{1,0:T(8,128)} custom-call(f32[1024,2048]{1,0:T(8,128)} %adj.3, f32[512,256]{1,0:T(8,128)} %get-tuple-element.37.a0, f32[512,256]{1,0:T(8,128)} %get-tuple-element.47.l1, f32[256,256]{1,0:T(8,128)} %get-tuple-element.68.inv1, f32[256,256]{1,0:T(8,128)} %broadcast_select_fusion.4.r31, ...), custom_call_target="tpu_custom_call", output_to_operand_aliasing={{}: (7, {})} | custom-call | flops 4294967296 | bytes 10485760 | tf_op jit(solution)/shard_map/trail/pallas_call | solution.py:326
  125.6 5.5 %all-to-all-start.2 = ((f32[16,64,256]{2,1,0:T(8,128)}), f32[16,64,256]{2,1,0:T(8,128)}, u32[]{:S(2)}, u32[]{:S(2)}) async-start(f32[16,64,256]{2,1,0:T(8,128)} %get-tuple-element.52), calls=%async_computation.2 | async-start | bytes 2097152 | tf_op jit(solution)/shard_map/all_to_all | solution.py:592
  131.4 1.9 %collective-permute-start.22 = (f32[16,8,256]{2,1,0:T(8,128)S(1)}, f32[16,8,256]{2,1,0:T(8,128)S(1)}, u32[]{:S(2)}, u32[]{:S(2)}) collective-permute-start(f32[16,8,256]{2,1,0:T(8,128)S(1)} %all-to-all-done.1.mine), channel_id=1, source_target_pairs={{0,2},{1,3},{2,4},{3,5},{4,6},{5,7},{6,0},{7,1},{8,10},{9,11},{10,... | collective-permute-start | bytes 393224 | tf_op jit(solution)/shard_map/ppermute | solution.py:595
  133.3 4.7 %collective-permute-done.24.across = f32[16,8,256]{2,1,0:T(8,128)S(1)} collective-permute-done((f32[16,8,256]{2,1,0:T(8,128)S(1)}, f32[16,8,256]{2,1,0:T(8,128)S(1)}, u32[]{:S(2)}, u32[]{:S(2)}) %collective-permute-start.24) | collective-permute-done | bytes 131104 | tf_op jit(solution)/shard_map/ppermute | solution.py:595
  141.3 4.0 %chain.1 = (f32[256,512]{1,0:T(8,128)}, f32[256,256]{1,0:T(8,128)}, f32[256,256]{1,0:T(8,128)}) custom-call(f32[16,8,256]{2,1,0:T(8,128)S(1)} %all-to-all-done.1.mine, f32[16,8,256]{2,1,0:T(8,128)S(1)} %collective-permute-done.22.before, f32[16,8,256]{2,1,0:T(8,128)S(1)} %collective-permute-done.23.after, f32[16,8,256]{2,1,0:T(8,128)S(1)} %collective-permute-done.24.across, ...), custom_call_target="tpu_custom_call" | custom-call | flops 1048576 | bytes 1024 | tf_op jit(solution)/shard_map/chain/pallas_call | solution.py:401
  145.3 2.1 %all-to-all-done.2.got = f32[16,64,256]{2,1,0:T(8,128)} async-done(((f32[16,64,256]{2,1,0:T(8,128)}), f32[16,64,256]{2,1,0:T(8,128)}, u32[]{:S(2)}, u32[]{:S(2)}) %all-to-all-start.2) | async-done | bytes 1048608 | tf_op jit(solution)/shard_map/all_to_all | solution.py:592
  147.5 4.4 %final.1 = f32[1024,2048]{1,0:T(8,128)} custom-call(f32[1024,2048]{1,0:T(8,128)} %trail.1.base, f32[16,64,256]{2,1,0:T(8,128)} %all-to-all-done.2.got, f32[256,512]{1,0:T(8,128)} %get-tuple-element.56.lhs, f32[256,256]{1,0:T(8,128)} %get-tuple-element.57.corner, f32[256,256]{1,0:T(8,128)} %get-tuple-element.58.diag, ...), custom_call_target="tpu_custom_call", output_to_operand_aliasing={{}: (0, {})} | custom-call | flops 2147483648 | bytes 8388608 | tf_op jit(solution)/shard_map/final/pallas_call | solution.py:472
  (81 shorter events, 40.2 us)
Async XLA Ops:
  2.0 14.0 %collective-permute-start.2 = (f32[64,1024]{1,0:T(8,128)}, f32[64,1024]{1,0:T(8,128)}, u32[]{:S(2)}, u32[]{:S(2)}) collective-permute-start(f32[64,1024]{1,0:T(8,128)} %get-tuple-element.59), channel_id=1, source_target_pairs={{0,32},{120,88},{1,33},{121,89},{2,34},{122,90},{3,35},{123,91},{4... | collective-permute-start | bytes 786440 | tf_op jit(solution)/shard_map/ppermute | solution.py:519
  6.6 10.7 %collective-permute-start = (f32[64,1024]{1,0:T(8,128)S(1)}, f32[64,1024]{1,0:T(8,128)}, u32[]{:S(2)}, u32[]{:S(2)}) collective-permute-start(f32[64,1024]{1,0:T(8,128)S(1)} %get-tuple-element.60), channel_id=1, source_target_pairs={{0,64},{120,56},{1,65},{121,57},{2,66},{122,58},{3,67},{123,59},{4... | collective-permute-start | bytes 786440 | tf_op jit(solution)/shard_map/ppermute | solution.py:523
  9.9 7.3 %collective-permute-start.1 = (f32[64,1024]{1,0:T(8,128)S(1)}, f32[64,1024]{1,0:T(8,128)}, u32[]{:S(2)}, u32[]{:S(2)}) collective-permute-start(f32[64,1024]{1,0:T(8,128)S(1)} %get-tuple-element.61), channel_id=1, source_target_pairs={{0,96},{120,24},{1,97},{121,25},{2,98},{122,26},{3,99},{123,27},{4... | collective-permute-start | bytes 786440 | tf_op jit(solution)/shard_map/ppermute | solution.py:522
  18.3 9.0 %collective-permute-start.3 = (f32[640,256]{1,0:T(8,128)S(1)}, f32[640,256]{1,0:T(8,128)S(1)}, u32[]{:S(2)}, u32[]{:S(2)}) collective-permute-start(f32[640,256]{1,0:T(8,128)S(1)} %get-tuple-element.32), channel_id=1, source_target_pairs={{0,2},{7,5},{8,10},{15,13},{16,18},{23,21},{24,26},{31,29},{32,34}... | collective-permute-start | bytes 1966088 | tf_op jit(solution)/shard_map/ppermute | solution.py:492
  19.0 16.9 %collective-permute-start.8 = (f32[640,256]{1,0:T(8,128)S(1)}, f32[640,256]{1,0:T(8,128)S(1)}, u32[]{:S(2)}, u32[]{:S(2)}) collective-permute-start(f32[640,256]{1,0:T(8,128)S(1)} %get-tuple-element.33), channel_id=1, source_target_pairs={{0,6},{7,1},{8,14},{15,9},{16,22},{23,17},{24,30},{31,25},{32,38},... | collective-permute-start | bytes 1966088 | tf_op jit(solution)/shard_map/ppermute | solution.py:493
  19.8 12.0 %collective-permute-start.13 = (f32[64,1024]{1,0:T(8,128)S(1)}, f32[64,1024]{1,0:T(8,128)S(1)}, u32[]{:S(2)}, u32[]{:S(2)}) collective-permute-start(f32[64,1024]{1,0:T(8,128)S(1)} %select_select_fusion.3), channel_id=1, source_target_pairs={{0,24},{24,0},{32,56},{56,32},{64,88},{88,64},{96,120},{120,96},{1... | collective-permute-start | bytes 786440 | tf_op jit(solution)/shard_map/ppermute | solution.py:537
  25.8 18.2 %collective-permute-start.4 = (f32[640,256]{1,0:T(8,128)S(1)}, f32[640,256]{1,0:T(8,128)}, u32[]{:S(2)}, u32[]{:S(2)}) collective-permute-start(f32[640,256]{1,0:T(8,128)S(1)} %get-tuple-element.32), channel_id=1, source_target_pairs={{0,6},{7,1},{8,14},{15,9},{16,22},{23,17},{24,30},{31,25},{32,38},... | collective-permute-start | bytes 1966088 | tf_op jit(solution)/shard_map/ppermute | solution.py:495
  27.3 18.6 %collective-permute-start.5 = (f32[640,256]{1,0:T(8,128)S(1)}, f32[640,256]{1,0:T(8,128)}, u32[]{:S(2)}, u32[]{:S(2)}) collective-permute-start(f32[640,256]{1,0:T(8,128)S(1)} %collective-permute-done.3), channel_id=1, source_target_pairs={{2,4},{5,3},{10,12},{13,11},{18,20},{21,19},{26,28},{29,27},{34,36... | collective-permute-start | bytes 1966088 | tf_op jit(solution)/shard_map/ppermute | solution.py:496
  28.6 6.6 %collective-permute-start.12 = (f32[64,1024]{1,0:T(8,128)S(1)}, f32[64,1024]{1,0:T(8,128)}, u32[]{:S(2)}, u32[]{:S(2)}) collective-permute-start(f32[64,1024]{1,0:T(8,128)S(1)} %select_select_fusion.3), channel_id=1, source_target_pairs={{0,16},{24,8},{32,48},{56,40},{64,80},{88,72},{96,112},{120,104},{... | collective-permute-start | bytes 786440 | tf_op jit(solution)/shard_map/ppermute | solution.py:538
  32.5 8.0 %collective-permute-start.11 = (f32[64,1024]{1,0:T(8,128)S(1)}, f32[64,1024]{1,0:T(8,128)}, u32[]{:S(2)}, u32[]{:S(2)}) collective-permute-start(f32[64,1024]{1,0:T(8,128)S(1)} %select_select_fusion.3), channel_id=1, source_target_pairs={{0,8},{24,16},{32,40},{56,48},{64,72},{88,80},{96,104},{120,112},{... | collective-permute-start | bytes 786440 | tf_op jit(solution)/shard_map/ppermute | solution.py:536
  35.2 12.0 %collective-permute-start.7 = (f32[640,256]{1,0:T(8,128)S(1)}, f32[640,256]{1,0:T(8,128)S(1)}, u32[]{:S(2)}, u32[]{:S(2)}) collective-permute-start(f32[640,256]{1,0:T(8,128)S(1)} %get-tuple-element.33), channel_id=1, source_target_pairs={{0,2},{7,5},{8,10},{15,13},{16,18},{23,21},{24,26},{31,29},{32,34}... | collective-permute-start | bytes 1966088 | tf_op jit(solution)/shard_map/ppermute | solution.py:494
  35.9 18.7 %collective-permute-start.9 = (f32[640,256]{1,0:T(8,128)S(1)}, f32[640,256]{1,0:T(8,128)S(1)}, u32[]{:S(2)}, u32[]{:S(2)}) collective-permute-start(f32[640,256]{1,0:T(8,128)S(1)} %collective-permute-done.8), channel_id=1, source_target_pairs={{6,4},{1,3},{14,12},{9,11},{22,20},{17,19},{30,28},{25,27},{38,36}... | collective-permute-start | bytes 1966088 | tf_op jit(solution)/shard_map/ppermute | solution.py:497
  41.7 15.9 %collective-permute-start.16 = (f32[2,64,1024]{2,1,0:T(8,128)S(1)}, f32[2,64,1024]{2,1,0:T(8,128)S(1)}, u32[]{:S(2)}, u32[]{:S(2)}) collective-permute-start(f32[2,64,1024]{2,1,0:T(8,128)S(1)} %pad_maximum_fusion.2.own), channel_id=1, source_target_pairs={{0,96},{8,104},{16,112},{24,120},{32,0},{40,8},{48,16},{56,24},{64... | collective-permute-start | bytes 1572872 | tf_op jit(solution)/shard_map/ppermute | solution.py:568
  44.0 15.3 %collective-permute-start.14 = (f32[2,64,1024]{2,1,0:T(8,128)S(1)}, f32[2,64,1024]{2,1,0:T(8,128)S(1)}, u32[]{:S(2)}, u32[]{:S(2)}) collective-permute-start(f32[2,64,1024]{2,1,0:T(8,128)S(1)} %pad_maximum_fusion.2.own), channel_id=1, source_target_pairs={{0,32},{8,40},{16,48},{24,56},{32,64},{40,72},{48,80},{56,88},{64,... | collective-permute-start | bytes 1572872 | tf_op jit(solution)/shard_map/ppermute | solution.py:567
  47.1 12.7 %collective-permute-start.6 = (f32[640,256]{1,0:T(8,128)S(1)}, f32[640,256]{1,0:T(8,128)S(1)}, u32[]{:S(2)}, u32[]{:S(2)}) collective-permute-start(f32[640,256]{1,0:T(8,128)S(1)} %select_select_fusion.1), channel_id=1, source_target_pairs={{0,1},{1,0},{2,3},{3,2},{4,5},{5,4},{6,7},{7,6},{8,9},{9,8},{10,11... | collective-permute-start | bytes 1966088 | tf_op jit(solution)/shard_map/ppermute | solution.py:508
  57.7 9.7 %collective-permute-start.17 = (f32[64,1024]{1,0:T(8,128)S(1)}, f32[64,1024]{1,0:T(8,128)S(1)}, u32[]{:S(2)}, u32[]{:S(2)}) collective-permute-start(f32[64,1024]{1,0:T(8,128)S(1)} %slice_bitcast_fusion), channel_id=1, source_target_pairs={{0,96},{8,104},{16,112},{24,120},{32,0},{40,8},{48,16},{56,24},{64... | collective-permute-start | bytes 786440 | tf_op jit(solution)/shard_map/ppermute | solution.py:575
  59.3 10.0 %collective-permute-start.15 = (f32[64,1024]{1,0:T(8,128)S(1)}, f32[64,1024]{1,0:T(8,128)S(1)}, u32[]{:S(2)}, u32[]{:S(2)}) collective-permute-start(f32[64,1024]{1,0:T(8,128)S(1)} %slice_bitcast_fusion.1), channel_id=1, source_target_pairs={{0,32},{8,40},{16,48},{24,56},{32,64},{40,72},{48,80},{56,88},{64,... | collective-permute-start | bytes 786440 | tf_op jit(solution)/shard_map/ppermute | solution.py:574
  70.0 41.1 %all-to-all-start = ((f32[16,136,256]{2,1,0:T(8,128)}), f32[16,136,256]{2,1,0:T(8,128)S(1)}, u32[]{:S(2)}, u32[]{:S(2)}) async-start(f32[16,136,256]{2,1,0:T(8,128)} %get-tuple-element.36), calls=%async_computation | async-start | bytes 4456448 | tf_op jit(solution)/shard_map/all_to_all | solution.py:577
  84.7 14.9 %collective-permute-start.21 = (f32[256,256]{1,0:T(8,128)S(1)}, f32[256,256]{1,0:T(8,128)S(1)}, u32[]{:S(2)}, u32[]{:S(2)}) collective-permute-start(f32[256,256]{1,0:T(8,128)S(1)} %select_select_fusion.2), channel_id=1, source_target_pairs={{1,0},{3,2},{5,4},{7,6},{9,8},{11,10},{13,12},{15,14},{17,16},{19,... | collective-permute-start | bytes 786440 | tf_op jit(solution)/shard_map/ppermute | solution.py:586
  114.1 11.5 %all-to-all-start.1 = ((f32[16,8,256]{2,1,0:T(8,128)}), f32[16,8,256]{2,1,0:T(8,128)S(1)}, u32[]{:S(2)}, u32[]{:S(2)}) async-start(f32[16,8,256]{2,1,0:T(8,128)} %get-tuple-element.45), calls=%async_computation.1 | async-start | bytes 262144 | tf_op jit(solution)/shard_map/all_to_all | solution.py:589
  125.6 21.9 %all-to-all-start.2 = ((f32[16,64,256]{2,1,0:T(8,128)}), f32[16,64,256]{2,1,0:T(8,128)}, u32[]{:S(2)}, u32[]{:S(2)}) async-start(f32[16,64,256]{2,1,0:T(8,128)} %get-tuple-element.52), calls=%async_computation.2 | async-start | bytes 2097152 | tf_op jit(solution)/shard_map/all_to_all | solution.py:592
  131.1 6.9 %collective-permute-start.24 = (f32[16,8,256]{2,1,0:T(8,128)S(1)}, f32[16,8,256]{2,1,0:T(8,128)S(1)}, u32[]{:S(2)}, u32[]{:S(2)}) collective-permute-start(f32[16,8,256]{2,1,0:T(8,128)S(1)} %all-to-all-done.1.mine), channel_id=1, source_target_pairs={{0,4},{1,5},{2,6},{3,7},{4,0},{5,1},{6,2},{7,3},{8,12},{9,13},{10,... | collective-permute-start | bytes 393224 | tf_op jit(solution)/shard_map/ppermute | solution.py:595
  131.2 6.8 %collective-permute-start.23 = (f32[16,8,256]{2,1,0:T(8,128)S(1)}, f32[16,8,256]{2,1,0:T(8,128)S(1)}, u32[]{:S(2)}, u32[]{:S(2)}) collective-permute-start(f32[16,8,256]{2,1,0:T(8,128)S(1)} %all-to-all-done.1.mine), channel_id=1, source_target_pairs={{0,6},{1,7},{2,0},{3,1},{4,2},{5,3},{6,4},{7,5},{8,14},{9,15},{10,... | collective-permute-start | bytes 393224 | tf_op jit(solution)/shard_map/ppermute | solution.py:595
  131.4 7.9 %collective-permute-start.22 = (f32[16,8,256]{2,1,0:T(8,128)S(1)}, f32[16,8,256]{2,1,0:T(8,128)S(1)}, u32[]{:S(2)}, u32[]{:S(2)}) collective-permute-start(f32[16,8,256]{2,1,0:T(8,128)S(1)} %all-to-all-done.1.mine), channel_id=1, source_target_pairs={{0,2},{1,3},{2,4},{3,5},{4,6},{5,7},{6,0},{7,1},{8,10},{9,11},{10,... | collective-permute-start | bytes 393224 | tf_op jit(solution)/shard_map/ppermute | solution.py:595
  (15 other events, 167.7 us)

commit v4 on v3

--- a/solution.py
+++ b/solution.py
@@ -347,7 +347,8 @@
 
 
 def chain_kernel(
-    mine, before, after, across, theirs, inverse, inverse_t, diag_t, diag31, r31, lhs, corner, diag, tiles
+    mine, before, after, across, theirs, inverse, inverse_t, diag_t, diag31, r31, r_high, r_low, base, out,
+    tiles, lhs, diag, r_high_v, r_low_v, rows_buf, sems
 ):
     w = inverse.shape[-1]
     rows = mine.shape[0]
@@ -358,6 +359,16 @@
 
     @pl.when((p == 0) | (p == rows - 1))
     def _():
+        left = 4 * w
+        start = jnp.where(p == 0, 2 * w, w)
+        region = (pl.ds(start, w), pl.ds(0, left))
+        fetches = [
+            pltpu.make_async_copy(r_high, r_high_v, sems.at[0]),
+            pltpu.make_async_copy(r_low, r_low_v, sems.at[1]),
+            pltpu.make_async_copy(base.at[region], rows_buf, sems.at[2]),
+        ]
+        for fetch in fetches:
+            fetch.start()
         core = lax.rem(q, 2)
         for k, shared in ((0, mine), (1, after), (2, across), (3, before)):
             chip = lax.rem(q // 2 + k, RING)
@@ -379,13 +390,34 @@
         side = product(inverse_t[1], x11 + product(known.T, t01))
         g0 = adjoint_diag(0, tiles[0])
         a132 = product(t01 - product(g0, known), inverse[1])
-        diag[...] = halved_lower(g0)
+        for fetch in fetches:
+            fetch.wait()
+
+        def update(corner):
+            rows_buf[...] = rows_buf[...] - product_split(lhs[...], r_high_v[...], r_low_v[...])
+
+            @pl.when(q == lax.axis_size(COL) - 1)
+            def _():
+                rows_buf[:, left - w :] = corner
+
+            store = pltpu.make_async_copy(rows_buf, out.at[region], sems.at[3])
+            store.start()
+            store.wait()
 
         @pl.when(p == 0)
         def _():
             lhs[:, :w] = g0
             lhs[:, w:] = a132
-            corner[...] = a132
+            update(a132)
+
+            @pl.when(q == 0)
+            def _():
+                diag[...] = halved_lower(g0)
+                store = pltpu.make_async_copy(
+                    diag, out.at[pl.ds(2 * w, w), pl.ds(left, w)], sems.at[4]
+                )
+                store.start()
+                store.wait()
 
         @pl.when(p != 0)
         def _():
@@ -393,25 +425,35 @@
             g1 = adjoint_diag(1, diag31[...] - side - product(a132_t, known))
             lhs[:, :w] = a132_t
             lhs[:, w:] = g1
-            corner[...] = halved_lower(g1)
+            update(halved_lower(g1))
 
 
 def chain(*operands):
     w = operands[5].shape[-1]
+    base = operands[-1]
+    panel = pltpu.VMEM((2 * w, 4 * w), jnp.bfloat16)
     return pl.pallas_call(
         chain_kernel,
-        out_shape=tuple(pltpu.HBM((w, n * w), jnp.float32) for n in (2, 1, 1)),
-        in_specs=[VMEM] * len(operands),
-        out_specs=(VMEM,) * 3,
-        scratch_shapes=[pltpu.VMEM((3, w, w), jnp.float32)],
-        compiler_params=params(14),
+        out_shape=pltpu.HBM(base.shape, jnp.float32),
+        in_specs=[VMEM] * (len(operands) - 3) + [HBM] * 3,
+        out_specs=HBM,
+        scratch_shapes=[
+            pltpu.VMEM((3, w, w), jnp.float32),
+            pltpu.VMEM((w, 2 * w), jnp.float32),
+            pltpu.VMEM((w, w), jnp.float32),
+            panel,
+            panel,
+            pltpu.VMEM((w, 4 * w), jnp.float32),
+            pltpu.SemaphoreType.DMA((5,)),
+        ],
+        input_output_aliases={len(operands) - 1: 0},
+        compiler_params=params(18),
         cost_estimate=cost(1 << 20, 1 << 10),
         name="chain",
-    )(*operands)
-
-
-def final_kernel(base, got, lhs, corner, diag, r_high, r_low, out, *scratch):
-    got_v, lhs_v, corner_v, diag_v, r_high_v, r_low_v, rows_buf, sems = scratch
+    )(*operands[:-3], *[in_hbm(value) for value in operands[-3:]])
+
+
+def final_kernel(base, got, out, got_v, rows_buf, sems):
     rows, cols, w = got.shape
     left = 4 * w
     p = lax.axis_index(ROW)
@@ -422,67 +464,47 @@
     def _():
         start = jnp.where(p == 0, 2 * w, w)
         region = (pl.ds(start, w), pl.ds(0, left))
-        moves = [
-            (lhs, lhs_v),
-            (r_high, r_high_v),
-            (r_low, r_low_v),
-            (base.at[region], rows_buf),
-            (got, got_v),
-            (corner, corner_v),
-            (diag, diag_v),
+        fetches = [
+            pltpu.make_async_copy(base.at[region], rows_buf, sems.at[0]),
+            pltpu.make_async_copy(got, got_v, sems.at[1]),
         ]
-        fetches = [pltpu.make_async_copy(src, dst, sems.at[i]) for i, (src, dst) in enumerate(moves)]
         for fetch in fetches:
             fetch.start()
         for fetch in fetches:
             fetch.wait()
         stores = []
+        piece = rows // 4
         for j in range(4):
             at = slice(j * w, (j + 1) * w)
-            piece = rows // 4
             value = rows_buf[:, at] - got_v[j * piece : (j + 1) * piece].reshape(w, w).T
-            rows_buf[:, at] = value - product_split(lhs_v[...], r_high_v[:, at], r_low_v[:, at])
             if j == 3:
-
-                @pl.when(q == last_q)
-                def _():
-                    rows_buf[:, at] = corner_v[...]
-
+                value = jnp.where(q == last_q, rows_buf[:, at], value)
+            rows_buf[:, at] = value
             stores.append(
-                pltpu.make_async_copy(
-                    rows_buf.at[:, at], out.at[pl.ds(start, w), at], sems.at[len(moves) + j]
-                )
+                pltpu.make_async_copy(rows_buf.at[:, at], out.at[pl.ds(start, w), at], sems.at[2 + j])
             )
             stores[-1].start()
-
-        @pl.when((p == 0) & (q == 0))
-        def _():
-            store = pltpu.make_async_copy(
-                diag_v, out.at[pl.ds(2 * w, w), pl.ds(left, w)], sems.at[len(moves) + 4]
-            )
-            store.start()
-            store.wait()
-
         for store in stores:
             store.wait()
 
 
-def final(base, *operands):
-    w = operands[1].shape[0]
+def final(base, got):
+    w = got.shape[2]
     return pl.pallas_call(
         final_kernel,
         out_shape=tile_shape(*base.shape),
-        in_specs=[HBM] * (1 + len(operands)),
+        in_specs=[HBM] * 2,
         out_specs=HBM,
         scratch_shapes=[
-            pltpu.VMEM(operands[i].shape, operands[i].dtype) for i in range(len(operands))
-        ]
-        + [pltpu.VMEM((w, 4 * w), jnp.float32), pltpu.SemaphoreType.DMA((12,))],
+            pltpu.VMEM(got.shape, jnp.float32),
+            pltpu.VMEM((w, 4 * w), jnp.float32),
+            pltpu.SemaphoreType.DMA((6,)),
+        ],
         input_output_aliases={0: 0},
-        compiler_params=params(16),
-        cost_estimate=cost(2 << 30, 8 << 20),
+        compiler_params=params(8),
+        cost_estimate=cost(1 << 20, 4 << 20),
         name="final",
-    )(base, *[in_hbm(value) for value in operands])
+    )(in_hbm(base), in_hbm(got))
 
 
 def column_hops(top, bottom):
@@ -597,10 +619,22 @@
     theirs = lax.ppermute(
         jnp.stack([small, after, across, before]), COL, [(i, i ^ 1) for i in range(count)]
     )
-    lhs, corner, diag = chain(
-        small, before, after, across, theirs, inverse, inverse_t, diag_t, odd_bottom[low - cut :], r31
+    base = chain(
+        small,
+        before,
+        after,
+        across,
+        theirs,
+        inverse,
+        inverse_t,
+        diag_t,
+        odd_bottom[low - cut :],
+        r31,
+        r_high,
+        r_low,
+        base,
     )
-    return final(base, shares, lhs, corner, diag, r_high, r_low)
+    return final(base, shares)
 
 
 def solution(mesh):

time: 154 us -> 153 us (level)
    pallas_call x1, Pallas kernels: 4.4 us -> 2.69 us  [final(): pl.pallas_call(final_kernel, out_shape=tile_shape(*base.shape), in_specs=...]
  transfers between devices with their start and end apart: 29 -> 29, of which waited for: 13 -> 13; matrix products, arithmetic and copies ran while one was open for 6% -> 6% of each run, Pallas kernels for 22% -> 23%
where the time goes in v4:
time: 153 us; the launch traced here: 150 us
  starting transfers between devices  56.6 us (37%)
  Pallas kernels  40.9 us (27%)
  waiting for transfers between devices  38.3 us (25%)
  other arithmetic  7.84 us (5%)
  local copies, waits for them, and re-layouts  6.24 us (4%)
    pallas_call x1, Pallas kernels, invert(): pl.pallas_call(invert_kernel, out_shape=(pltpu.HBM((2, w, w), jnp.float32...  13.6 us
    all_to_all x1, waiting for transfers between devices, per_device(): terms = lax.all_to_all(terms, ROW, 0, 0)  10.9 us
    ppermute x1, waiting for transfers between devices, column_hops(): lower = lax.ppermute(far_bottom, COL, [(last - 1, 4), (1, last - 4)])  7.47 us
    pallas_call x1, Pallas kernels, sums(): pl.pallas_call(sums_kernel, grid=(4,), out_shape=(pltpu.HBM((rows, height...  7.29 us
    all_to_all x1, starting transfers between devices, per_device(): terms = lax.all_to_all(terms, ROW, 0, 0)  6.44 us
    pallas_call x1, Pallas kernels, trail(): pl.pallas_call(trail_kernel, grid=(steps,), out_shape=pltpu.HBM(adjoint.s...  6.21 us
    ppermute x3, waiting for transfers between devices, per_device(): lax.ppermute(small, COL, [(i, (i + step) % count) for i in range(count)])  6 us
    ppermute x1, starting transfers between devices, row_spread(): lax.ppermute(mine, ROW, [e for s in lines for e in ((s, s + top), (s + to...  5.99 us
  transfers between devices with their start and end apart: 29, of which 13 were waited for; matrix products, arithmetic and copies ran while one was open for 6% of the time, Pallas kernels for 23%

profile of v4, /device:TPU:16, one launch (start us, length us, event | category | flops | bytes accessed | tf_op | source)
XLA Modules:
  0.0 150.3 jit_solution(6899409388467610163)
XLA Ops:
  0.0 2.0 %dynamic-slice_select_fusion.1 = (f32[64,1024]{1,0:T(8,128)}, f32[64,1024]{1,0:T(8,128)S(1)}, f32[64,1024]{1,0:T(8,128)S(1)}) fusion(f32[1024,2048]{1,0:T(8,128)} %factor.1, s32[]{:T(128)S(6)} %add.16, s32[]{:T(128)S(6)} %add.15, pred[]{:T(512)S(6)} %eq.83, s32[]{:T(128)S(6)} %select_n.177, s32[]{:T(128)S(6)} %add.17), kind=kLoop, calls=%fused_computation.19 | loop fusion | flops 196608 | bytes 1835025 | tf_op jit(solution)/shard_map/jit(_where)/select_n | solution.py:542
  2.0 4.5 %collective-permute-start.2 = (f32[64,1024]{1,0:T(8,128)}, f32[64,1024]{1,0:T(8,128)}, u32[]{:S(2)}, u32[]{:S(2)}) collective-permute-start(f32[64,1024]{1,0:T(8,128)} %get-tuple-element.53), channel_id=1, source_target_pairs={{0,32},{120,88},{1,33},{121,89},{2,34},{122,90},{3,35},{123,91},{4... | collective-permute-start | bytes 786440 | tf_op jit(solution)/shard_map/ppermute | solution.py:541
  6.6 3.3 %collective-permute-start = (f32[64,1024]{1,0:T(8,128)S(1)}, f32[64,1024]{1,0:T(8,128)}, u32[]{:S(2)}, u32[]{:S(2)}) collective-permute-start(f32[64,1024]{1,0:T(8,128)S(1)} %get-tuple-element.54), channel_id=1, source_target_pairs={{0,64},{120,56},{1,65},{121,57},{2,66},{122,58},{3,67},{123,59},{4... | collective-permute-start | bytes 786440 | tf_op jit(solution)/shard_map/ppermute | solution.py:545
  9.9 2.0 %collective-permute-start.1 = (f32[64,1024]{1,0:T(8,128)S(1)}, f32[64,1024]{1,0:T(8,128)}, u32[]{:S(2)}, u32[]{:S(2)}) collective-permute-start(f32[64,1024]{1,0:T(8,128)S(1)} %get-tuple-element.55), channel_id=1, source_target_pairs={{0,96},{120,24},{1,97},{121,25},{2,98},{122,26},{3,99},{123,27},{4... | collective-permute-start | bytes 786440 | tf_op jit(solution)/shard_map/ppermute | solution.py:544
  19.8 6.0 %collective-permute-start.13 = (f32[64,1024]{1,0:T(8,128)S(1)}, f32[64,1024]{1,0:T(8,128)S(1)}, u32[]{:S(2)}, u32[]{:S(2)}) collective-permute-start(f32[64,1024]{1,0:T(8,128)S(1)} %select_select_fusion.3), channel_id=1, source_target_pairs={{0,24},{24,0},{32,56},{56,32},{64,88},{88,64},{96,120},{120,96},{1... | collective-permute-start | bytes 786440 | tf_op jit(solution)/shard_map/ppermute | solution.py:559
  28.6 2.0 %collective-permute-start.12 = (f32[64,1024]{1,0:T(8,128)S(1)}, f32[64,1024]{1,0:T(8,128)}, u32[]{:S(2)}, u32[]{:S(2)}) collective-permute-start(f32[64,1024]{1,0:T(8,128)S(1)} %select_select_fusion.3), channel_id=1, source_target_pairs={{0,16},{24,8},{32,48},{56,40},{64,80},{88,72},{96,112},{120,104},{... | collective-permute-start | bytes 786440 | tf_op jit(solution)/shard_map/ppermute | solution.py:560
  32.5 2.0 %collective-permute-start.11 = (f32[64,1024]{1,0:T(8,128)S(1)}, f32[64,1024]{1,0:T(8,128)}, u32[]{:S(2)}, u32[]{:S(2)}) collective-permute-start(f32[64,1024]{1,0:T(8,128)S(1)} %select_select_fusion.3), channel_id=1, source_target_pairs={{0,8},{24,16},{32,40},{56,48},{64,72},{88,80},{96,104},{120,112},{... | collective-permute-start | bytes 786440 | tf_op jit(solution)/shard_map/ppermute | solution.py:558
  37.2 3.3 %collective-permute-done.11 = f32[64,1024]{1,0:T(8,128)} collective-permute-done((f32[64,1024]{1,0:T(8,128)S(1)}, f32[64,1024]{1,0:T(8,128)}, u32[]{:S(2)}, u32[]{:S(2)}) %collective-permute-start.11) | collective-permute-done | bytes 262176 | tf_op jit(solution)/shard_map/ppermute | solution.py:558
  41.7 2.2 %collective-permute-start.16 = (f32[2,64,1024]{2,1,0:T(8,128)S(1)}, f32[2,64,1024]{2,1,0:T(8,128)S(1)}, u32[]{:S(2)}, u32[]{:S(2)}) collective-permute-start(f32[2,64,1024]{2,1,0:T(8,128)S(1)} %pad_maximum_fusion.2.own), channel_id=1, source_target_pairs={{0,96},{8,104},{16,112},{24,120},{32,0},{40,8},{48,16},{56,24},{64... | collective-permute-start | bytes 1572872 | tf_op jit(solution)/shard_map/ppermute | solution.py:590
  47.2 7.5 %collective-permute-done.9 = f32[640,256]{1,0:T(8,128)S(1)} collective-permute-done((f32[640,256]{1,0:T(8,128)S(1)}, f32[640,256]{1,0:T(8,128)S(1)}, u32[]{:S(2)}, u32[]{:S(2)}) %collective-permute-start.9) | collective-permute-done | bytes 655392 | tf_op jit(solution)/shard_map/ppermute | solution.py:519
  60.1 7.3 %sums.1 = (f32[16,136,256]{2,1,0:T(8,128)}, f32[512,256]{1,0:T(8,128)}, f32[512,256]{1,0:T(8,128)}) custom-call(f32[640,256]{1,0:T(8,128)S(1)} %get-tuple-element.59.even_top, f32[640,256]{1,0:T(8,128)S(1)} %get-tuple-element.57.even_bottom, f32[640,256]{1,0:T(8,128)S(1)} %get-tuple-element.58.odd_top, f32[640,256]{1,0:T(8,128)S(1)} %get-tuple-element.56.odd_bottom, ...), custom_call_target="tpu_custom_call" | custom-call | flops 4294967296 | bytes 8388608 | tf_op jit(solution)/shard_map/sums/pallas_call | solution.py:221
  67.4 1.9 %collective-permute-done.15.across_first = f32[64,1024]{1,0:T(8,128)S(1)} collective-permute-done((f32[64,1024]{1,0:T(8,128)S(1)}, f32[64,1024]{1,0:T(8,128)S(1)}, u32[]{:S(2)}, u32[]{:S(2)}) %collective-permute-start.15) | collective-permute-done | bytes 262176 | tf_op jit(solution)/shard_map/ppermute | solution.py:596
  70.0 6.4 %all-to-all-start = ((f32[16,136,256]{2,1,0:T(8,128)}), f32[16,136,256]{2,1,0:T(8,128)S(1)}, u32[]{:S(2)}, u32[]{:S(2)}) async-start(f32[16,136,256]{2,1,0:T(8,128)} %get-tuple-element.33), calls=%async_computation | async-start | bytes 4456448 | tf_op jit(solution)/shard_map/all_to_all | solution.py:599
  76.5 3.0 %rows.1 = (f32[256,256]{1,0:T(8,128)}, bf16[512,1024]{1,0:T(8,128)(2,1)}, bf16[512,1024]{1,0:T(8,128)(2,1)}) custom-call(f32[2,64,1024]{2,1,0:T(8,128)} %copy-done.4, f32[2,64,1024]{2,1,0:T(8,128)} %copy-done.5, f32[2,64,1024]{2,1,0:T(8,128)} %copy-done.6, f32[64,1024]{1,0:T(8,128)} %copy-done.9, f32[64,1024]{1,0:T(8,128)} %copy-done.8), custom_call_target="tpu_custom_call" | custom-call | flops 1024 | bytes 524288 | tf_op jit(solution)/shard_map/rows/pallas_call | solution.py:149
  85.9 13.6 %invert.1 = (f32[2,256,256]{2,1,0:T(8,128)}, f32[2,256,256]{2,1,0:T(8,128)}, f32[1024,2048]{1,0:T(8,128)}) custom-call(f32[2,256,256]{2,1,0:T(8,128)S(1)} %copy-done.1, f32[1024,2048]{1,0:T(8,128)} %adj.3, f32[512,256]{1,0:T(8,128)} %get-tuple-element.34.a0), custom_call_target="tpu_custom_call" | custom-call | flops 5637144576 | bytes 1048576 | tf_op jit(solution)/shard_map/invert/pallas_call | solution.py:112
  100.3 10.9 %all-to-all-done.terms = f32[16,136,256]{2,1,0:T(8,128)S(1)} async-done(((f32[16,136,256]{2,1,0:T(8,128)}), f32[16,136,256]{2,1,0:T(8,128)S(1)}, u32[]{:S(2)}, u32[]{:S(2)}) %all-to-all-start) | async-done | bytes 2228256 | tf_op jit(solution)/shard_map/all_to_all | solution.py:599
  111.2 2.9 %middle.1 = (f32[16,64,256]{2,1,0:T(8,128)}, f32[16,8,256]{2,1,0:T(8,128)}) custom-call(f32[16,136,256]{2,1,0:T(8,128)S(1)} %all-to-all-done.terms, f32[256,256]{1,0:T(8,128)} %broadcast_select_fusion.4.r31, f32[256,256]{1,0:T(8,128)} %get-tuple-element.62.inv1), custom_call_target="tpu_custom_call" | custom-call | flops 268435456 | bytes 6291456 | tf_op jit(solution)/shard_map/middle/pallas_call | solution.py:279
  114.1 3.5 %all-to-all-start.1 = ((f32[16,8,256]{2,1,0:T(8,128)}), f32[16,8,256]{2,1,0:T(8,128)S(1)}, u32[]{:S(2)}, u32[]{:S(2)}) async-start(f32[16,8,256]{2,1,0:T(8,128)} %get-tuple-element.42), calls=%async_computation.1 | async-start | bytes 262144 | tf_op jit(solution)/shard_map/all_to_all | solution.py:611
  117.6 6.2 %trail.1.base = f32[1024,2048]{1,0:T(8,128)} custom-call(f32[1024,2048]{1,0:T(8,128)} %adj.3, f32[512,256]{1,0:T(8,128)} %get-tuple-element.34.a0, f32[512,256]{1,0:T(8,128)} %get-tuple-element.44.l1, f32[256,256]{1,0:T(8,128)} %get-tuple-element.62.inv1, f32[256,256]{1,0:T(8,128)} %broadcast_select_fusion.4.r31, ...), custom_call_target="tpu_custom_call", output_to_operand_aliasing={{}: (7, {})} | custom-call | flops 4294967296 | bytes 10485760 | tf_op jit(solution)/shard_map/trail/pallas_call | solution.py:326
  125.6 5.5 %all-to-all-start.2 = ((f32[16,64,256]{2,1,0:T(8,128)}), f32[16,64,256]{2,1,0:T(8,128)}, u32[]{:S(2)}, u32[]{:S(2)}) async-start(f32[16,64,256]{2,1,0:T(8,128)} %get-tuple-element.52), calls=%async_computation.2 | async-start | bytes 2097152 | tf_op jit(solution)/shard_map/all_to_all | solution.py:614
  131.4 1.9 %collective-permute-start.22 = (f32[16,8,256]{2,1,0:T(8,128)S(1)}, f32[16,8,256]{2,1,0:T(8,128)S(1)}, u32[]{:S(2)}, u32[]{:S(2)}) collective-permute-start(f32[16,8,256]{2,1,0:T(8,128)S(1)} %all-to-all-done.1.mine), channel_id=1, source_target_pairs={{0,2},{1,3},{2,4},{3,5},{4,6},{5,7},{6,0},{7,1},{8,10},{9,11},{10,... | collective-permute-start | bytes 393224 | tf_op jit(solution)/shard_map/ppermute | solution.py:617
  133.3 4.7 %collective-permute-done.24.across = f32[16,8,256]{2,1,0:T(8,128)S(1)} collective-permute-done((f32[16,8,256]{2,1,0:T(8,128)S(1)}, f32[16,8,256]{2,1,0:T(8,128)S(1)}, u32[]{:S(2)}, u32[]{:S(2)}) %collective-permute-start.24) | collective-permute-done | bytes 131104 | tf_op jit(solution)/shard_map/ppermute | solution.py:617
  141.4 5.2 %chain.1.base = f32[1024,2048]{1,0:T(8,128)} custom-call(f32[16,8,256]{2,1,0:T(8,128)S(1)} %all-to-all-done.1.mine, f32[16,8,256]{2,1,0:T(8,128)S(1)} %collective-permute-done.22.before, f32[16,8,256]{2,1,0:T(8,128)S(1)} %collective-permute-done.23.after, f32[16,8,256]{2,1,0:T(8,128)S(1)} %collective-permute-done.24.across, ...), custom_call_target="tpu_custom_call", output_to_operand_aliasing={{}: (12, {})} | custom-call | flops 1048576 | bytes 1024 | tf_op jit(solution)/shard_map/chain/pallas_call | solution.py:435
  147.5 2.7 %final.1 = f32[1024,2048]{1,0:T(8,128)} custom-call(f32[1024,2048]{1,0:T(8,128)} %chain.1.base, f32[16,64,256]{2,1,0:T(8,128)} %all-to-all-done.2.got), custom_call_target="tpu_custom_call", output_to_operand_aliasing={{}: (0, {})} | custom-call | flops 1048576 | bytes 4194304 | tf_op jit(solution)/shard_map/final/pallas_call | solution.py:493
  (81 shorter events, 39.2 us)
Async XLA Ops:
  2.0 14.0 %collective-permute-start.2 = (f32[64,1024]{1,0:T(8,128)}, f32[64,1024]{1,0:T(8,128)}, u32[]{:S(2)}, u32[]{:S(2)}) collective-permute-start(f32[64,1024]{1,0:T(8,128)} %get-tuple-element.53), channel_id=1, source_target_pairs={{0,32},{120,88},{1,33},{121,89},{2,34},{122,90},{3,35},{123,91},{4... | collective-permute-start | bytes 786440 | tf_op jit(solution)/shard_map/ppermute | solution.py:541
  6.6 10.7 %collective-permute-start = (f32[64,1024]{1,0:T(8,128)S(1)}, f32[64,1024]{1,0:T(8,128)}, u32[]{:S(2)}, u32[]{:S(2)}) collective-permute-start(f32[64,1024]{1,0:T(8,128)S(1)} %get-tuple-element.54), channel_id=1, source_target_pairs={{0,64},{120,56},{1,65},{121,57},{2,66},{122,58},{3,67},{123,59},{4... | collective-permute-start | bytes 786440 | tf_op jit(solution)/shard_map/ppermute | solution.py:545
  9.9 7.3 %collective-permute-start.1 = (f32[64,1024]{1,0:T(8,128)S(1)}, f32[64,1024]{1,0:T(8,128)}, u32[]{:S(2)}, u32[]{:S(2)}) collective-permute-start(f32[64,1024]{1,0:T(8,128)S(1)} %get-tuple-element.55), channel_id=1, source_target_pairs={{0,96},{120,24},{1,97},{121,25},{2,98},{122,26},{3,99},{123,27},{4... | collective-permute-start | bytes 786440 | tf_op jit(solution)/shard_map/ppermute | solution.py:544
  18.3 8.9 %collective-permute-start.3 = (f32[640,256]{1,0:T(8,128)S(1)}, f32[640,256]{1,0:T(8,128)S(1)}, u32[]{:S(2)}, u32[]{:S(2)}) collective-permute-start(f32[640,256]{1,0:T(8,128)S(1)} %get-tuple-element.29), channel_id=1, source_target_pairs={{0,2},{7,5},{8,10},{15,13},{16,18},{23,21},{24,26},{31,29},{32,34}... | collective-permute-start | bytes 1966088 | tf_op jit(solution)/shard_map/ppermute | solution.py:514
  19.0 16.9 %collective-permute-start.8 = (f32[640,256]{1,0:T(8,128)S(1)}, f32[640,256]{1,0:T(8,128)S(1)}, u32[]{:S(2)}, u32[]{:S(2)}) collective-permute-start(f32[640,256]{1,0:T(8,128)S(1)} %get-tuple-element.30), channel_id=1, source_target_pairs={{0,6},{7,1},{8,14},{15,9},{16,22},{23,17},{24,30},{31,25},{32,38},... | collective-permute-start | bytes 1966088 | tf_op jit(solution)/shard_map/ppermute | solution.py:515
  19.8 12.0 %collective-permute-start.13 = (f32[64,1024]{1,0:T(8,128)S(1)}, f32[64,1024]{1,0:T(8,128)S(1)}, u32[]{:S(2)}, u32[]{:S(2)}) collective-permute-start(f32[64,1024]{1,0:T(8,128)S(1)} %select_select_fusion.3), channel_id=1, source_target_pairs={{0,24},{24,0},{32,56},{56,32},{64,88},{88,64},{96,120},{120,96},{1... | collective-permute-start | bytes 786440 | tf_op jit(solution)/shard_map/ppermute | solution.py:559
  25.7 18.2 %collective-permute-start.4 = (f32[640,256]{1,0:T(8,128)S(1)}, f32[640,256]{1,0:T(8,128)}, u32[]{:S(2)}, u32[]{:S(2)}) collective-permute-start(f32[640,256]{1,0:T(8,128)S(1)} %get-tuple-element.29), channel_id=1, source_target_pairs={{0,6},{7,1},{8,14},{15,9},{16,22},{23,17},{24,30},{31,25},{32,38},... | collective-permute-start | bytes 1966088 | tf_op jit(solution)/shard_map/ppermute | solution.py:517
  27.3 18.6 %collective-permute-start.5 = (f32[640,256]{1,0:T(8,128)S(1)}, f32[640,256]{1,0:T(8,128)}, u32[]{:S(2)}, u32[]{:S(2)}) collective-permute-start(f32[640,256]{1,0:T(8,128)S(1)} %collective-permute-done.3), channel_id=1, source_target_pairs={{2,4},{5,3},{10,12},{13,11},{18,20},{21,19},{26,28},{29,27},{34,36... | collective-permute-start | bytes 1966088 | tf_op jit(solution)/shard_map/ppermute | solution.py:518
  28.6 6.7 %collective-permute-start.12 = (f32[64,1024]{1,0:T(8,128)S(1)}, f32[64,1024]{1,0:T(8,128)}, u32[]{:S(2)}, u32[]{:S(2)}) collective-permute-start(f32[64,1024]{1,0:T(8,128)S(1)} %select_select_fusion.3), channel_id=1, source_target_pairs={{0,16},{24,8},{32,48},{56,40},{64,80},{88,72},{96,112},{120,104},{... | collective-permute-start | bytes 786440 | tf_op jit(solution)/shard_map/ppermute | solution.py:560
  32.5 8.0 %collective-permute-start.11 = (f32[64,1024]{1,0:T(8,128)S(1)}, f32[64,1024]{1,0:T(8,128)}, u32[]{:S(2)}, u32[]{:S(2)}) collective-permute-start(f32[64,1024]{1,0:T(8,128)S(1)} %select_select_fusion.3), channel_id=1, source_target_pairs={{0,8},{24,16},{32,40},{56,48},{64,72},{88,80},{96,104},{120,112},{... | collective-permute-start | bytes 786440 | tf_op jit(solution)/shard_map/ppermute | solution.py:558
  35.2 12.0 %collective-permute-start.7 = (f32[640,256]{1,0:T(8,128)S(1)}, f32[640,256]{1,0:T(8,128)S(1)}, u32[]{:S(2)}, u32[]{:S(2)}) collective-permute-start(f32[640,256]{1,0:T(8,128)S(1)} %get-tuple-element.30), channel_id=1, source_target_pairs={{0,2},{7,5},{8,10},{15,13},{16,18},{23,21},{24,26},{31,29},{32,34}... | collective-permute-start | bytes 1966088 | tf_op jit(solution)/shard_map/ppermute | solution.py:516
  35.9 18.8 %collective-permute-start.9 = (f32[640,256]{1,0:T(8,128)S(1)}, f32[640,256]{1,0:T(8,128)S(1)}, u32[]{:S(2)}, u32[]{:S(2)}) collective-permute-start(f32[640,256]{1,0:T(8,128)S(1)} %collective-permute-done.8), channel_id=1, source_target_pairs={{6,4},{1,3},{14,12},{9,11},{22,20},{17,19},{30,28},{25,27},{38,36}... | collective-permute-start | bytes 1966088 | tf_op jit(solution)/shard_map/ppermute | solution.py:519
  41.7 15.9 %collective-permute-start.16 = (f32[2,64,1024]{2,1,0:T(8,128)S(1)}, f32[2,64,1024]{2,1,0:T(8,128)S(1)}, u32[]{:S(2)}, u32[]{:S(2)}) collective-permute-start(f32[2,64,1024]{2,1,0:T(8,128)S(1)} %pad_maximum_fusion.2.own), channel_id=1, source_target_pairs={{0,96},{8,104},{16,112},{24,120},{32,0},{40,8},{48,16},{56,24},{64... | collective-permute-start | bytes 1572872 | tf_op jit(solution)/shard_map/ppermute | solution.py:590
  44.0 15.3 %collective-permute-start.14 = (f32[2,64,1024]{2,1,0:T(8,128)S(1)}, f32[2,64,1024]{2,1,0:T(8,128)S(1)}, u32[]{:S(2)}, u32[]{:S(2)}) collective-permute-start(f32[2,64,1024]{2,1,0:T(8,128)S(1)} %pad_maximum_fusion.2.own), channel_id=1, source_target_pairs={{0,32},{8,40},{16,48},{24,56},{32,64},{40,72},{48,80},{56,88},{64,... | collective-permute-start | bytes 1572872 | tf_op jit(solution)/shard_map/ppermute | solution.py:589
  47.1 12.8 %collective-permute-start.6 = (f32[640,256]{1,0:T(8,128)S(1)}, f32[640,256]{1,0:T(8,128)S(1)}, u32[]{:S(2)}, u32[]{:S(2)}) collective-permute-start(f32[640,256]{1,0:T(8,128)S(1)} %select_select_fusion.1), channel_id=1, source_target_pairs={{0,1},{1,0},{2,3},{3,2},{4,5},{5,4},{6,7},{7,6},{8,9},{9,8},{10,11... | collective-permute-start | bytes 1966088 | tf_op jit(solution)/shard_map/ppermute | solution.py:530
  57.7 9.7 %collective-permute-start.17 = (f32[64,1024]{1,0:T(8,128)S(1)}, f32[64,1024]{1,0:T(8,128)S(1)}, u32[]{:S(2)}, u32[]{:S(2)}) collective-permute-start(f32[64,1024]{1,0:T(8,128)S(1)} %slice_bitcast_fusion), channel_id=1, source_target_pairs={{0,96},{8,104},{16,112},{24,120},{32,0},{40,8},{48,16},{56,24},{64... | collective-permute-start | bytes 786440 | tf_op jit(solution)/shard_map/ppermute | solution.py:597
  59.3 10.0 %collective-permute-start.15 = (f32[64,1024]{1,0:T(8,128)S(1)}, f32[64,1024]{1,0:T(8,128)S(1)}, u32[]{:S(2)}, u32[]{:S(2)}) collective-permute-start(f32[64,1024]{1,0:T(8,128)S(1)} %slice_bitcast_fusion.1), channel_id=1, source_target_pairs={{0,32},{8,40},{16,48},{24,56},{32,64},{40,72},{48,80},{56,88},{64,... | collective-permute-start | bytes 786440 | tf_op jit(solution)/shard_map/ppermute | solution.py:596
  70.0 41.2 %all-to-all-start = ((f32[16,136,256]{2,1,0:T(8,128)}), f32[16,136,256]{2,1,0:T(8,128)S(1)}, u32[]{:S(2)}, u32[]{:S(2)}) async-start(f32[16,136,256]{2,1,0:T(8,128)} %get-tuple-element.33), calls=%async_computation | async-start | bytes 4456448 | tf_op jit(solution)/shard_map/all_to_all | solution.py:599
  84.6 14.9 %collective-permute-start.21 = (f32[256,256]{1,0:T(8,128)S(1)}, f32[256,256]{1,0:T(8,128)S(1)}, u32[]{:S(2)}, u32[]{:S(2)}) collective-permute-start(f32[256,256]{1,0:T(8,128)S(1)} %select_select_fusion.2), channel_id=1, source_target_pairs={{1,0},{3,2},{5,4},{7,6},{9,8},{11,10},{13,12},{15,14},{17,16},{19,... | collective-permute-start | bytes 786440 | tf_op jit(solution)/shard_map/ppermute | solution.py:608
  114.1 11.5 %all-to-all-start.1 = ((f32[16,8,256]{2,1,0:T(8,128)}), f32[16,8,256]{2,1,0:T(8,128)S(1)}, u32[]{:S(2)}, u32[]{:S(2)}) async-start(f32[16,8,256]{2,1,0:T(8,128)} %get-tuple-element.42), calls=%async_computation.1 | async-start | bytes 262144 | tf_op jit(solution)/shard_map/all_to_all | solution.py:611
  125.6 21.9 %all-to-all-start.2 = ((f32[16,64,256]{2,1,0:T(8,128)}), f32[16,64,256]{2,1,0:T(8,128)}, u32[]{:S(2)}, u32[]{:S(2)}) async-start(f32[16,64,256]{2,1,0:T(8,128)} %get-tuple-element.52), calls=%async_computation.2 | async-start | bytes 2097152 | tf_op jit(solution)/shard_map/all_to_all | solution.py:614
  131.1 6.9 %collective-permute-start.24 = (f32[16,8,256]{2,1,0:T(8,128)S(1)}, f32[16,8,256]{2,1,0:T(8,128)S(1)}, u32[]{:S(2)}, u32[]{:S(2)}) collective-permute-start(f32[16,8,256]{2,1,0:T(8,128)S(1)} %all-to-all-done.1.mine), channel_id=1, source_target_pairs={{0,4},{1,5},{2,6},{3,7},{4,0},{5,1},{6,2},{7,3},{8,12},{9,13},{10,... | collective-permute-start | bytes 393224 | tf_op jit(solution)/shard_map/ppermute | solution.py:617
  131.2 6.8 %collective-permute-start.23 = (f32[16,8,256]{2,1,0:T(8,128)S(1)}, f32[16,8,256]{2,1,0:T(8,128)S(1)}, u32[]{:S(2)}, u32[]{:S(2)}) collective-permute-start(f32[16,8,256]{2,1,0:T(8,128)S(1)} %all-to-all-done.1.mine), channel_id=1, source_target_pairs={{0,6},{1,7},{2,0},{3,1},{4,2},{5,3},{6,4},{7,5},{8,14},{9,15},{10,... | collective-permute-start | bytes 393224 | tf_op jit(solution)/shard_map/ppermute | solution.py:617
  131.4 7.9 %collective-permute-start.22 = (f32[16,8,256]{2,1,0:T(8,128)S(1)}, f32[16,8,256]{2,1,0:T(8,128)S(1)}, u32[]{:S(2)}, u32[]{:S(2)}) collective-permute-start(f32[16,8,256]{2,1,0:T(8,128)S(1)} %all-to-all-done.1.mine), channel_id=1, source_target_pairs={{0,2},{1,3},{2,4},{3,5},{4,6},{5,7},{6,0},{7,1},{8,10},{9,11},{10,... | collective-permute-start | bytes 393224 | tf_op jit(solution)/shard_map/ppermute | solution.py:617
  (15 other events, 167.7 us)

commit v5 on v4

--- a/solution.py
+++ b/solution.py
@@ -583,7 +583,7 @@
     bottom = jnp.concatenate([fac_col[cut:], adjoint[w:low, left - w : left]], axis=0)
     row_block = lax.dynamic_slice(factor, (jnp.where(p == 0, low, w), 0), (w, left))
     quarter = row_quarters(row_block)
-    top, bottom, quarter = lax.optimization_barrier((top, bottom, quarter))
+    top, quarter = lax.optimization_barrier((top, quarter))
     top, bottom = column_hops(top, bottom)
     own = row_spread(quarter)
     up = lax.ppermute(own, ROW, ring_pairs(1))

time: 153 us -> 151 us (0.987)
  starting transfers between devices: 56.6 us -> 51.7 us
  waiting for transfers between devices: 38.3 us -> 42.3 us
    ppermute x1, waiting for transfers between devices: 7.47 us -> 0.01 us  [column_hops(): lower = lax.ppermute(far_bottom, COL, [(last - 1, 4), (1, last - 4)])]
    ppermute x1, waiting for transfers between devices: 1.51 us -> 5.91 us  [per_device(): down = lax.ppermute(own, ROW, ring_pairs(-1))]
    ppermute x1, waiting for transfers between devices: 0.01 us -> 2.7 us  [column_hops(): upper = lax.ppermute(near_top, COL, [(2, 4), (last - 2, last - 4)])]
    ppermute x1, waiting for transfers between devices: 1.21 us -> 3.74 us  [row_quarters(): lax.ppermute(jnp.where(first, quarters[2], quarters[1]), ROW, [(0, 2 * RI...]
    all_to_all x1, starting transfers between devices: 6.44 us -> 4 us  [per_device(): terms = lax.all_to_all(terms, ROW, 0, 0)]
  transfers between devices with their start and end apart: 29 -> 29, of which waited for: 13 -> 14; matrix products, arithmetic and copies ran while one was open for 6% -> 7% of each run, Pallas kernels for 23% -> 24%
where the time goes in v5:
time: 151 us; the launch traced here: 150 us
  starting transfers between devices  51.7 us (34%)
  waiting for transfers between devices  42.3 us (28%)
  Pallas kernels  40.9 us (27%)
  other arithmetic  7.93 us (5%)
  local copies, waits for them, and re-layouts  6.29 us (4%)
    pallas_call x1, Pallas kernels, invert(): pl.pallas_call(invert_kernel, out_shape=(pltpu.HBM((2, w, w), jnp.float32...  13.6 us
    all_to_all x1, waiting for transfers between devices, per_device(): terms = lax.all_to_all(terms, ROW, 0, 0)  10.6 us
    pallas_call x1, Pallas kernels, sums(): pl.pallas_call(sums_kernel, grid=(4,), out_shape=(pltpu.HBM((rows, height...  7.3 us
    ppermute x3, waiting for transfers between devices, per_device(): lax.ppermute(small, COL, [(i, (i + step) % count) for i in range(count)])  6.99 us
    pallas_call x1, Pallas kernels, trail(): pl.pallas_call(trail_kernel, grid=(steps,), out_shape=pltpu.HBM(adjoint.s...  6.21 us
    ppermute x1, waiting for transfers between devices, per_device(): down = lax.ppermute(own, ROW, ring_pairs(-1))  5.91 us
    all_to_all x1, starting transfers between devices, per_device(): shares = lax.all_to_all(shares, ROW, 0, 0)  5.7 us
    ppermute x1, starting transfers between devices, row_spread(): lax.ppermute(mine, ROW, [e for s in lines for e in ((s, s + top), (s + to...  5.49 us
  transfers between devices with their start and end apart: 29, of which 14 were waited for; matrix products, arithmetic and copies ran while one was open for 7% of the time, Pallas kernels for 24%

profile of v5, /device:TPU:16, one launch (start us, length us, event | category | flops | bytes accessed | tf_op | source)
XLA Modules:
  0.0 149.7 jit_solution(10966158187939487071)
XLA Ops:
  4.9 3.8 %collective-permute-start.2 = (f32[64,1024]{1,0:T(8,128)S(1)}, f32[64,1024]{1,0:T(8,128)S(1)}, u32[]{:S(2)}, u32[]{:S(2)}) collective-permute-start(f32[64,1024]{1,0:T(8,128)S(1)} %get-tuple-element.51), channel_id=1, source_target_pairs={{0,32},{120,88},{1,33},{121,89},{2,34},{122,90},{3,35},{123,91},{4... | collective-permute-start | bytes 786440 | tf_op jit(solution)/shard_map/ppermute | solution.py:541
  8.8 3.3 %collective-permute-start = (f32[64,1024]{1,0:T(8,128)S(1)}, f32[64,1024]{1,0:T(8,128)}, u32[]{:S(2)}, u32[]{:S(2)}) collective-permute-start(f32[64,1024]{1,0:T(8,128)S(1)} %get-tuple-element.52), channel_id=1, source_target_pairs={{0,64},{120,56},{1,65},{121,57},{2,66},{122,58},{3,67},{123,59},{4... | collective-permute-start | bytes 786440 | tf_op jit(solution)/shard_map/ppermute | solution.py:545
  12.1 2.0 %collective-permute-start.1 = (f32[64,1024]{1,0:T(8,128)S(1)}, f32[64,1024]{1,0:T(8,128)}, u32[]{:S(2)}, u32[]{:S(2)}) collective-permute-start(f32[64,1024]{1,0:T(8,128)S(1)} %get-tuple-element.53), channel_id=1, source_target_pairs={{0,96},{120,24},{1,97},{121,25},{2,98},{122,26},{3,99},{123,27},{4... | collective-permute-start | bytes 786440 | tf_op jit(solution)/shard_map/ppermute | solution.py:544
  16.2 3.7 %collective-permute-done = f32[64,1024]{1,0:T(8,128)} collective-permute-done((f32[64,1024]{1,0:T(8,128)S(1)}, f32[64,1024]{1,0:T(8,128)}, u32[]{:S(2)}, u32[]{:S(2)}) %collective-permute-start) | collective-permute-done | bytes 262176 | tf_op jit(solution)/shard_map/ppermute | solution.py:545
  21.8 5.5 %collective-permute-start.13 = (f32[64,1024]{1,0:T(8,128)S(1)}, f32[64,1024]{1,0:T(8,128)S(1)}, u32[]{:S(2)}, u32[]{:S(2)}) collective-permute-start(f32[64,1024]{1,0:T(8,128)S(1)} %select_select_fusion.3), channel_id=1, source_target_pairs={{0,24},{24,0},{32,56},{56,32},{64,88},{88,64},{96,120},{120,96},{1... | collective-permute-start | bytes 786440 | tf_op jit(solution)/shard_map/ppermute | solution.py:559
  30.1 2.0 %collective-permute-start.12 = (f32[64,1024]{1,0:T(8,128)S(1)}, f32[64,1024]{1,0:T(8,128)}, u32[]{:S(2)}, u32[]{:S(2)}) collective-permute-start(f32[64,1024]{1,0:T(8,128)S(1)} %select_select_fusion.3), channel_id=1, source_target_pairs={{0,16},{24,8},{32,48},{56,40},{64,80},{88,72},{96,112},{120,104},{... | collective-permute-start | bytes 786440 | tf_op jit(solution)/shard_map/ppermute | solution.py:560
  34.0 2.0 %collective-permute-start.11 = (f32[64,1024]{1,0:T(8,128)S(1)}, f32[64,1024]{1,0:T(8,128)}, u32[]{:S(2)}, u32[]{:S(2)}) collective-permute-start(f32[64,1024]{1,0:T(8,128)S(1)} %select_select_fusion.3), channel_id=1, source_target_pairs={{0,8},{24,16},{32,40},{56,48},{64,72},{88,80},{96,104},{120,112},{... | collective-permute-start | bytes 786440 | tf_op jit(solution)/shard_map/ppermute | solution.py:558
  40.1 2.1 %collective-permute-done.11 = f32[64,1024]{1,0:T(8,128)} collective-permute-done((f32[64,1024]{1,0:T(8,128)S(1)}, f32[64,1024]{1,0:T(8,128)}, u32[]{:S(2)}, u32[]{:S(2)}) %collective-permute-start.11) | collective-permute-done | bytes 262176 | tf_op jit(solution)/shard_map/ppermute | solution.py:558
  43.5 1.8 %collective-permute-start.16 = (f32[2,64,1024]{2,1,0:T(8,128)S(1)}, f32[2,64,1024]{2,1,0:T(8,128)S(1)}, u32[]{:S(2)}, u32[]{:S(2)}) collective-permute-start(f32[2,64,1024]{2,1,0:T(8,128)S(1)} %pad_maximum_fusion.2.own), channel_id=1, source_target_pairs={{0,96},{8,104},{16,112},{24,120},{32,0},{40,8},{48,16},{56,24},{64... | collective-permute-start | bytes 1572872 | tf_op jit(solution)/shard_map/ppermute | solution.py:590
  48.6 2.7 %collective-permute-done.5 = f32[640,256]{1,0:T(8,128)S(1)} collective-permute-done((f32[640,256]{1,0:T(8,128)S(1)}, f32[640,256]{1,0:T(8,128)S(1)}, u32[]{:S(2)}, u32[]{:S(2)}) %collective-permute-start.5) | collective-permute-done | bytes 655392 | tf_op jit(solution)/shard_map/ppermute | solution.py:518
  51.6 5.9 %collective-permute-done.16.down = f32[2,64,1024]{2,1,0:T(8,128)S(1)} collective-permute-done((f32[2,64,1024]{2,1,0:T(8,128)S(1)}, f32[2,64,1024]{2,1,0:T(8,128)S(1)}, u32[]{:S(2)}, u32[]{:S(2)}) %collective-permute-start.16) | collective-permute-done | bytes 524320 | tf_op jit(solution)/shard_map/ppermute | solution.py:590
  61.4 7.3 %sums.1 = (f32[16,136,256]{2,1,0:T(8,128)}, f32[512,256]{1,0:T(8,128)}, f32[512,256]{1,0:T(8,128)}) custom-call(f32[640,256]{1,0:T(8,128)S(1)} %get-tuple-element.57.even_top, f32[640,256]{1,0:T(8,128)S(1)} %get-tuple-element.55.even_bottom, f32[640,256]{1,0:T(8,128)S(1)} %get-tuple-element.56.odd_top, f32[640,256]{1,0:T(8,128)S(1)} %get-tuple-element.54.odd_bottom, ...), custom_call_target="tpu_custom_call" | custom-call | flops 4294967296 | bytes 8388608 | tf_op jit(solution)/shard_map/sums/pallas_call | solution.py:221
  70.7 4.0 %all-to-all-start = ((f32[16,136,256]{2,1,0:T(8,128)}), f32[16,136,256]{2,1,0:T(8,128)S(1)}, u32[]{:S(2)}, u32[]{:S(2)}) async-start(f32[16,136,256]{2,1,0:T(8,128)} %get-tuple-element.31), calls=%async_computation | async-start | bytes 4456448 | tf_op jit(solution)/shard_map/all_to_all | solution.py:599
  74.7 3.0 %rows.1 = (f32[256,256]{1,0:T(8,128)}, bf16[512,1024]{1,0:T(8,128)(2,1)}, bf16[512,1024]{1,0:T(8,128)(2,1)}) custom-call(f32[2,64,1024]{2,1,0:T(8,128)} %copy-done.4, f32[2,64,1024]{2,1,0:T(8,128)} %copy-done.5, f32[2,64,1024]{2,1,0:T(8,128)} %copy-done.6, f32[64,1024]{1,0:T(8,128)} %copy-done.10, f32[64,1024]{1,0:T(8,128)} %copy-done.9), custom_call_target="tpu_custom_call" | custom-call | flops 1024 | bytes 524288 | tf_op jit(solution)/shard_map/rows/pallas_call | solution.py:149
  84.2 13.6 %invert.1 = (f32[2,256,256]{2,1,0:T(8,128)}, f32[2,256,256]{2,1,0:T(8,128)}, f32[1024,2048]{1,0:T(8,128)}) custom-call(f32[2,256,256]{2,1,0:T(8,128)S(1)} %copy-done.1, f32[1024,2048]{1,0:T(8,128)} %adj.3, f32[512,256]{1,0:T(8,128)} %get-tuple-element.32.a0), custom_call_target="tpu_custom_call" | custom-call | flops 5637144576 | bytes 1048576 | tf_op jit(solution)/shard_map/invert/pallas_call | solution.py:112
  98.5 10.6 %all-to-all-done.terms = f32[16,136,256]{2,1,0:T(8,128)S(1)} async-done(((f32[16,136,256]{2,1,0:T(8,128)}), f32[16,136,256]{2,1,0:T(8,128)S(1)}, u32[]{:S(2)}, u32[]{:S(2)}) %all-to-all-start) | async-done | bytes 2228256 | tf_op jit(solution)/shard_map/all_to_all | solution.py:599
  109.1 2.9 %middle.1 = (f32[16,64,256]{2,1,0:T(8,128)}, f32[16,8,256]{2,1,0:T(8,128)}) custom-call(f32[16,136,256]{2,1,0:T(8,128)S(1)} %all-to-all-done.terms, f32[256,256]{1,0:T(8,128)} %broadcast_select_fusion.4.r31, f32[256,256]{1,0:T(8,128)} %get-tuple-element.60.inv1), custom_call_target="tpu_custom_call" | custom-call | flops 268435456 | bytes 6291456 | tf_op jit(solution)/shard_map/middle/pallas_call | solution.py:279
  111.9 3.6 %all-to-all-start.1 = ((f32[16,8,256]{2,1,0:T(8,128)}), f32[16,8,256]{2,1,0:T(8,128)S(1)}, u32[]{:S(2)}, u32[]{:S(2)}) async-start(f32[16,8,256]{2,1,0:T(8,128)} %get-tuple-element.40), calls=%async_computation.1 | async-start | bytes 262144 | tf_op jit(solution)/shard_map/all_to_all | solution.py:611
  115.6 6.2 %trail.1.base = f32[1024,2048]{1,0:T(8,128)} custom-call(f32[1024,2048]{1,0:T(8,128)} %adj.3, f32[512,256]{1,0:T(8,128)} %get-tuple-element.32.a0, f32[512,256]{1,0:T(8,128)} %get-tuple-element.42.l1, f32[256,256]{1,0:T(8,128)} %get-tuple-element.60.inv1, f32[256,256]{1,0:T(8,128)} %broadcast_select_fusion.4.r31, ...), custom_call_target="tpu_custom_call", output_to_operand_aliasing={{}: (7, {})} | custom-call | flops 4294967296 | bytes 10485760 | tf_op jit(solution)/shard_map/trail/pallas_call | solution.py:326
  123.6 5.7 %all-to-all-start.2 = ((f32[16,64,256]{2,1,0:T(8,128)}), f32[16,64,256]{2,1,0:T(8,128)}, u32[]{:S(2)}, u32[]{:S(2)}) async-start(f32[16,64,256]{2,1,0:T(8,128)} %get-tuple-element.50), calls=%async_computation.2 | async-start | bytes 2097152 | tf_op jit(solution)/shard_map/all_to_all | solution.py:614
  131.5 5.7 %collective-permute-done.24.across = f32[16,8,256]{2,1,0:T(8,128)S(1)} collective-permute-done((f32[16,8,256]{2,1,0:T(8,128)S(1)}, f32[16,8,256]{2,1,0:T(8,128)S(1)}, u32[]{:S(2)}, u32[]{:S(2)}) %collective-permute-start.24) | collective-permute-done | bytes 131104 | tf_op jit(solution)/shard_map/ppermute | solution.py:617
  138.6 1.9 %collective-permute-done.25.theirs = f32[4,16,8,256]{3,2,1,0:T(8,128)S(1)} collective-permute-done((f32[4,16,8,256]{3,2,1,0:T(8,128)S(1)}, f32[4,16,8,256]{3,2,1,0:T(8,128)S(1)}, u32[]{:S(2)}, u32[]{:S(2)}) %collective-permute-start.25) | collective-permute-done | bytes 524320 | tf_op jit(solution)/shard_map/ppermute | solution.py:619
  140.5 5.2 %chain.1.base = f32[1024,2048]{1,0:T(8,128)} custom-call(f32[16,8,256]{2,1,0:T(8,128)S(1)} %all-to-all-done.1.mine, f32[16,8,256]{2,1,0:T(8,128)S(1)} %collective-permute-done.22.before, f32[16,8,256]{2,1,0:T(8,128)S(1)} %collective-permute-done.23.after, f32[16,8,256]{2,1,0:T(8,128)S(1)} %collective-permute-done.24.across, ...), custom_call_target="tpu_custom_call", output_to_operand_aliasing={{}: (12, {})} | custom-call | flops 1048576 | bytes 1024 | tf_op jit(solution)/shard_map/chain/pallas_call | solution.py:435
  146.8 2.7 %final.1 = f32[1024,2048]{1,0:T(8,128)} custom-call(f32[1024,2048]{1,0:T(8,128)} %chain.1.base, f32[16,64,256]{2,1,0:T(8,128)} %all-to-all-done.2.got), custom_call_target="tpu_custom_call", output_to_operand_aliasing={{}: (0, {})} | custom-call | flops 1048576 | bytes 4194304 | tf_op jit(solution)/shard_map/final/pallas_call | solution.py:493
  (84 shorter events, 41.9 us)
Async XLA Ops:
  3.0 25.8 %collective-permute-start.8 = (f32[640,256]{1,0:T(8,128)}, f32[640,256]{1,0:T(8,128)S(1)}, u32[]{:S(2)}, u32[]{:S(2)}) collective-permute-start(f32[640,256]{1,0:T(8,128)} %pad_maximum_fusion.1), channel_id=1, source_target_pairs={{0,6},{7,1},{8,14},{15,9},{16,22},{23,17},{24,30},{31,25},{32,38},... | collective-permute-start | bytes 1966088 | tf_op jit(solution)/shard_map/ppermute | solution.py:515
  4.9 11.2 %collective-permute-start.2 = (f32[64,1024]{1,0:T(8,128)S(1)}, f32[64,1024]{1,0:T(8,128)S(1)}, u32[]{:S(2)}, u32[]{:S(2)}) collective-permute-start(f32[64,1024]{1,0:T(8,128)S(1)} %get-tuple-element.51), channel_id=1, source_target_pairs={{0,32},{120,88},{1,33},{121,89},{2,34},{122,90},{3,35},{123,91},{4... | collective-permute-start | bytes 786440 | tf_op jit(solution)/shard_map/ppermute | solution.py:541
  8.8 11.1 %collective-permute-start = (f32[64,1024]{1,0:T(8,128)S(1)}, f32[64,1024]{1,0:T(8,128)}, u32[]{:S(2)}, u32[]{:S(2)}) collective-permute-start(f32[64,1024]{1,0:T(8,128)S(1)} %get-tuple-element.52), channel_id=1, source_target_pairs={{0,64},{120,56},{1,65},{121,57},{2,66},{122,58},{3,67},{123,59},{4... | collective-permute-start | bytes 786440 | tf_op jit(solution)/shard_map/ppermute | solution.py:545
  12.1 7.8 %collective-permute-start.1 = (f32[64,1024]{1,0:T(8,128)S(1)}, f32[64,1024]{1,0:T(8,128)}, u32[]{:S(2)}, u32[]{:S(2)}) collective-permute-start(f32[64,1024]{1,0:T(8,128)S(1)} %get-tuple-element.53), channel_id=1, source_target_pairs={{0,96},{120,24},{1,97},{121,25},{2,98},{122,26},{3,99},{123,27},{4... | collective-permute-start | bytes 786440 | tf_op jit(solution)/shard_map/ppermute | solution.py:544
  21.0 17.8 %collective-permute-start.3 = (f32[640,256]{1,0:T(8,128)S(1)}, f32[640,256]{1,0:T(8,128)S(1)}, u32[]{:S(2)}, u32[]{:S(2)}) collective-permute-start(f32[640,256]{1,0:T(8,128)S(1)} %pad_maximum_fusion), channel_id=1, source_target_pairs={{0,2},{7,5},{8,10},{15,13},{16,18},{23,21},{24,26},{31,29},{32,34}... | collective-permute-start | bytes 1966088 | tf_op jit(solution)/shard_map/ppermute | solution.py:514
  21.8 11.5 %collective-permute-start.13 = (f32[64,1024]{1,0:T(8,128)S(1)}, f32[64,1024]{1,0:T(8,128)S(1)}, u32[]{:S(2)}, u32[]{:S(2)}) collective-permute-start(f32[64,1024]{1,0:T(8,128)S(1)} %select_select_fusion.3), channel_id=1, source_target_pairs={{0,24},{24,0},{32,56},{56,32},{64,88},{88,64},{96,120},{120,96},{1... | collective-permute-start | bytes 786440 | tf_op jit(solution)/shard_map/ppermute | solution.py:559
  27.3 18.0 %collective-permute-start.7 = (f32[640,256]{1,0:T(8,128)}, f32[640,256]{1,0:T(8,128)}, u32[]{:S(2)}, u32[]{:S(2)}) collective-permute-start(f32[640,256]{1,0:T(8,128)} %pad_maximum_fusion.1), channel_id=1, source_target_pairs={{0,2},{7,5},{8,10},{15,13},{16,18},{23,21},{24,26},{31,29},{32,34}... | collective-permute-start | bytes 1966088 | tf_op jit(solution)/shard_map/ppermute | solution.py:516
  28.8 18.1 %collective-permute-start.9 = (f32[640,256]{1,0:T(8,128)S(1)}, f32[640,256]{1,0:T(8,128)}, u32[]{:S(2)}, u32[]{:S(2)}) collective-permute-start(f32[640,256]{1,0:T(8,128)S(1)} %collective-permute-done.8), channel_id=1, source_target_pairs={{6,4},{1,3},{14,12},{9,11},{22,20},{17,19},{30,28},{25,27},{38,36}... | collective-permute-start | bytes 1966088 | tf_op jit(solution)/shard_map/ppermute | solution.py:519
  30.1 8.0 %collective-permute-start.12 = (f32[64,1024]{1,0:T(8,128)S(1)}, f32[64,1024]{1,0:T(8,128)}, u32[]{:S(2)}, u32[]{:S(2)}) collective-permute-start(f32[64,1024]{1,0:T(8,128)S(1)} %select_select_fusion.3), channel_id=1, source_target_pairs={{0,16},{24,8},{32,48},{56,40},{64,80},{88,72},{96,112},{120,104},{... | collective-permute-start | bytes 786440 | tf_op jit(solution)/shard_map/ppermute | solution.py:560
  34.0 8.3 %collective-permute-start.11 = (f32[64,1024]{1,0:T(8,128)S(1)}, f32[64,1024]{1,0:T(8,128)}, u32[]{:S(2)}, u32[]{:S(2)}) collective-permute-start(f32[64,1024]{1,0:T(8,128)S(1)} %select_select_fusion.3), channel_id=1, source_target_pairs={{0,8},{24,16},{32,40},{56,48},{64,72},{88,80},{96,104},{120,112},{... | collective-permute-start | bytes 786440 | tf_op jit(solution)/shard_map/ppermute | solution.py:558
  38.1 10.5 %collective-permute-start.4 = (f32[640,256]{1,0:T(8,128)S(1)}, f32[640,256]{1,0:T(8,128)S(1)}, u32[]{:S(2)}, u32[]{:S(2)}) collective-permute-start(f32[640,256]{1,0:T(8,128)S(1)} %pad_maximum_fusion), channel_id=1, source_target_pairs={{0,6},{7,1},{8,14},{15,9},{16,22},{23,17},{24,30},{31,25},{32,38},... | collective-permute-start | bytes 1966088 | tf_op jit(solution)/shard_map/ppermute | solution.py:517
  38.8 12.5 %collective-permute-start.5 = (f32[640,256]{1,0:T(8,128)S(1)}, f32[640,256]{1,0:T(8,128)S(1)}, u32[]{:S(2)}, u32[]{:S(2)}) collective-permute-start(f32[640,256]{1,0:T(8,128)S(1)} %collective-permute-done.3), channel_id=1, source_target_pairs={{2,4},{5,3},{10,12},{13,11},{18,20},{21,19},{26,28},{29,27},{34,36... | collective-permute-start | bytes 1966088 | tf_op jit(solution)/shard_map/ppermute | solution.py:518
  43.5 14.0 %collective-permute-start.16 = (f32[2,64,1024]{2,1,0:T(8,128)S(1)}, f32[2,64,1024]{2,1,0:T(8,128)S(1)}, u32[]{:S(2)}, u32[]{:S(2)}) collective-permute-start(f32[2,64,1024]{2,1,0:T(8,128)S(1)} %pad_maximum_fusion.2.own), channel_id=1, source_target_pairs={{0,96},{8,104},{16,112},{24,120},{32,0},{40,8},{48,16},{56,24},{64... | collective-permute-start | bytes 1572872 | tf_op jit(solution)/shard_map/ppermute | solution.py:590
  45.3 15.5 %collective-permute-start.14 = (f32[2,64,1024]{2,1,0:T(8,128)S(1)}, f32[2,64,1024]{2,1,0:T(8,128)S(1)}, u32[]{:S(2)}, u32[]{:S(2)}) collective-permute-start(f32[2,64,1024]{2,1,0:T(8,128)S(1)} %pad_maximum_fusion.2.own), channel_id=1, source_target_pairs={{0,32},{8,40},{16,48},{24,56},{32,64},{40,72},{48,80},{56,88},{64,... | collective-permute-start | bytes 1572872 | tf_op jit(solution)/shard_map/ppermute | solution.py:589
  48.1 13.2 %collective-permute-start.10 = (f32[640,256]{1,0:T(8,128)S(1)}, f32[640,256]{1,0:T(8,128)S(1)}, u32[]{:S(2)}, u32[]{:S(2)}) collective-permute-start(f32[640,256]{1,0:T(8,128)S(1)} %select_select_fusion), channel_id=1, source_target_pairs={{0,1},{1,0},{2,3},{3,2},{4,5},{5,4},{6,7},{7,6},{8,9},{9,8},{10,11... | collective-permute-start | bytes 1966088 | tf_op jit(solution)/shard_map/ppermute | solution.py:530
  51.5 9.9 %collective-permute-start.6 = (f32[640,256]{1,0:T(8,128)S(1)}, f32[640,256]{1,0:T(8,128)S(1)}, u32[]{:S(2)}, u32[]{:S(2)}) collective-permute-start(f32[640,256]{1,0:T(8,128)S(1)} %select_select_fusion.1), channel_id=1, source_target_pairs={{0,1},{1,0},{2,3},{3,2},{4,5},{5,4},{6,7},{7,6},{8,9},{9,8},{10,11... | collective-permute-start | bytes 1966088 | tf_op jit(solution)/shard_map/ppermute | solution.py:530
  57.5 11.3 %collective-permute-start.17 = (f32[64,1024]{1,0:T(8,128)S(1)}, f32[64,1024]{1,0:T(8,128)S(1)}, u32[]{:S(2)}, u32[]{:S(2)}) collective-permute-start(f32[64,1024]{1,0:T(8,128)S(1)} %slice_bitcast_fusion), channel_id=1, source_target_pairs={{0,96},{8,104},{16,112},{24,120},{32,0},{40,8},{48,16},{56,24},{64... | collective-permute-start | bytes 786440 | tf_op jit(solution)/shard_map/ppermute | solution.py:597
  60.8 9.2 %collective-permute-start.15 = (f32[64,1024]{1,0:T(8,128)S(1)}, f32[64,1024]{1,0:T(8,128)S(1)}, u32[]{:S(2)}, u32[]{:S(2)}) collective-permute-start(f32[64,1024]{1,0:T(8,128)S(1)} %slice_bitcast_fusion.1), channel_id=1, source_target_pairs={{0,32},{8,40},{16,48},{24,56},{32,64},{40,72},{48,80},{56,88},{64,... | collective-permute-start | bytes 786440 | tf_op jit(solution)/shard_map/ppermute | solution.py:596
  70.7 38.4 %all-to-all-start = ((f32[16,136,256]{2,1,0:T(8,128)}), f32[16,136,256]{2,1,0:T(8,128)S(1)}, u32[]{:S(2)}, u32[]{:S(2)}) async-start(f32[16,136,256]{2,1,0:T(8,128)} %get-tuple-element.31), calls=%async_computation | async-start | bytes 4456448 | tf_op jit(solution)/shard_map/all_to_all | solution.py:599
  82.9 14.9 %collective-permute-start.21 = (f32[256,256]{1,0:T(8,128)S(1)}, f32[256,256]{1,0:T(8,128)S(1)}, u32[]{:S(2)}, u32[]{:S(2)}) collective-permute-start(f32[256,256]{1,0:T(8,128)S(1)} %select_select_fusion.2), channel_id=1, source_target_pairs={{1,0},{3,2},{5,4},{7,6},{9,8},{11,10},{13,12},{15,14},{17,16},{19,... | collective-permute-start | bytes 786440 | tf_op jit(solution)/shard_map/ppermute | solution.py:608
  111.9 11.6 %all-to-all-start.1 = ((f32[16,8,256]{2,1,0:T(8,128)}), f32[16,8,256]{2,1,0:T(8,128)S(1)}, u32[]{:S(2)}, u32[]{:S(2)}) async-start(f32[16,8,256]{2,1,0:T(8,128)} %get-tuple-element.40), calls=%async_computation.1 | async-start | bytes 262144 | tf_op jit(solution)/shard_map/all_to_all | solution.py:611
  123.6 23.2 %all-to-all-start.2 = ((f32[16,64,256]{2,1,0:T(8,128)}), f32[16,64,256]{2,1,0:T(8,128)}, u32[]{:S(2)}, u32[]{:S(2)}) async-start(f32[16,64,256]{2,1,0:T(8,128)} %get-tuple-element.50), calls=%async_computation.2 | async-start | bytes 2097152 | tf_op jit(solution)/shard_map/all_to_all | solution.py:614
  129.3 7.9 %collective-permute-start.24 = (f32[16,8,256]{2,1,0:T(8,128)S(1)}, f32[16,8,256]{2,1,0:T(8,128)S(1)}, u32[]{:S(2)}, u32[]{:S(2)}) collective-permute-start(f32[16,8,256]{2,1,0:T(8,128)S(1)} %all-to-all-done.1.mine), channel_id=1, source_target_pairs={{0,4},{1,5},{2,6},{3,7},{4,0},{5,1},{6,2},{7,3},{8,12},{9,13},{10,... | collective-permute-start | bytes 393224 | tf_op jit(solution)/shard_map/ppermute | solution.py:617
  129.4 7.8 %collective-permute-start.23 = (f32[16,8,256]{2,1,0:T(8,128)S(1)}, f32[16,8,256]{2,1,0:T(8,128)S(1)}, u32[]{:S(2)}, u32[]{:S(2)}) collective-permute-start(f32[16,8,256]{2,1,0:T(8,128)S(1)} %all-to-all-done.1.mine), channel_id=1, source_target_pairs={{0,6},{1,7},{2,0},{3,1},{4,2},{5,3},{6,4},{7,5},{8,14},{9,15},{10,... | collective-permute-start | bytes 393224 | tf_op jit(solution)/shard_map/ppermute | solution.py:617
  (16 other events, 179.5 us)
